TPU v7x, 32 devices: a whole 2x2x4 slice. The times are simulated.
32 devices in a mesh: dp: 4 (over y, core), mp: 8 (over z, x).
Axes of the slice: x: 2, y: 2, z: 4, core: 2. Of those that a mesh axis runs over, the one named last changes fastest.
Arguments:
- inputs: bfloat16 [8192, 2048], P('dp', 'mp'), may hold values from -6 to 6
- segments: int32 [4, 2048], P('dp'), may hold values from 0 to 7, never falling along the last dimension, each value on 1 to 1024 neighbouring positions
- gain_attn: float32 [2048], P('mp'), may hold values from 0.5 to 1.5
- gain_ffn: float32 [2048], P('mp'), may hold values from 0.5 to 1.5
- w_qkv: bfloat16 [3, 2048, 2048], P(None, 'mp'), may hold values from -0.125 to 0.125
- a_qkv: float32 [3, 2048, 16], P(None, 'mp'), may hold values from -0.125 to 0.125
- query_key_value_factor: float32 [3, 16, 2048], replicated, may hold values from -0.3 to 0.3
- m_qkv: float32 [3, 2048], P(None, 'mp'), may hold values from 1 to 1.6
- w_out: bfloat16 [2048, 2048], P('mp'), may hold values from -0.125 to 0.125
- a_out: float32 [2048, 16], P('mp'), may hold values from -0.125 to 0.125
- b_out: float32 [16, 2048], replicated, may hold values from -0.3 to 0.3
- m_out: float32 [2048], P('mp'), may hold values from 3 to 6
- w_gu: bfloat16 [2, 2048, 5632], P(None, 'mp'), may hold values from -0.125 to 0.125
- a_gu: float32 [2, 2048, 16], P(None, 'mp'), may hold values from -0.125 to 0.125
- gate_up_factor: float32 [2, 16, 5632], replicated, may hold values from -0.3 to 0.3
- m_gu: float32 [2, 5632], P(None, 'mp'), may hold values from 1 to 1.6
- w_down: bfloat16 [5632, 2048], P('mp'), may hold values from -0.078125 to 0.078125
- a_down: float32 [5632, 16], P('mp'), may hold values from -0.078125 to 0.078125
- b_down: float32 [16, 2048], replicated, may hold values from -0.3 to 0.3
- m_down: float32 [2048], P('mp'), may hold values from 1.5 to 3
- cotangent: bfloat16 [8192, 2048], P('dp', 'mp'), may hold values from -6 to 6
Outputs:
- block_out: bfloat16 [8192, 2048], P('dp', 'mp')
- grad_input: float32 [8192, 2048], P('dp', 'mp')
- grad_a_qkv: float32 [3, 2048, 16], P(None, 'mp')
- grad_b_qkv: float32 [3, 16, 2048], P(None, None, 'mp')
- grad_m_qkv: float32 [3, 2048], P(None, 'mp')
- grad_a_out: float32 [2048, 16], P('mp')
- grad_b_out: float32 [16, 2048], P(None, 'mp')
- grad_m_out: float32 [2048], P('mp')
- grad_a_gu: float32 [2, 2048, 16], P(None, 'mp')
- grad_b_gu: float32 [2, 16, 5632], P(None, None, 'mp')
- grad_m_gu: float32 [2, 5632], P(None, 'mp')
- grad_a_down: float32 [5632, 16], P('mp')
- grad_b_down: float32 [16, 2048], P(None, 'mp')
- grad_m_down: float32 [2048], P('mp')
Inputs may be any that keep to these rules, and one draw needn't show every extreme that they name: Within each packed row the segment numbers never fall; each of the 8 segments holds 1 to 1024 tokens, and one holds exactly 1024.
All inputs are finite; a program needn't handle non-finite values.
Results may differ from a plain program's by a relative error of at most 0.019.
Values may be sent and summed in bfloat16 or wider, within the bound.
A program may use at most 320 MiB of HBM per device.

v0:
```python
import math

import jax
import jax.numpy as jnp
from jax import lax
from jax.sharding import PartitionSpec as P

D = 2048
HD = 128
ADAPTER_RANK = 16
ADAPTER_ALPHA = 32
SEQ = 2048


highest_precision = lax.Precision.HIGHEST
epsilon = 1e-05
masked_score = -1e30


def local_columns(whole_array, axis_dim):
    width_each = whole_array.shape[axis_dim] // lax.axis_size("mp")
    return lax.dynamic_slice_in_dim(
        whole_array, lax.axis_index("mp") * width_each, width_each, axis_dim
    )


def positions_of(segment_rows):
    index_row = jnp.arange(segment_rows.shape[1], dtype=jnp.int32)
    starts = jnp.concatenate(
        [
            jnp.ones((segment_rows.shape[0], 1), jnp.bool_),
            segment_rows[:, 1:] != segment_rows[:, :-1],
        ],
        axis=1,
    )
    begin_at = lax.cummax(jnp.where(starts, index_row[None, :], 0), axis=1)
    return index_row[None, :] - begin_at


def rotary_tables(positions):
    freq_rows = jnp.exp(jnp.arange(HD // 2, dtype=jnp.float32) * (-2.0 * math.log(10000.0) / HD))
    angles = positions.astype(jnp.float32)[:, None] * freq_rows[None, :]
    return (jnp.cos(angles), jnp.sin(angles))


def rotate(head_values, cosine, sine_table):
    first_half = head_values[..., : HD // 2]
    second_half = head_values[..., HD // 2 :]
    cosine = cosine[:, None, :]
    sine_table = sine_table[:, None, :]
    return jnp.concatenate(
        [
            first_half * cosine - second_half * sine_table,
            second_half * cosine + first_half * sine_table,
        ],
        axis=-1,
    )


def norm_forward(residual, gain_row):
    squares = lax.psum(jnp.sum(residual * residual, axis=1), "mp")
    inverse = lax.rsqrt(squares / D + epsilon)
    return ((residual * inverse[:, None] * gain_row).astype(jnp.bfloat16), inverse)


def norm_backward(residual, gain_row, inverse, grad_normed):
    weighted = grad_normed * gain_row
    row_inner = lax.psum(jnp.sum(weighted * residual, axis=1), "mp")
    return inverse[:, None] * weighted - residual * (inverse**3 * row_inner / D)[:, None]


def output_grads(output_gradient, projected_rows, magnitude_vector, column_slice):
    grad_mag = jnp.sum(output_gradient * projected_rows, axis=0) / column_slice
    grad_column = -grad_mag * magnitude_vector / column_slice
    projection_gradient = (output_gradient * (magnitude_vector / column_slice)[None]).astype(
        jnp.bfloat16
    )
    return (grad_mag, grad_column, projection_gradient)


def column_weights(w_qkv, a_qkv, query_key_value_factor, w_gu, a_gu, gate_up_factor):
    adapter_scale = ADAPTER_ALPHA / ADAPTER_RANK
    query_key_value_columns, gate_up_columns = (
        lax.all_to_all(w_qkv, "mp", split_axis=2, concat_axis=1, tiled=True),
        lax.all_to_all(w_gu, "mp", split_axis=2, concat_axis=1, tiled=True),
    )
    query_key_value_rows, gate_up_rows = (
        lax.all_gather(a_qkv, "mp", axis=1, tiled=True),
        lax.all_gather(a_gu, "mp", axis=1, tiled=True),
    )
    prepared = []
    for frozen_weight_columns, complete_rows, adapter_up_factor in (
        (query_key_value_columns, query_key_value_rows, query_key_value_factor),
        (gate_up_columns, gate_up_rows, gate_up_factor),
    ):
        local_up_factor = local_columns(adapter_up_factor, 2)
        merged_weight = frozen_weight_columns.astype(jnp.float32) + adapter_scale * jnp.einsum(
            "cwt,ctn->cwn", complete_rows, local_up_factor, precision=highest_precision
        )
        column_slice = jnp.sqrt(jnp.sum(merged_weight * merged_weight, axis=1))
        across_devices = jnp.einsum(
            "gda,gdj->gaj", complete_rows, merged_weight, precision=highest_precision
        )
        prepared.append(
            (frozen_weight_columns, complete_rows, local_up_factor, column_slice, across_devices)
        )
    return (prepared[0], prepared[1])


def column_forward(input_portion, prepared, magnitude_vector):
    adapter_scale = ADAPTER_ALPHA / ADAPTER_RANK
    frozen_weight_columns, complete_rows, local_up_factor, column_slice, across_devices = prepared
    entire_rows = lax.all_gather(input_portion, "mp", axis=1, tiled=True)
    adapter_input = jnp.einsum(
        "td,kdr->tkr",
        entire_rows,
        complete_rows,
        precision=highest_precision,
        preferred_element_type=jnp.float32,
    )
    projected_rows = jnp.einsum(
        "td,kdo->tko", entire_rows, frozen_weight_columns, preferred_element_type=jnp.float32
    )
    projected_rows = projected_rows + adapter_scale * jnp.einsum(
        "dev,evc->dec", adapter_input, local_up_factor, precision=highest_precision
    )
    return (
        projected_rows * (magnitude_vector / column_slice)[None],
        (projected_rows, column_slice, across_devices, adapter_input, entire_rows),
    )


def column_backward(prepared, magnitude_vector, retained_state, output_gradient):
    adapter_scale = ADAPTER_ALPHA / ADAPTER_RANK
    frozen_weight_columns, complete_rows, local_up_factor, column_slice, across_devices = prepared
    projected_rows, column_slice, across_devices, adapter_input, entire_rows = retained_state
    grad_mag, grad_column, projection_gradient = output_grads(
        output_gradient, projected_rows, magnitude_vector, column_slice
    )
    adapter_gradient = adapter_scale * jnp.einsum(
        "vqn,qen->vqe",
        projection_gradient,
        local_up_factor,
        precision=highest_precision,
        preferred_element_type=jnp.float32,
    )
    complete_gradient = jnp.einsum(
        "tko,kdo->td",
        projection_gradient,
        frozen_weight_columns,
        preferred_element_type=jnp.float32,
    )
    complete_gradient = complete_gradient + jnp.einsum(
        "pxu,xfu->pf", adapter_gradient, complete_rows, precision=highest_precision
    )
    grad_rows_a = jnp.einsum(
        "ui,ulv->liv",
        entire_rows,
        adapter_gradient,
        precision=highest_precision,
        preferred_element_type=jnp.float32,
    )
    input_gradient, grad_a = (
        lax.psum_scatter(complete_gradient, "mp", scatter_dimension=1, tiled=True),
        lax.psum_scatter(grad_rows_a, "mp", scatter_dimension=1, tiled=True),
    )
    factor_gradient = adapter_scale * jnp.einsum(
        "dsj,dsv->sjv",
        adapter_input,
        projection_gradient,
        precision=highest_precision,
        preferred_element_type=jnp.float32,
    )
    return (input_gradient, grad_a, factor_gradient, grad_mag, grad_column)


def sharded_forward(
    input_portion, frozen_weight, adapter_down_factor, adapter_up_factor, magnitude_vector
):
    adapter_scale = ADAPTER_ALPHA / ADAPTER_RANK
    merged_weight = frozen_weight.astype(jnp.float32) + adapter_scale * jnp.einsum(
        "cwt,ctn->cwn", adapter_down_factor, adapter_up_factor, precision=highest_precision
    )
    sharded_output = jnp.einsum(
        "ti,kio->tko", input_portion, frozen_weight, preferred_element_type=jnp.float32
    )
    summed_result, squares, across_devices = (
        lax.psum_scatter(sharded_output, "mp", scatter_dimension=2, tiled=True),
        lax.psum_scatter(
            jnp.sum(merged_weight * merged_weight, axis=1), "mp", scatter_dimension=1, tiled=True
        ),
        lax.psum_scatter(
            jnp.einsum(
                "gda,gdj->gaj", adapter_down_factor, merged_weight, precision=highest_precision
            ),
            "mp",
            scatter_dimension=2,
            tiled=True,
        ),
    )
    adapter_input = lax.psum(
        jnp.einsum(
            "ti,kir->tkr",
            input_portion,
            adapter_down_factor,
            precision=highest_precision,
            preferred_element_type=jnp.float32,
        ),
        "mp",
    )
    projected_rows = summed_result + adapter_scale * jnp.einsum(
        "dev,evc->dec",
        adapter_input,
        local_columns(adapter_up_factor, 2),
        precision=highest_precision,
    )
    column_slice = jnp.sqrt(squares)
    return (
        projected_rows * (magnitude_vector / column_slice)[None],
        (projected_rows, column_slice, across_devices, adapter_input, input_portion),
    )


def sharded_backward(
    frozen_weight,
    adapter_down_factor,
    adapter_up_factor,
    magnitude_vector,
    retained_state,
    output_gradient,
):
    adapter_scale = ADAPTER_ALPHA / ADAPTER_RANK
    projected_rows, column_slice, across_devices, adapter_input, input_portion = retained_state
    grad_mag, grad_column, projection_gradient = output_grads(
        output_gradient, projected_rows, magnitude_vector, column_slice
    )
    block_portion = lax.all_gather(projection_gradient, "mp", axis=2, tiled=True)
    partial_gradient = jnp.einsum(
        "tko,kio->ti", block_portion, frozen_weight, preferred_element_type=jnp.float32
    )
    adapter_portion = jnp.einsum(
        "vqn,qen->vqe",
        block_portion,
        adapter_up_factor,
        precision=highest_precision,
        preferred_element_type=jnp.float32,
    )
    adapter_gradient = adapter_scale * adapter_portion
    input_gradient = partial_gradient + jnp.einsum(
        "eoy,ojy->ej", adapter_gradient, adapter_down_factor, precision=highest_precision
    )
    grad_a = jnp.einsum(
        "jg,juy->ugy",
        input_portion,
        adapter_gradient,
        precision=highest_precision,
        preferred_element_type=jnp.float32,
    )
    factor_gradient = adapter_scale * jnp.einsum(
        "dsj,dsv->sjv",
        adapter_input,
        projection_gradient,
        precision=highest_precision,
        preferred_element_type=jnp.float32,
    )
    return (input_gradient, grad_a, factor_gradient, grad_mag, grad_column)


def column_factor_term(frozen_weight, adapter_down_factor, adapter_up_factor, complete_ratio):
    adapter_scale = ADAPTER_ALPHA / ADAPTER_RANK
    merged_weight = frozen_weight.astype(jnp.float32) + adapter_scale * jnp.einsum(
        "cwt,ctn->cwn", adapter_down_factor, adapter_up_factor, precision=highest_precision
    )
    return adapter_scale * jnp.einsum(
        "wcm,wdm->wcd",
        merged_weight * complete_ratio[:, None, :],
        adapter_up_factor,
        precision=highest_precision,
    )


def score_block(query_block, first_row, key_rows, segment_row):
    key_index = jnp.arange(segment_row.shape[0], dtype=jnp.int32)
    query_index = first_row + jnp.arange(query_block.shape[0], dtype=jnp.int32)
    query_segments = lax.dynamic_slice_in_dim(segment_row, first_row, query_block.shape[0])
    allowed = (query_segments[:, None] == segment_row[None, :]) & (
        key_index[None, :] <= query_index[:, None]
    )
    scores = jnp.dot(query_block, key_rows.T, preferred_element_type=jnp.float32) * HD ** (-0.5)
    return (scores, allowed)


def attend_one(packed):
    query_rows, key_rows, value_rows, segment_row = packed
    block_rows = min(512, SEQ)

    def one_block(block_index):
        first_row = block_index * block_rows
        query_block = lax.dynamic_slice_in_dim(query_rows, first_row, block_rows)
        scores, allowed = score_block(query_block, first_row, key_rows, segment_row)
        scores = jnp.where(allowed, scores, masked_score)
        top_score = jnp.max(scores, axis=1, keepdims=True)
        shifted = jnp.exp(scores - top_score)
        denominator = jnp.sum(shifted, axis=1, keepdims=True)
        weights = (shifted / denominator).astype(jnp.bfloat16)
        mixed_out = jnp.dot(weights, value_rows, preferred_element_type=jnp.float32)
        return (mixed_out, (top_score + jnp.log(denominator))[:, 0])

    mixed_out, log_total = lax.map(one_block, jnp.arange(SEQ // block_rows, dtype=jnp.int32))
    return (mixed_out.reshape(SEQ, HD), log_total.reshape(SEQ))


def attend_back(packed):
    query_rows, key_rows, value_rows, segment_row, log_total, grad_mixed = packed
    block_rows = min(512, SEQ)
    scale_factor = HD ** (-0.5)

    def one_block(running, block_index):
        grad_keys, grad_values = running
        first_row = block_index * block_rows
        query_block = lax.dynamic_slice_in_dim(query_rows, first_row, block_rows)
        grad_block = lax.dynamic_slice_in_dim(grad_mixed, first_row, block_rows)
        lse_block = lax.dynamic_slice_in_dim(log_total, first_row, block_rows)
        scores, allowed = score_block(query_block, first_row, key_rows, segment_row)
        probability = jnp.where(allowed, jnp.exp(scores - lse_block[:, None]), 0.0)
        grad_probs = jnp.dot(grad_block, value_rows.T, preferred_element_type=jnp.float32)
        row_inner = jnp.sum(probability * grad_probs, axis=1, keepdims=True)
        grad_scores = (probability * (grad_probs - row_inner)).astype(jnp.bfloat16)
        grad_query = (
            jnp.dot(grad_scores, key_rows, preferred_element_type=jnp.float32) * scale_factor
        )
        grad_keys = (
            grad_keys
            + jnp.dot(grad_scores.T, query_block, preferred_element_type=jnp.float32) * scale_factor
        )
        grad_values = grad_values + jnp.dot(
            probability.astype(jnp.bfloat16).T, grad_block, preferred_element_type=jnp.float32
        )
        return ((grad_keys, grad_values), grad_query)

    zeros_rows = jnp.zeros((SEQ, HD), jnp.float32)
    (grad_keys, grad_values), grad_queries = lax.scan(
        one_block, (zeros_rows, zeros_rows), jnp.arange(SEQ // block_rows, dtype=jnp.int32)
    )
    return (grad_queries.reshape(SEQ, HD), grad_keys, grad_values)


def heads_first(tensor, rows_here):
    heads_here = tensor.shape[1] // HD
    return (
        tensor.reshape(rows_here, SEQ, heads_here, HD)
        .transpose(0, 2, 1, 3)
        .reshape(rows_here * heads_here, SEQ, HD)
    )


def tokens_first(tensor, rows_here):
    heads_here = tensor.shape[0] // rows_here
    return (
        tensor.reshape(rows_here, heads_here, SEQ, HD)
        .transpose(0, 2, 1, 3)
        .reshape(rows_here * SEQ, heads_here * HD)
    )


def on_device(
    inputs,
    segments,
    gain_attn,
    gain_ffn,
    w_qkv,
    a_qkv,
    query_key_value_factor,
    m_qkv,
    w_out,
    a_out,
    b_out,
    m_out,
    w_gu,
    a_gu,
    gate_up_factor,
    m_gu,
    w_down,
    a_down,
    b_down,
    m_down,
    cotangent,
):
    adapter_scale = ADAPTER_ALPHA / ADAPTER_RANK
    tokens_here = inputs.shape[0]
    width_here = inputs.shape[1]
    rows_here = segments.shape[0]
    heads_here = width_here // HD
    positions = positions_of(segments).reshape(tokens_here)
    cosine, sine_table = rotary_tables(positions)
    segment_heads = jnp.repeat(segments, heads_here, axis=0)
    prepared_qkv, prepared_gu = column_weights(
        w_qkv, a_qkv, query_key_value_factor, w_gu, a_gu, gate_up_factor
    )

    def project_in(input_portion, magnitude_vector, prepared):
        return column_forward(input_portion, prepared, magnitude_vector)

    def project_back(magnitude_vector, prepared, retained_state, output_gradient):
        return column_backward(prepared, magnitude_vector, retained_state, output_gradient)

    def turn_heads(flat_rows):
        return rotate(flat_rows.reshape(tokens_here, heads_here, HD), cosine, sine_table).reshape(
            tokens_here, width_here
        )

    def run_forward(block_in):
        residual = block_in.astype(jnp.float32)
        normed, inverse_attn = norm_forward(residual, gain_attn)
        qkv_out, query_key_value_saved_state = project_in(normed, m_qkv, prepared_qkv)
        query_rows = turn_heads(qkv_out[:, 0]).astype(jnp.bfloat16)
        key_rows = turn_heads(qkv_out[:, 1]).astype(jnp.bfloat16)
        value_rows = qkv_out[:, 2].astype(jnp.bfloat16)
        mixed_out, log_total = lax.map(
            attend_one,
            (
                heads_first(query_rows, rows_here),
                heads_first(key_rows, rows_here),
                heads_first(value_rows, rows_here),
                segment_heads,
            ),
        )
        attended = tokens_first(mixed_out, rows_here).astype(jnp.bfloat16)
        attn_out, output_saved_state = sharded_forward(
            attended, w_out[None], a_out[None], b_out[None], m_out[None]
        )
        middle = residual + attn_out[:, 0]
        normed_ffn, inverse_ffn = norm_forward(middle, gain_ffn)
        gu_out, gate_up_saved_state = project_in(normed_ffn, m_gu, prepared_gu)
        hidden = (jax.nn.silu(gu_out[:, 0]) * gu_out[:, 1]).astype(jnp.bfloat16)
        down_out, down_saved_state = sharded_forward(
            hidden, w_down[None], a_down[None], b_down[None], m_down[None]
        )
        result = middle + down_out[:, 0]
        saved_state = (
            residual,
            inverse_attn,
            qkv_out,
            query_key_value_saved_state,
            query_rows,
            key_rows,
            value_rows,
            log_total,
            output_saved_state,
            middle,
            inverse_ffn,
            gu_out,
            gate_up_saved_state,
            down_saved_state,
        )
        return (result, saved_state)

    result, saved_state = run_forward(inputs)
    again_in, grad_seed = lax.optimization_barrier((inputs, cotangent))
    unused_result, saved_state = run_forward(again_in)
    (
        residual,
        inverse_attn,
        qkv_out,
        query_key_value_saved_state,
        query_rows,
        key_rows,
        value_rows,
        log_total,
        output_saved_state,
        middle,
        inverse_ffn,
        gu_out,
        gate_up_saved_state,
        down_saved_state,
    ) = saved_state
    output_gradient = grad_seed.astype(jnp.float32)
    grad_hidden, ga_down, down_factor_gradient, gm_down, gc_down = sharded_backward(
        w_down[None],
        a_down[None],
        b_down[None],
        m_down[None],
        down_saved_state,
        output_gradient[:, None],
    )
    unused_value, silu_pull = jax.vjp(
        lambda gate_up: jax.nn.silu(gate_up[:, 0]) * gate_up[:, 1], gu_out
    )
    grad_gu = silu_pull(grad_hidden)[0]
    grad_ffn, ga_gu, gate_up_factor_gradient, gm_gu, gc_gu = project_back(
        m_gu, prepared_gu, gate_up_saved_state, grad_gu
    )
    grad_middle = output_gradient + norm_backward(middle, gain_ffn, inverse_ffn, grad_ffn)
    grad_att, ga_out, output_factor_gradient, gm_out, gc_out = sharded_backward(
        w_out[None], a_out[None], b_out[None], m_out[None], output_saved_state, grad_middle[:, None]
    )
    grad_queries, grad_keys, grad_values = lax.map(
        attend_back,
        (
            heads_first(query_rows, rows_here),
            heads_first(key_rows, rows_here),
            heads_first(value_rows, rows_here),
            segment_heads,
            log_total,
            heads_first(grad_att.astype(jnp.bfloat16), rows_here),
        ),
    )
    unused_turn, turn_pull = jax.vjp(turn_heads, qkv_out[:, 0])
    grad_qkv = jnp.stack(
        [
            turn_pull(tokens_first(grad_queries, rows_here))[0],
            turn_pull(tokens_first(grad_keys, rows_here))[0],
            tokens_first(grad_values, rows_here),
        ],
        axis=1,
    )
    grad_normed, ga_qkv, query_key_value_factor_gradient, gm_qkv, gc_qkv = project_back(
        m_qkv, prepared_qkv, query_key_value_saved_state, grad_qkv
    )
    grad_input = grad_middle + norm_backward(residual, gain_attn, inverse_attn, grad_normed)
    (
        ga_qkv,
        query_key_value_factor_gradient,
        gm_qkv,
        gc_qkv,
        ga_out,
        output_factor_gradient,
        gm_out,
        gc_out,
        ga_gu,
        gate_up_factor_gradient,
        gm_gu,
        gc_gu,
        ga_down,
        down_factor_gradient,
        gm_down,
        gc_down,
    ) = (
        lax.psum(ga_qkv.astype(jnp.bfloat16), "dp").astype(jnp.float32),
        lax.psum(query_key_value_factor_gradient.astype(jnp.bfloat16), "dp").astype(jnp.float32),
        lax.psum(gm_qkv.astype(jnp.bfloat16), "dp").astype(jnp.float32),
        lax.psum(gc_qkv.astype(jnp.bfloat16), "dp").astype(jnp.float32),
        lax.psum(ga_out.astype(jnp.bfloat16), "dp").astype(jnp.float32),
        lax.psum(output_factor_gradient.astype(jnp.bfloat16), "dp").astype(jnp.float32),
        lax.psum(gm_out.astype(jnp.bfloat16), "dp").astype(jnp.float32),
        lax.psum(gc_out.astype(jnp.bfloat16), "dp").astype(jnp.float32),
        lax.psum(ga_gu.astype(jnp.bfloat16), "dp").astype(jnp.float32),
        lax.psum(gate_up_factor_gradient.astype(jnp.bfloat16), "dp").astype(jnp.float32),
        lax.psum(gm_gu.astype(jnp.bfloat16), "dp").astype(jnp.float32),
        lax.psum(gc_gu.astype(jnp.bfloat16), "dp").astype(jnp.float32),
        lax.psum(ga_down.astype(jnp.bfloat16), "dp").astype(jnp.float32),
        lax.psum(down_factor_gradient.astype(jnp.bfloat16), "dp").astype(jnp.float32),
        lax.psum(gm_down.astype(jnp.bfloat16), "dp").astype(jnp.float32),
        lax.psum(gc_down.astype(jnp.bfloat16), "dp").astype(jnp.float32),
    )
    query_key_value_norm_ratio = gc_qkv / query_key_value_saved_state[1]
    output_norm_ratio = gc_out / output_saved_state[1]
    gate_up_norm_ratio = gc_gu / gate_up_saved_state[1]
    down_norm_ratio = gc_down / down_saved_state[1]
    full_qkv, full_out, full_gu, full_down = (
        lax.all_gather(query_key_value_norm_ratio, "mp", axis=1, tiled=True),
        lax.all_gather(output_norm_ratio, "mp", axis=1, tiled=True),
        lax.all_gather(gate_up_norm_ratio, "mp", axis=1, tiled=True),
        lax.all_gather(down_norm_ratio, "mp", axis=1, tiled=True),
    )
    ga_qkv = ga_qkv + column_factor_term(w_qkv, a_qkv, query_key_value_factor, full_qkv)
    ga_out = ga_out + column_factor_term(w_out[None], a_out[None], b_out[None], full_out)
    ga_gu = ga_gu + column_factor_term(w_gu, a_gu, gate_up_factor, full_gu)
    ga_down = ga_down + column_factor_term(w_down[None], a_down[None], b_down[None], full_down)
    query_key_value_factor_gradient = (
        query_key_value_factor_gradient
        + adapter_scale * query_key_value_norm_ratio[:, None, :] * query_key_value_saved_state[2]
    )
    output_factor_gradient = (
        output_factor_gradient
        + adapter_scale * output_norm_ratio[:, None, :] * output_saved_state[2]
    )
    gate_up_factor_gradient = (
        gate_up_factor_gradient
        + adapter_scale * gate_up_norm_ratio[:, None, :] * gate_up_saved_state[2]
    )
    down_factor_gradient = (
        down_factor_gradient + adapter_scale * down_norm_ratio[:, None, :] * down_saved_state[2]
    )
    return (
        result.astype(jnp.bfloat16),
        grad_input,
        ga_qkv,
        query_key_value_factor_gradient,
        gm_qkv,
        ga_out[0],
        output_factor_gradient[0],
        gm_out[0],
        ga_gu,
        gate_up_factor_gradient,
        gm_gu,
        ga_down[0],
        down_factor_gradient[0],
        gm_down[0],
    )


def solution(mesh):
    in_specs = (
        P("dp", "mp"),
        P("dp", None),
        P("mp"),
        P("mp"),
        P(None, "mp", None),
        P(None, "mp", None),
        P(),
        P(None, "mp"),
        P("mp", None),
        P("mp", None),
        P(),
        P("mp"),
        P(None, "mp", None),
        P(None, "mp", None),
        P(),
        P(None, "mp"),
        P("mp", None),
        P("mp", None),
        P(),
        P("mp"),
        P("dp", "mp"),
    )
    out_specs = (
        P("dp", "mp"),
        P("dp", "mp"),
        P(None, "mp", None),
        P(None, None, "mp"),
        P(None, "mp"),
        P("mp", None),
        P(None, "mp"),
        P("mp"),
        P(None, "mp", None),
        P(None, None, "mp"),
        P(None, "mp"),
        P("mp", None),
        P(None, "mp"),
        P("mp"),
    )
    return jax.shard_map(
        on_device, mesh=mesh, in_specs=in_specs, out_specs=out_specs, check_vma=False
    )
```

profile of v0, /device:TPU:1, one launch (start us, length us, event | category | flops | bytes accessed | tf_op | source)
XLA Modules:
  0.0 3685.3 jit_solution(15346056062087505824)
XLA Ops:
  59.5 161.8 %all_gather.37 = f32[3,2048,16]{1,2,0:T(8,128)S(1)} all-gather(f32[3,256,16]{1,2,0:T(8,128)S(1)} %copy-done.75), channel_id=1, replica_groups=mesh['dp'=4,'mp'=8] {'mp'}, dimensions={1}, use_global_device_ids=true | all-gather | bytes 442368 | tf_op jit(solution)/shard_map/all_gather | solution.py:88
  305.6 63.3 %while.76 = (s32[]{:T(128)}, bf16[2,2048,128]{1,2,0:T(8,128)(2,1)}, f32[2,2048]{1,0:T(2,128)S(1)}, bf16[2,2048,128]{2,1,0:T(8,128)(2,1)}, s32[2,2048]{1,0:T(2,12...) while((s32[]{:T(128)}, bf16[2,2048,128]{1,2,0:T(8,128)(2,1)}, ...), condition=%wide.region_29.30_spmd, body=%wide.region_24.29_spmd.sunk | while | flops 548405248 | bytes 23550484 | solution.py:419
  308.6 26.5 while.80
  340.2 26.6 while.80
  385.7 64.3 %all-reduce.17.cloned.1.call-done = f32[2048,16]{0,1:T(8,128)} async-done(((f32[2048,16]{0,1:T(8,128)}), f32[2048,16]{0,1:T(8,128)}) %all-reduce.17.cloned.1.call-update) | async-done | bytes 131088 | tf_op jit(solution)/shard_map/psum | solution.py:201
  450.0 288.0 %reduce-scatter.21.cloned.1.call-done = f32[2048,1,256]{2,0,1:T(8,128)} async-done(((f32[2048,1,2048]{2,0,1:T(8,128)}), f32[2048,1,256]{2,0,1:T(8,128)}) %reduce-scatter.21.cloned.1.call-update) | async-done | bytes 2097168 | tf_op jit(solution)/shard_map/reduce_scatter | solution.py:188
  782.7 210.9 %all_gather.39 = f32[2,2048,16]{1,2,0:T(8,128)S(1)} all-gather(f32[2,256,16]{1,2,0:T(8,128)S(1)} %copy-done.79), channel_id=1, replica_groups=mesh['dp'=4,'mp'=8] {'mp'}, dimensions={1}, use_global_device_ids=true | all-gather | bytes 294912 | tf_op jit(solution)/shard_map/all_gather | solution.py:89
  1030.5 70.4 %all-gather.16.cloned.1.call-done = bf16[2048,2048]{1,0:T(8,128)(2,1)} async-done(((bf16[2048,256]{1,0:T(8,128)(2,1)}), bf16[2048,2048]{1,0:T(8,128)(2,1)}) %all-gather.16.cloned.1.call-update) | async-done | bytes 8388624 | tf_op jit(solution)/shard_map/all_gather | solution.py:113
  1209.2 281.1 %reduce-scatter.23.cloned.1.call-done = f32[2048,256]{1,0:T(8,128)} async-done(((f32[2048,2048]{1,0:T(8,128)}), f32[2048,256]{1,0:T(8,128)}) %reduce-scatter.23.cloned.1.call-update) | async-done | bytes 2097168 | tf_op jit(solution)/shard_map/reduce_scatter | solution.py:164
  1492.9 28.2 all-reduce.7
  1528.6 127.6 %all-gather.20.cloned.1.call-done = bf16[2048,2048]{1,0:T(8,128)(2,1)} async-done(((bf16[2048,256]{1,0:T(8,128)(2,1)}), bf16[2048,2048]{1,0:T(8,128)(2,1)}) %all-gather.20.cloned.1.call-update) | async-done | bytes 8388624 | tf_op jit(solution)/shard_map/all_gather | solution.py:237
  1671.6 156.2 %while.78 = (s32[]{:T(128)}, f32[2,2048,128]{2,1,0:T(8,128)}, f32[2,2048,128]{2,1,0:T(8,128)}, f32[2,2048,128]{2,1,0:T(8,128)}, bf16[2,2048,128]{2,1,0:T(8,128)(...) while((s32[]{:T(128)}, f32[2,2048,128]{2,1,0:T(8,128)}, ...), condition=%wide.region_41.42_spmd, body=%wide.region_37.41_spmd.sunk | while | flops 1356136448 | bytes 90501808 | solution.py:497
  1677.8 66.6 %while.81 = (s32[]{:T(128)}, f32[2048,128]{1,0:T(8,128)}, f32[2048,128]{1,0:T(8,128)}, f32[4,512,128]{2,1,0:T(8,128)}, s32[4]{0:T(128)S(1)}, /*index=5*/s32[2048...) while((s32[]{:T(128)}, f32[2048,128]{1,0:T(8,128)}, ...), condition=%wide.region_40.40_spmd.clone, body=%wide.region_38.39_spmd.clone.sunk | while | flops 1356136448 | bytes 71594288 | solution.py:342
  1756.0 66.5 %while.81 = (s32[]{:T(128)}, f32[2048,128]{1,0:T(8,128)}, f32[2048,128]{1,0:T(8,128)}, f32[4,512,128]{2,1,0:T(8,128)}, s32[4]{0:T(128)S(1)}, /*index=5*/s32[2048...) while((s32[]{:T(128)}, f32[2048,128]{1,0:T(8,128)}, ...), condition=%wide.region_40.40_spmd.clone, body=%wide.region_38.39_spmd.clone.sunk | while | flops 1356136448 | bytes 71594288 | solution.py:342
  1935.8 41.7 %while.74 = (s32[]{:T(128)}, bf16[2,2048,128]{1,2,0:T(8,128)(2,1)}, bf16[2,2048,128]{2,1,0:T(8,128)(2,1)}, s32[2,2048]{1,0:T(2,128)S(1)}, bf16[2,2048,128]{2,1,0...) while((s32[]{:T(128)}, bf16[2,2048,128]{1,2,0:T(8,128)(2,1)}, ...), condition=%wide.region_10.11_spmd, body=%wide.region_5.10_spmd.sunk | while | flops 548404736 | bytes 19313084 | solution.py:419
  1990.2 215.9 %reduce-scatter.25.cloned.1.call-done = f32[2048,256]{1,0:T(8,128)} async-done(((f32[2048,2048]{1,0:T(8,128)}), f32[2048,256]{1,0:T(8,128)}) %reduce-scatter.25.cloned.1.call-update) | async-done | bytes 2097168 | tf_op jit(solution)/shard_map/reduce_scatter | solution.py:164
  2208.1 68.8 %all-reduce.15.cloned.1.call-done = f32[2048,16]{0,1:T(8,128)} async-done(((f32[2048,16]{0,1:T(8,128)}), f32[2048,16]{0,1:T(8,128)}) %all-reduce.15.cloned.1.call-update) | async-done | bytes 131088 | tf_op jit(solution)/shard_map/psum | solution.py:201
  2276.9 288.1 %reduce-scatter.17.cloned.1.call-done = f32[2048,1,256]{2,0,1:T(8,128)} async-done(((f32[2048,1,2048]{2,0,1:T(8,128)}), f32[2048,1,256]{2,0,1:T(8,128)}) %reduce-scatter.17.cloned.1.call-update) | async-done | bytes 2097168 | tf_op jit(solution)/shard_map/reduce_scatter | solution.py:188
  2570.3 28.7 all-reduce.6
  2625.8 105.5 %all-gather.12.cloned.1.call-done = bf16[2048,2048]{1,0:T(8,128)(2,1)} async-done(((bf16[2048,256]{1,0:T(8,128)(2,1)}), bf16[2048,2048]{1,0:T(8,128)(2,1)}) %all-gather.12.cloned.1.call-update) | async-done | bytes 8388624 | tf_op jit(solution)/shard_map/all_gather | solution.py:113
  2823.3 35.3 reduce-scatter.27.cloned.1.call-done
  2860.0 72.5 %all-reduce.19.cloned.1.call-done = (f32[2048,16]{0,1:T(8,128)}, f32[2048,16]{0,1:T(8,128)}) async-done(((f32[2048,16]{0,1:T(8,128)}, f32[2048,16]{0,1:T(8,128)}), (f32[2048,16]{0,1:T(8,128)}, f32[2048,16]{0,1:T(8,128)})) %all-reduce.19.cloned.1.call-update) | async-done | bytes 262160 | tf_op jit(solution)/shard_map/psum | solution.py:201
  2934.6 285.9 %reduce-scatter.33.cloned.1.call-done = f32[2048,1,256]{2,0,1:T(8,128)} async-done(((f32[2048,1,2048]{2,0,1:T(8,128)}), f32[2048,1,256]{2,0,1:T(8,128)}) %reduce-scatter.33.cloned.1.call-update) | async-done | bytes 2097168 | tf_op jit(solution)/shard_map/reduce_scatter | solution.py:188
  3444.2 229.5 %reduce-scatter.19.cloned.1.call-done = f32[2048,1,256]{2,0,1:T(8,128)} async-done(((f32[2048,1,2048]{2,0,1:T(8,128)}), f32[2048,1,256]{2,0,1:T(8,128)}) %reduce-scatter.19.cloned.1.call-update) | async-done | bytes 2097168 | tf_op jit(solution)/shard_map/reduce_scatter | solution.py:188
  (790 shorter events, 1124.3 us)
Async XLA Ops:
  7.2 241.4 %all-gather.14.cloned.1.call-start = ((), (), s32[]{:S(2)}) async-start(), calls=%async_computation.19 | async-start | bytes 9437184 | tf_op jit(solution)/shard_map/all_gather | solution.py:113
  38.2 188.6 %all-to-all-start = ((bf16[3,256,2048]{1,0,2:T(4,128)(2,1)}), bf16[3,256,2048]{1,0,2:T(4,128)(2,1)}, u32[]{:S(2)}, u32[]{:S(2)}) async-start(bf16[3,256,2048]{1,0,2:T(4,128)(2,1)} %copy.93), calls=%async_computation | async-start | bytes 8388608 | tf_op jit(solution)/shard_map/all_to_all | solution.py:84
  43.0 339.2 %reduce-scatter.39.cloned.1.call-start = ((), (), s32[]{:S(2)}) async-start(), calls=%async_computation.33 | async-start | bytes 1179648
  53.2 331.5 %reduce-scatter.37.cloned.1.call-start = ((), (), s32[]{:S(2)}) async-start(), calls=%async_computation.32 | async-start | bytes 1179648
  58.6 391.4 %all-reduce.17.cloned.1.call-start = ((), (), s32[]{:S(2)}) async-start(), calls=%async_computation.21 | async-start | bytes 262144 | tf_op jit(solution)/shard_map/psum | solution.py:201
  372.2 365.8 %reduce-scatter.21.cloned.1.call-start = ((), (), s32[]{:S(2)}) async-start(), calls=%async_computation.20 | async-start | bytes 18874368 | tf_op jit(solution)/shard_map/reduce_scatter | solution.py:188
  382.1 630.6 %all-gather.18.cloned.1.call-start = ((), (), s32[]{:S(2)}) async-start(), calls=%async_computation.30 | async-start | bytes 9437184 | tf_op jit(solution)/shard_map/all_gather | solution.py:237
  384.6 716.3 %all-gather.16.cloned.1.call-start = ((), (), s32[]{:S(2)}) async-start(), calls=%async_computation.22 | async-start | bytes 9437184 | tf_op jit(solution)/shard_map/all_gather | solution.py:113
  777.8 215.8 %all-to-all-start.1 = ((bf16[2,256,5632]{1,0,2:T(2,128)(2,1)}), bf16[2,256,5632]{1,0,2:T(2,128)(2,1)}, u32[]{:S(2)}, u32[]{:S(2)}) async-start(bf16[2,256,5632]{1,0,2:T(2,128)(2,1)} %copy.104), calls=%async_computation.2 | async-start | bytes 11534336 | tf_op jit(solution)/shard_map/all_to_all | solution.py:85
  782.6 707.6 %reduce-scatter.23.cloned.1.call-start = ((), (), s32[]{:S(2)}) async-start(), calls=%async_computation.23 | async-start | bytes 18874368 | tf_op jit(solution)/shard_map/reduce_scatter | solution.py:164
  1208.8 447.5 %all-gather.20.cloned.1.call-start = ((), (), s32[]{:S(2)}) async-start(), calls=%async_computation.31 | async-start | bytes 9437184 | tf_op jit(solution)/shard_map/all_gather | solution.py:237
  1527.0 300.9 %all-gather.10.cloned.1.call-start = ((), (), s32[]{:S(2)}) async-start(), calls=%async_computation.14 | async-start | bytes 9437184 | tf_op jit(solution)/shard_map/all_gather | solution.py:113
  1528.4 677.7 %reduce-scatter.25.cloned.1.call-start = ((), (), s32[]{:S(2)}) async-start(), calls=%async_computation.24 | async-start | bytes 18874368 | tf_op jit(solution)/shard_map/reduce_scatter | solution.py:164
  1924.5 352.4 %all-reduce.15.cloned.1.call-start = ((), (), s32[]{:S(2)}) async-start(), calls=%async_computation.16 | async-start | bytes 262144 | tf_op jit(solution)/shard_map/psum | solution.py:201
  1979.9 585.1 %reduce-scatter.17.cloned.1.call-start = ((), (), s32[]{:S(2)}) async-start(), calls=%async_computation.15 | async-start | bytes 18874368 | tf_op jit(solution)/shard_map/reduce_scatter | solution.py:188
  1989.7 741.7 %all-gather.12.cloned.1.call-start = ((), (), s32[]{:S(2)}) async-start(), calls=%async_computation.17 | async-start | bytes 9437184 | tf_op jit(solution)/shard_map/all_gather | solution.py:113
  2601.9 206.1 %reduce-scatter.31.cloned.1.call-start = ((), (), s32[]{:S(2)}) async-start(), calls=%async_computation.27 | async-start | bytes 294912 | tf_op jit(solution)/shard_map/reduce_scatter | solution.py:165
  2618.0 240.6 %reduce-scatter.27.cloned.1.call-start = ((), (), s32[]{:S(2)}) async-start(), calls=%async_computation.25 | async-start | bytes 442368 | tf_op jit(solution)/shard_map/reduce_scatter | solution.py:165
  2625.6 306.9 %all-reduce.19.cloned.1.call-start = ((), (), s32[]{:S(2)}) async-start(), calls=%async_computation.34 | async-start | bytes 524288 | tf_op jit(solution)/shard_map/psum | solution.py:201
  2780.9 439.7 %reduce-scatter.33.cloned.1.call-start = ((), (), s32[]{:S(2)}) async-start(), calls=%async_computation.28 | async-start | bytes 18874368 | tf_op jit(solution)/shard_map/reduce_scatter | solution.py:188
  2793.4 477.3 %all-reduce.21.cloned.1.call-start = ((), (), s32[]{:S(2)}) async-start(), calls=%async_computation.35 | async-start | bytes 354304 | tf_op jit(solution)/shard_map/psum | solution.py:542
  3225.7 132.3 %reduce-scatter.29.cloned.1.call-start = ((), (), s32[]{:S(2)}) async-start(), calls=%async_computation.26 | async-start | bytes 147456 | tf_op jit(solution)/shard_map/reduce_scatter | solution.py:192
  3229.8 155.6 %reduce-scatter.35.cloned.1.call-start = ((), (), s32[]{:S(2)}) async-start(), calls=%async_computation.29 | async-start | bytes 147456 | tf_op jit(solution)/shard_map/reduce_scatter | solution.py:192
  3236.4 437.3 %reduce-scatter.19.cloned.1.call-start = ((), (), s32[]{:S(2)}) async-start(), calls=%async_computation.18 | async-start | bytes 18874368 | tf_op jit(solution)/shard_map/reduce_scatter | solution.py:188
  (155 other events, 8949.0 us)
Sparse Core Ops, SparseCore 0:
  31.2 211.4 all-gather.13
  246.1 62.3 reduce-scatter.38
  312.9 62.4 reduce-scatter.36
  379.2 70.6 all-reduce.16
  454.1 283.8 reduce-scatter.20
  739.9 232.3 all-gather.17
  974.8 125.9 all-gather.15
  1208.9 281.2 reduce-scatter.22
  1527.1 129.0 all-gather.19
  1658.9 123.7 all-gather.9
  1924.6 281.4 reduce-scatter.24
  2209.9 66.9 all-reduce.14
  2281.2 283.8 reduce-scatter.16
  2602.1 129.2 all-gather.11
  2734.6 58.3 reduce-scatter.30
  2796.7 61.8 reduce-scatter.26
  2862.5 70.0 all-reduce.18
  2936.7 283.8 reduce-scatter.32
  3225.8 31.1 all-reduce.20
  3261.1 60.5 reduce-scatter.28
  3325.3 60.0 reduce-scatter.34
  3389.7 283.9 reduce-scatter.18
where the time goes:
time: 3700 us; the launch traced here: 3690 us
  waiting for transfers between devices  2160 us (58%)
  matrix products  637 us (17%)
  blocking collectives  542 us (15%)
  local copies, waits for them, and re-layouts  190 us (5%)
  other arithmetic  113 us (3%)
    reduce_scatter x4, waiting for transfers between devices, sharded_forward(): lax.psum_scatter(sharded_output, 'mp', scatter_dimension=2, tiled=True)  1090 us
    reduce_scatter x2, waiting for transfers between devices, column_backward(): lax.psum_scatter(complete_gradient, 'mp', scatter_dimension=1, tiled=True)  497 us
    all_gather x1, blocking collectives, column_weights(): lax.all_gather(a_gu, 'mp', axis=1, tiled=True)  211 us
    psum x3, waiting for transfers between devices, sharded_forward(): lax.psum(jnp.einsum('ti,kir->tkr', input_portion, adapter_down_factor, pr...  206 us
    all_gather x4, waiting for transfers between devices, column_forward(): entire_rows = lax.all_gather(input_portion, 'mp', axis=1, tiled=True)  176 us
    all_gather x1, blocking collectives, column_weights(): lax.all_gather(a_qkv, 'mp', axis=1, tiled=True)  162 us
    all_gather x2, waiting for transfers between devices, sharded_backward(): lax.all_gather(projection_gradient, 'mp', axis=2, tiled=True)  128 us
    psum x4, blocking collectives, norm_forward(): squares = lax.psum(jnp.sum(residual * residual, axis=1), 'mp')  92.7 us
  transfers between devices with their start and end apart: 24, of which 14 were waited for; matrix products, arithmetic and copies ran while one was open for 18% of the time, Pallas kernels for 0%

commit v1 on v0

v1 whole, which is shorter than its diff:
```python
import math

import jax
import jax.numpy as jnp
from jax import lax
from jax.experimental import pallas as pl
from jax.experimental.pallas import tpu as pltpu
from jax.sharding import Mesh
from jax.sharding import PartitionSpec as P

HD = 128
RANK = 16
SCALE = 2.0
EPS = 1e-05
MASKED = -1e30
HIGHEST = lax.Precision.HIGHEST
MESH = pl.DeviceIdType.MESH
F32 = jnp.float32
BF16 = jnp.bfloat16
LANES = 128
VMEM_LIMIT = 60 * 1024 * 1024


def nt(a, b, precision=None):
    return lax.dot_general(
        a, b, (((1,), (1,)), ((), ())), precision=precision, preferred_element_type=F32
    )


def tn(a, b, precision=None):
    return lax.dot_general(
        a, b, (((0,), (0,)), ((), ())), precision=precision, preferred_element_type=F32
    )


def nn(a, b, precision=None):
    return lax.dot_general(
        a, b, (((1,), (0,)), ((), ())), precision=precision, preferred_element_type=F32
    )


WINDOW = 3


class Comm:
    def __init__(self, nl, nc, tc, fw, out_by_one=0.5, back_by_two=0.5):
        self.nl, self.nc, self.tc, self.fw = nl, nc, tc, fw
        self.square = nl == 4
        self.cut = int(tc * out_by_one) // 16 * 16
        self.back = int(tc * back_by_two) // 16 * 16
        self.c = lax.axis_index("c")
        self.g = lax.axis_index("g")

    def rows(self, i):
        return pl.ds(pl.multiple_of(i * self.tc, self.tc), self.tc)

    def after(self, m):
        return lax.rem(self.g + m, self.nl)

    def before(self, m):
        return lax.rem(self.g + self.nl - m, self.nl)

    def columns(self, c, g):
        return pl.ds(pl.multiple_of((c * self.nl + g) * self.fw, self.fw), self.fw)

    def copy(self, src, dst, send, recv, c, g):
        return pltpu.make_async_remote_copy(
            src_ref=src,
            dst_ref=dst,
            send_sem=send,
            recv_sem=recv,
            device_id={"c": c, "g": g},
            device_id_type=MESH,
        )

    def barrier(self, others=(), one_more=None):
        sem = pltpu.get_barrier_semaphore()
        everyone = [
            {"c": 1 - self.c if other else self.c, "g": self.after(m)}
            for other in (0, 1)
            for m in range(self.nl)
            if (other, m) != (0, 0)
        ] + list(others)
        for device in everyone:
            pl.semaphore_signal(sem, inc=1, device_id=device, device_id_type=MESH)
        if one_more is None:
            pl.semaphore_wait(sem, len(everyone))
        else:
            apart = self.c - lax.axis_index("h")

            @pl.when(apart != 0)
            def _():
                for device in one_more:
                    pl.semaphore_signal(sem, inc=1, device_id=device, device_id_type=MESH)

            pl.semaphore_wait(sem, len(everyone) + len(one_more) * apart * apart)

    def other(self, m):
        if m == 1:
            return self.g + 1 - 2 * lax.rem(self.g, 2)
        return lax.rem(self.g + 2, 4) if m == 2 else 3 - self.g

    def comes_from(self, m):
        if m == 0:
            return self.g
        return self.other(m) if self.square else self.before(m)

    def goes_to(self, m):
        return self.other(m) if self.square else self.after(m)

    def some(self, i, way):
        cut = self.cut
        start, size = (0, cut) if way == 0 else (cut, self.tc - cut)
        return pl.ds(pl.multiple_of(i * self.tc + start, 16), size)

    def ag_refs(self, x, full, own, sd, rd, sc, rc):
        self.x, self.full, self.own = x, full, own
        self.sd, self.rd, self.sc, self.rc = sd, rd, sc, rc

    def ag_steps(self):
        return (1, 2) if self.square else range(1, self.nl)

    def ag_direct(self, i, m):
        rows = self.rows(i)
        return self.copy(
            self.x.at[rows],
            self.full.at[rows, self.columns(self.c, self.g)],
            self.sd.at[i, m],
            self.rd.at[i, m],
            self.c,
            self.goes_to(m),
        )

    def ag_relay(self, i, way):
        rows = self.some(i, way)
        columns = self.columns(self.c, self.other(2 - way))
        return self.copy(
            self.full.at[rows, columns],
            self.full.at[rows, columns],
            self.sd.at[i, 3 * way],
            self.rd.at[i, 3 * way],
            self.c,
            self.other(1 + way),
        )

    def ag_across(self, i, m):
        rows = self.rows(i)
        columns = self.columns(self.c, self.comes_from(m))
        src = self.x.at[rows] if m == 0 else self.full.at[rows, columns]
        return self.copy(
            src,
            self.full.at[rows, columns],
            self.sc.at[i, m],
            self.rc.at[i, m],
            1 - self.c,
            self.g,
        )

    def ag_own(self, i):
        rows = self.rows(i)
        return pltpu.make_async_copy(
            self.x.at[rows],
            self.full.at[rows, self.columns(self.c, self.g)],
            self.own.at[i],
        )

    def ag_send(self, i):
        for m in self.ag_steps():
            self.ag_direct(i, m).start()
        self.ag_across(i, 0).start()
        self.ag_own(i).start()

    def ag_start(self):
        for i in range(min(WINDOW, self.nc)):
            self.ag_send(jnp.int32(i))

    def ag_forward(self, i):
        for m in self.ag_steps():
            self.ag_direct(i, m).wait_recv()
        if self.square:
            for way in (0, 1):
                self.ag_relay(i, way).start()
        for m in self.ag_steps():
            self.ag_across(i, m).start()

    def ag_corner(self, i):
        if self.square:
            for way in (0, 1):
                self.ag_relay(i, way).wait_recv()
            self.ag_across(i, 3).start()

    def ag_step(self, i, more=True):
        @pl.when(i < self.nc)
        def _():
            self.ag_forward(i)

        if more:

            @pl.when(i + WINDOW < self.nc)
            def _():
                self.ag_send(i + WINDOW)

        @pl.when((i >= 1) & (i <= self.nc))
        def _():
            self.ag_corner(i - 1)

    def ag_ahead(self):
        self.ag_step(jnp.int32(0))
        self.ag_step(jnp.int32(1))

    def ag_wait(self, i):
        self.ag_own(i).wait()
        for m in range(self.nl):
            self.ag_across(i, m).wait_recv()

    def ag_drain(self, i):
        for m in self.ag_steps():
            self.ag_direct(i, m).wait_send()
        if self.square:
            for way in (0, 1):
                self.ag_relay(i, way).wait_send()
        for m in range(self.nl):
            self.ag_across(i, m).wait_send()

    def rs_refs(self, sb, cb, gb, s1, r1, s2, r2):
        self.sb, self.cb, self.gb = sb, cb, gb
        self.s1, self.r1, self.s2, self.r2 = s1, r1, s2, r2

    def rs_across(self, i):
        return self.copy(
            self.sb.at[i, 1 - self.c],
            self.cb.at[i],
            self.s1.at[i],
            self.r1.at[i],
            1 - self.c,
            self.g,
        )

    def rs_direct(self, i, m):
        to = self.goes_to(m)
        return self.copy(
            self.sb.at[i, self.c, to],
            self.gb.at[i, m - 1],
            self.s2.at[i, m],
            self.r2.at[i, m],
            self.c,
            to,
        )

    def rs_corner(self, i, way):
        rows = pl.ds(0, self.back) if way == 0 else pl.ds(self.back, self.tc - self.back)
        return self.copy(
            self.sb.at[i, self.c, self.other(3), rows],
            self.gb.at[i, 2, rows],
            self.s2.at[i, 3 * way],
            self.r2.at[i, 3 * way],
            self.c,
            self.other(2 - way),
        )

    def rs_middle(self, i):
        self.rs_across(i).wait_recv()
        for gp in range(self.nl):
            mine = self.sb[i, self.c, gp].astype(F32) + self.cb[i, gp].astype(F32)
            self.sb[i, self.c, gp] = mine.astype(BF16)
        if self.square:
            for way in (0, 1):
                self.rs_corner(i, way).start()
        else:
            for m in range(1, self.nl):
                self.rs_direct(i, m).start()

    def rs_second(self, i):
        if not self.square:
            return
        for way in (0, 1):
            self.rs_corner(i, way).wait_recv()
            rows = pl.ds(0, self.back) if way == 0 else pl.ds(self.back, self.tc - self.back)
            to = self.other(1 + way)
            both = self.sb[i, self.c, to, rows].astype(F32) + self.gb[i, 2, rows].astype(F32)
            self.sb[i, self.c, to, rows] = both.astype(BF16)
        for m in (1, 2):
            self.rs_direct(i, m).start()

    def rs_total(self, i):
        steps = (1, 2) if self.square else range(1, self.nl)
        for m in steps:
            self.rs_direct(i, m).wait_recv()
        total = self.sb[i, self.c, self.g].astype(F32)
        for m in steps:
            total = total + self.gb[i, m - 1].astype(F32)
        return total

    def rs_drain(self, i):
        self.rs_across(i).wait_send()
        if self.square:
            for way in (0, 1):
                self.rs_corner(i, way).wait_send()
        for m in (1, 2) if self.square else range(1, self.nl):
            self.rs_direct(i, m).wait_send()

    def rs_steps(self, i):
        @pl.when((i >= 1) & (i <= self.nc))
        def _():
            self.rs_middle(i - 1)

        @pl.when((i >= 2) & (i <= self.nc + 1))
        def _():
            self.rs_second(i - 2)

    def st_refs(self, st, sa, ss, sr):
        self.st, self.sa, self.ss, self.sr = st, sa, ss, sr

    def st_copy(self, i, other, m):
        rows = self.rows(i)
        place = pl.ds(pl.multiple_of((self.c * self.nl + self.g) * 8, 8), 8)
        return self.copy(
            self.st.at[:, rows],
            self.sa.at[place, rows],
            self.ss.at[i, other * self.nl + m],
            self.sr.at[i, other * self.nl + m],
            1 - self.c if other else self.c,
            self.after(m),
        )

    def st_peers(self):
        return [(o, m) for o in (0, 1) for m in range(self.nl) if (o, m) != (0, 0)]

    def st_send(self, i):
        for o, m in self.st_peers():
            self.st_copy(i, o, m).start()
        place = pl.ds(pl.multiple_of((self.c * self.nl + self.g) * 8, 8), 8)
        self.sa[place, self.rows(i)] = self.st[:, self.rows(i)]

    def st_wait(self, i):
        for o, m in self.st_peers():
            self.st_copy(i, o, m).wait_recv()

    def st_sum(self, i):
        held = self.sa[:, self.rows(i)]
        return tn(held, jnp.full((held.shape[0], LANES), 0.125, F32), HIGHEST)

    def st_drain(self, i):
        for o, m in self.st_peers():
            self.st_copy(i, o, m).wait_send()

    def cs_refs(self, part, held, ss, sr):
        self.part, self.held, self.cs, self.cr = part, held, ss, sr

    def cs_copy(self, other, m):
        c, g = 1 - self.c if other else self.c, self.after(m)
        place = pl.ds(pl.multiple_of((self.c * self.nl + self.g) * 8, 8), 8)
        k = other * self.nl + m
        return self.copy(
            self.part.at[:, self.columns(c, g)], self.held.at[place], self.cs.at[k], self.cr.at[k], c, g
        )

    def cs_start(self, w_ref):
        for role in range(2 * self.nl):
            at = slice(role * self.fw, (role + 1) * self.fw)
            value = w_ref[:, at].astype(F32)
            self.part[:, at] = jnp.broadcast_to(row_sum(value * value), (8, self.fw))
        for o, m in self.st_peers():
            self.cs_copy(o, m).start()
        place = pl.ds(pl.multiple_of((self.c * self.nl + self.g) * 8, 8), 8)
        self.held[place, :] = self.part[:, self.columns(self.c, self.g)]

    def cs_total(self):
        for o, m in self.st_peers():
            self.cs_copy(o, m).wait_recv()
        return row_sum(self.held[...]) * 0.125

    def cs_drain(self):
        for o, m in self.st_peers():
            self.cs_copy(o, m).wait_send()


class Swap:
    def __init__(self, cm):
        self.cm = cm
        self.h = lax.axis_index("h")
        self.moves = cm.c != self.h
        self.partner = {"c": self.h, "h": cm.c}

    def far(self, src, dst, send, recv):
        return pltpu.make_async_remote_copy(
            src_ref=src, dst_ref=dst, send_sem=send, recv_sem=recv, device_id=self.partner, device_id_type=MESH
        )

    def start(self, src, dst, sems):
        @pl.when(self.moves)
        def _():
            self.far(src, dst, sems[0], sems[1]).start()

        @pl.when(jnp.logical_not(self.moves))
        def _():
            pltpu.make_async_copy(src, dst, sems[2]).start()

    def wait(self, src, dst, sems):
        @pl.when(self.moves)
        def _():
            self.far(src, dst, sems[0], sems[1]).wait_recv()

        @pl.when(jnp.logical_not(self.moves))
        def _():
            pltpu.make_async_copy(src, dst, sems[2]).wait()

    def drain(self, src, dst, sems):
        @pl.when(self.moves)
        def _():
            self.far(src, dst, sems[0], sems[1]).wait_send()


PIECES = 2


class RowMove:
    def __init__(self, swap, ny, part, e_ref, w_ref, ws, wr, wl, ys, yr):
        self.swap, self.ny, self.part, self.size = swap, ny, part, part // PIECES
        self.e, self.w = e_ref, w_ref
        self.ws, self.wr, self.wl, self.ys, self.yr = ws, wr, wl, ys, yr
        self.y = lax.axis_index("y")

    def rows(self, y, p):
        return pl.ds(pl.multiple_of(y * self.part + p * self.size, 16), self.size)

    def far(self, p):
        mine = self.rows(self.y, p)
        return self.swap.far(self.e.at[mine], self.w.at[mine], self.ws.at[p], self.wr.at[p])

    def near(self):
        every = pl.ds(0, self.part * self.ny)
        return pltpu.make_async_copy(self.e.at[every], self.w.at[every], self.wl)

    def shared(self, k, p, y):
        where = self.rows(y, p)
        return pltpu.make_async_remote_copy(
            src_ref=self.w.at[where], dst_ref=self.w.at[where],
            send_sem=self.ys.at[k - 1, p], recv_sem=self.yr.at[k - 1, p],
            device_id={"y": lax.rem(self.y + k, self.ny)}, device_id_type=MESH,
        )

    def start(self):
        @pl.when(self.swap.moves)
        def _():
            for p in range(PIECES):
                self.far(p).start()

        @pl.when(jnp.logical_not(self.swap.moves))
        def _():
            self.near().start()

    def pass_on(self):
        @pl.when(self.swap.moves)
        def _():
            for p in range(PIECES):
                self.far(p).wait_recv()
                for k in range(1, self.ny):
                    self.shared(k, p, self.y).start()

    def wait(self):
        @pl.when(self.swap.moves)
        def _():
            for k in range(1, self.ny):
                for p in range(PIECES):
                    self.shared(k, p, lax.rem(self.y + self.ny - k, self.ny)).wait_recv()

        @pl.when(jnp.logical_not(self.swap.moves))
        def _():
            self.near().wait()

    def drain(self):
        @pl.when(self.swap.moves)
        def _():
            for p in range(PIECES):
                self.far(p).wait_send()
                for k in range(1, self.ny):
                    self.shared(k, p, self.y).wait_send()


def row_move_scratch(ny):
    dma = pltpu.SemaphoreType.DMA
    between = dma((max(ny - 1, 1), PIECES))
    return [dma((PIECES,)), dma((PIECES,)), dma, between, between]


class Spread:
    def __init__(self, cm, ny, e_ref, w_ref, hs, hr, ps, pr, pn, ys, yr):
        self.cm, self.ny, self.e, self.w = cm, ny, e_ref, w_ref
        self.hs, self.hr, self.ps, self.pr, self.pn, self.ys, self.yr = hs, hr, ps, pr, pn, ys, yr
        self.y, self.h = lax.axis_index("y"), lax.axis_index("h")
        self.part = cm.fw // ny

    def place(self, hh, gg, yy):
        return self.w.at[
            pl.ds(pl.multiple_of((hh * self.cm.nl + gg) * self.cm.fw + yy * self.part, self.part), self.part)
        ]

    def piece(self, m):
        cm, to = self.cm, self.cm.after(m)
        return cm.copy(
            self.e.at[to], self.place(self.h, cm.g, self.y), self.ps.at[m], self.pr.at[m], cm.c, to
        )

    def here(self):
        return pltpu.make_async_copy(
            self.e.at[self.cm.g], self.place(self.h, self.cm.g, self.y), self.pn
        )

    def crossed(self, m, hh):
        where = self.place(hh, self.cm.before(m), self.y)
        return pltpu.make_async_remote_copy(
            src_ref=where, dst_ref=where, send_sem=self.hs.at[m], recv_sem=self.hr.at[m],
            device_id={"h": 1 - self.h}, device_id_type=MESH,
        )

    def shared(self, side, m, k, yy):
        where = self.place(self.h if side == 0 else 1 - self.h, self.cm.before(m), yy)
        return pltpu.make_async_remote_copy(
            src_ref=where, dst_ref=where,
            send_sem=self.ys.at[side, m, k - 1], recv_sem=self.yr.at[side, m, k - 1],
            device_id={"y": lax.rem(self.y + k, self.ny)}, device_id_type=MESH,
        )

    def start(self):
        self.here().start()
        for m in range(1, self.cm.nl):
            self.piece(m).start()

    def pass_own(self, m):
        if m == 0:
            self.here().wait()
        else:
            self.piece(m).wait_recv()
        if m < 2:
            self.crossed(m, self.h).start()
        for k in range(1, self.ny):
            self.shared(0, m, k, self.y).start()

    def pass_crossed(self, m):
        self.crossed(m, 1 - self.h).wait_recv()
        if m + 2 < self.cm.nl:
            self.crossed(m + 2, self.h).start()
        for k in range(1, self.ny):
            self.shared(1, m, k, self.y).start()

    def wait(self):
        for side in (0, 1):
            for m in range(self.cm.nl):
                for k in range(1, self.ny):
                    self.shared(side, m, k, lax.rem(self.y + self.ny - k, self.ny)).wait_recv()

    def drain(self):
        for m in range(self.cm.nl):
            self.crossed(m, self.h).wait_send()
            if m > 0:
                self.piece(m).wait_send()
            for side in (0, 1):
                for k in range(1, self.ny):
                    self.shared(side, m, k, self.y).wait_send()


def spread_scratch(ny, nl):
    dma = pltpu.SemaphoreType.DMA
    return [
        dma((nl,)),
        dma((nl,)),
        dma((nl,)),
        dma((nl,)),
        dma,
        dma((2, nl, max(ny - 1, 1))),
        dma((2, nl, max(ny - 1, 1))),
    ]


def movers(ny):
    y, h = lax.axis_index("y"), lax.axis_index("h")
    return [{"y": lax.rem(y + k, ny)} for k in range(1, ny)] + [{"h": 1 - h}]


def ag_scratch(nl, nc, t, d):
    return [
        pltpu.VMEM((t, d), BF16),
        pltpu.SemaphoreType.DMA((nc,)),
        pltpu.SemaphoreType.DMA((nc, nl)),
        pltpu.SemaphoreType.DMA((nc, nl)),
        pltpu.SemaphoreType.DMA((nc, nl)),
        pltpu.SemaphoreType.DMA((nc, nl)),
    ]


def rs_scratch(nl, nc, tc, fw):
    return [
        pltpu.VMEM((nc, 2, nl, tc, fw), BF16),
        pltpu.VMEM((nc, nl, tc, fw), BF16),
        pltpu.VMEM((nc, nl - 1, tc, fw), BF16),
        pltpu.SemaphoreType.DMA((nc,)),
        pltpu.SemaphoreType.DMA((nc,)),
        pltpu.SemaphoreType.DMA((nc, nl)),
        pltpu.SemaphoreType.DMA((nc, nl)),
    ]


def st_scratch(nl, nc, t):
    return [
        pltpu.VMEM((2 * nl * 8, t), F32),
        pltpu.SemaphoreType.DMA((nc, 2 * nl)),
        pltpu.SemaphoreType.DMA((nc, 2 * nl)),
    ]


def cs_scratch(nl, d, fw):
    return [
        pltpu.VMEM((8, d), F32),
        pltpu.VMEM((2 * nl * 8, fw), F32),
        pltpu.SemaphoreType.DMA((2 * nl,)),
        pltpu.SemaphoreType.DMA((2 * nl,)),
    ]


VM = pl.BlockSpec(memory_space=pltpu.VMEM)
SM = pl.BlockSpec(memory_space=pltpu.SMEM)
ANY = pl.BlockSpec(memory_space=pl.ANY)


class Background:
    def __init__(self, loads, stores, step):
        self.loads, self.stores, self.step = loads, stores, step
        for copy in loads:
            copy.start()

    def ready(self):
        for copy in self.loads:
            copy.wait()

    def copy(self, k, i):
        held, out, sems = self.stores[k]
        rows = pl.ds(pl.multiple_of(i * self.step, self.step), self.step)
        return pltpu.make_async_copy(held.at[rows], out.at[rows], sems.at[i])

    def store(self, i, *which):
        for k in which:
            self.copy(k, i).start()

    def stored(self, i):
        for k in self.stores:
            self.copy(k, i).wait()


def call(kernel, name, outs, in_specs, out_specs, scratch, collective, us, args, late=(), flow=(), step=1):
    extra = {}
    if collective is not None:
        extra = {"collective_id": collective, "has_side_effects": True}
    single = not isinstance(outs, tuple)
    results = (outs,) if single else outs
    in_specs, out_specs = list(in_specs), [out_specs] if single else list(out_specs)
    n_in, n_out, n_scratch = len(args), len(results), len(scratch)
    dma = pltpu.SemaphoreType.DMA
    more = []
    for k in late:
        in_specs[k] = ANY
        more += [pltpu.VMEM(args[k].shape, args[k].dtype), dma]
    for k in flow:
        out_specs[k] = ANY
        more += [pltpu.VMEM(results[k].shape, results[k].dtype), dma((results[k].shape[0] // step,))]

    def whole(*refs):
        ins, results_here = list(refs[:n_in]), list(refs[n_in : n_in + n_out])
        own = refs[n_in + n_out : n_in + n_out + n_scratch]
        extras = list(refs[n_in + n_out + n_scratch :])
        loads, stores = [], {}
        for k in late:
            held, sem = extras.pop(0), extras.pop(0)
            loads.append(pltpu.make_async_copy(ins[k], held, sem))
            ins[k] = held
        for k in flow:
            held, sems = extras.pop(0), extras.pop(0)
            stores[k] = (held, results_here[k], sems)
            results_here[k] = held
        kernel(Background(loads, stores, step), *ins, *results_here, *own)

    return pl.pallas_call(
        whole,
        name=name,
        out_shape=outs,
        in_specs=in_specs,
        out_specs=out_specs[0] if single else tuple(out_specs),
        scratch_shapes=scratch + more,
        compiler_params=pltpu.CompilerParams(vmem_limit_bytes=VMEM_LIMIT, **extra),
        cost_estimate=pl.CostEstimate(
            flops=int(us * 5e8), bytes_accessed=int(us * 3e6), transcendentals=0
        ),
    )(*args)


def shape(s, dtype):
    return jax.ShapeDtypeStruct(s, dtype)


def ones_rows(values):
    folded = values[:, :LANES]
    for k in range(1, values.shape[1] // LANES):
        folded = folded + values[:, k * LANES : (k + 1) * LANES]
    return nt(jnp.ones((8, LANES), F32), folded, HIGHEST)


def row_sum(values):
    return jnp.sum(values, axis=0, keepdims=True)


def merged_tile(frozen, down, up):
    return frozen.astype(F32) + SCALE * nn(down, up, HIGHEST)


def qkv_forward(
    cfg, ny, npad, nf, x_in, w_qkv, a_qkv, b_qkv, tail_qkv, gains, rows_out, small, small_gu, cosine, sine,
    w_gu, a_gu, b_gu, tail_gu,
):
    t, fw, d, nl, nc, tc = cfg
    width = 3 * fw
    wide = width + LANES
    part = fw // ny
    ff_half = w_gu.shape[2] // 2

    def kernel(
        io, x_ref, wq_hbm, aq_ref, bq_ref, tq_ref, gain_ref, eo_ref, m_ref, mg_ref, cos_ref, sin_ref,
        wg_hbm, ag_ref, bg_ref, tg_ref,
        xs_ref, w_ref, wo_ref, ms_ref, mgs_ref, sc_ref, sq_ref, qkv_ref, lora_ref, rate_ref, eg_ref, out_ref,
        full, own, sd, rd, sc, rc, keep, xs_s, xs_r, xs_l, small_sems,
        hs, hr, ps, pr, pn, ys, yr, os, orr, ol, oys, oyr,
        e_ref, wq, wg, wload,
    ):
        cm = Comm(nl, nc, tc, fw, out_by_one=0.9375)
        cm.ag_refs(xs_ref, full, own, sd, rd, sc, rc)
        swap = Swap(cm)
        weights = Spread(cm, ny, e_ref, w_ref, hs, hr, ps, pr, pn, ys, yr)
        mine = pl.ds(pl.multiple_of(weights.y * part, part), part)
        load_q = pltpu.make_async_copy(
            wq_hbm.at[:, mine, pl.ds(pl.multiple_of(cm.c * (d // 2), LANES), d // 2)], wq, wload.at[0]
        )
        load_g = pltpu.make_async_copy(
            wg_hbm.at[:, mine, pl.ds(pl.multiple_of(cm.c * ff_half, LANES), ff_half)], wg, wload.at[1]
        )
        load_q.start()
        load_g.start()
        output = RowMove(swap, ny, fw // ny, eo_ref, wo_ref, os, orr, ol, oys, oyr)
        cm.barrier(movers(ny), [swap.partner])

        def token_swap(i):
            rows = cm.rows(i)
            return x_ref.at[rows], xs_ref.at[rows], (xs_s.at[i], xs_r.at[i], xs_l.at[i])

        m_swap = (m_ref, ms_ref, tuple(small_sems.at[k] for k in range(3)))
        mg_swap = (mg_ref, mgs_ref, tuple(small_sems.at[k] for k in range(3, 6)))

        def start_swap(i, carry_on):
            swap.start(*token_swap(i))
            return carry_on

        lax.fori_loop(0, min(WINDOW, nc), start_swap, 0)
        swap.start(*m_swap)
        swap.start(*mg_swap)
        load_q.wait()
        gain_attn, gain_ffn = gain_ref[mine, 0:1], gain_ref[mine, 1:2]
        for gg in range(nl):
            columns = pl.ds(pl.multiple_of((cm.c * nl + gg) * fw, fw), fw)
            for k in range(3):
                tile = merged_tile(wq[k, :, gg * fw : (gg + 1) * fw], aq_ref[k, mine, :], bq_ref[k, :, columns])
                e_ref[gg, :, k * fw : (k + 1) * fw] = (tile * gain_attn).astype(BF16)
            e_ref[gg, :, width:] = tq_ref[mine, :]
        weights.start()

        def gate_up(gg):
            off = gg * nf % LANES
            window = -(-(off + nf) // LANES) * LANES
            for k in range(2):
                raw = wg[k, :, gg * nf - off : gg * nf - off + window].astype(F32)
                if off:
                    raw = pltpu.roll(raw, window - off, 1)
                tile = merged_tile(raw[:, :npad], ag_ref[k, mine, :], bg_ref[k, cm.c * nl + gg]) * gain_ffn
                lane = lax.broadcasted_iota(jnp.int32, tile.shape, 1)
                eg_ref[gg, :, k * npad : (k + 1) * npad] = jnp.where(
                    lane < nf, tile, tg_ref[k, mine, :].astype(F32)
                ).astype(BF16)

        def gather(i, carry_on):
            swap.wait(*token_swap(i))

            @pl.when(i + WINDOW < nc)
            def _():
                swap.start(*token_swap(i + WINDOW))

            cm.ag_send(i)
            return carry_on

        def forward(i, carry_on):
            cm.ag_step(i, more=False)
            return carry_on

        weights.pass_own(0)
        half = nc // 2
        lax.fori_loop(0, half, gather, 0)
        weights.pass_own(1)
        lax.fori_loop(half, nc, gather, 0)
        for m in range(2, nl):
            weights.pass_own(m)
        load_g.wait()
        io.ready()
        for m in range(nl):
            lax.fori_loop(nc * m // nl, nc * (m + 1) // nl, forward, 0)
            gate_up(m)
            weights.pass_crossed(m)
        output.start()
        cm.ag_step(jnp.int32(nc), more=False)

        def stored(i):
            rows = cm.rows(i)
            return pltpu.make_async_copy(full.at[rows], out_ref.at[rows], keep.at[i])

        def rates(i, carry_on):
            cm.ag_wait(i)
            stored(i).start()
            wide_block = full[cm.rows(i), :].astype(F32)
            rate = lax.rsqrt(jnp.sum(wide_block * wide_block, axis=1, keepdims=True) / d + EPS)
            rate_ref[cm.rows(i), :] = jnp.broadcast_to(rate, (tc, LANES))
            return carry_on

        lax.fori_loop(0, nc, rates, 0)
        weights.wait()
        output.pass_on()

        def squares(i, total):
            rows = pl.ds(pl.multiple_of(i * fw, fw), fw)
            tail = w_ref[rows, width:].astype(F32)
            gain = tail[:, 3 * RANK : 3 * RANK + 1] + tail[:, 3 * RANK + 1 : 3 * RANK + 2]
            value = w_ref[rows, :width].astype(F32) * (1.0 / gain)
            return total + row_sum(value * value)

        square = lax.fori_loop(0, 2 * nl, squares, jnp.zeros((1, width), F32))
        swap.wait(*m_swap)
        sq_ref[...] = jnp.broadcast_to(square, (8, width))
        for k in range(3):
            at = slice(k * fw, (k + 1) * fw)
            sc_ref[:, at] = jnp.broadcast_to(ms_ref[k : k + 1, :] * lax.rsqrt(square[:, at]), (8, fw))
        sc_ref[:, width:] = jnp.ones((8, LANES), F32)

        big = 2 * tc if nc % 2 == 0 else tc

        def body(i, carry_on):
            rows = pl.ds(pl.multiple_of(i * big, big), big)
            out = nn(full[rows, :], w_ref[...]) * rate_ref[rows, 0:1] * sc_ref[0:1, :]
            cosine_here, sine_here = cos_ref[rows, :], sin_ref[rows, :]
            for k in range(3):
                for hd in range(fw // HD):
                    at = k * fw + hd * HD
                    value = out[:, at : at + HD]
                    if k < 2:
                        value = value * cosine_here + pltpu.roll(value, HD // 2, 1) * sine_here
                    qkv_ref[rows, at : at + HD] = value.astype(BF16)
            lora_ref[rows, :] = out[:, width:].astype(BF16)
            for k in range(big // tc):
                io.store(i * (big // tc) + k, 7, 8, 9)
            return carry_on

        lax.fori_loop(0, t // big, body, 0)
        output.wait()
        swap.wait(*mg_swap)

        def drain(i, carry_on):
            cm.ag_drain(i)
            stored(i).wait()
            io.stored(i)
            swap.drain(*token_swap(i))
            return carry_on

        lax.fori_loop(0, nc, drain, 0)
        swap.drain(*m_swap)
        swap.drain(*mg_swap)
        weights.drain()
        output.drain()

    dma = pltpu.SemaphoreType.DMA
    return call(
        kernel,
        "qkv_forward",
        (
            shape((t, fw), BF16),
            shape((d, wide), BF16),
            shape(rows_out.shape, BF16),
            shape(small.shape, F32),
            shape(small_gu.shape, F32),
            shape((8, wide), F32),
            shape((8, width), F32),
            shape((t, width), BF16),
            shape((t, LANES), BF16),
            shape((t, LANES), F32),
            shape((nl, part, 2 * npad), BF16),
            shape((t, d), BF16),
        ),
        [VM, ANY, VM, VM, VM, VM, ANY, VM, VM, VM, VM, ANY, VM, VM, VM],
        (VM,) * 11 + (ANY,),
        ag_scratch(nl, nc, t, d)
        + [dma((nc,))] * 4
        + [dma((6,))]
        + spread_scratch(ny, nl)
        + row_move_scratch(ny)
        + [
            pltpu.VMEM((nl, part, wide), BF16),
            pltpu.VMEM((3, part, d // 2), BF16),
            pltpu.VMEM((2, part, ff_half), BF16),
            dma((2,)),
        ],
        1,
        90,
        (
            x_in, w_qkv, a_qkv, b_qkv, tail_qkv, gains, rows_out, small, small_gu, cosine, sine,
            w_gu, a_gu, b_gu, tail_gu,
        ),
        late=(9, 10, 12, 13, 14),
        flow=(7, 8, 9),
        step=tc,
    )


def allowed_of(key_segment, query_segment, j, i, block):
    key_at = j * block + lax.broadcasted_iota(jnp.int32, (block, block), 0)
    query_at = i * block + lax.broadcasted_iota(jnp.int32, (block, block), 1)
    return (key_segment == query_segment) & (key_at <= query_at)


def attention_forward(cfg, qkv, seg_column, seg_row, first_block, block):
    t, fw = cfg[0], cfg[1]
    heads = fw // HD

    def kernel(io, qkv_ref, sc_ref, sr_ref, first_ref, out_ref, lse_ref):
        def at(i):
            return pl.ds(pl.multiple_of(i * block, block), block)

        def columns(k, hd):
            return slice(k * fw + hd * HD, k * fw + (hd + 1) * HD)

        def one_query(i, carry_on):
            queries = [qkv_ref[at(i), columns(0, hd)] for hd in range(heads)]
            query_segment = sr_ref[0:1, at(i)]

            def one_key(j, carry):
                allowed = allowed_of(sc_ref[at(j), 0:1], query_segment, j, i, block)
                out = []
                for hd in range(heads):
                    top, total, acc = carry[hd]
                    s = nt(qkv_ref[at(j), columns(1, hd)], queries[hd]) * (HD**-0.5)
                    s = jnp.where(allowed, s, MASKED)
                    new = jnp.maximum(top, jnp.max(s, axis=0, keepdims=True))
                    p = jnp.exp(s - new)
                    shrink = jnp.exp(top - new)
                    total = total * shrink + jnp.sum(p, axis=0, keepdims=True)
                    acc = acc * shrink + tn(qkv_ref[at(j), columns(2, hd)], p.astype(BF16))
                    out.append((new, total, acc))
                return tuple(out)

            first = (
                jnp.full((1, block), MASKED, F32),
                jnp.zeros((1, block), F32),
                jnp.zeros((HD, block), F32),
            )
            out = lax.fori_loop(first_ref[i], i + 1, one_key, (first,) * heads)
            for hd in range(heads):
                top, total, acc = out[hd]
                out_ref[at(i), hd * HD : (hd + 1) * HD] = (acc / total).T.astype(BF16)
                lse_ref[hd * 8 : hd * 8 + 8, at(i)] = jnp.broadcast_to(
                    top + jnp.log(total), (8, block)
                )
            return carry_on

        lax.fori_loop(0, t // block, one_query, 0)

    return call(
        kernel,
        "attention_forward",
        (shape((t, fw), BF16), shape((heads * 8, t), F32)),
        [VM, VM, VM, SM],
        (VM, VM),
        [],
        None,
        15,
        (qkv, seg_column, seg_row, first_block),
    )


def out_forward(cfg, ny, npad, attended, weights, x, magnitude, blocks, w_down, a_down, b_down):
    t, fw, d, nl, nc, tc = cfg
    wide = blocks.shape[2]
    nf = w_down.shape[0]
    part = -(-(-(-nf // ny)) // (16 * PIECES)) * 16 * PIECES
    tiles = 2 * nl

    def kernel(
        io, a_ref, w_ref, x_ref, m_ref, e_ref, wdown_ref, ad_ref, bd_ref,
        mid_ref, u_ref, st_ref, sc_ref, sq_ref, lora_ref, wg_ref, wd_ref,
        sb, cb, gb, s1, r1, s2, r2, cpart, cheld, css, csr,
        hs, hr, ps, pr, pn, ys, yr, dws, dwr, dwl, dys, dyr, ed_ref,
    ):
        cm = Comm(nl, nc, tc, fw, back_by_two=0.0625)
        cm.rs_refs(sb, cb, gb, s1, r1, s2, r2)
        cm.cs_refs(cpart, cheld, css, csr)
        columns = Spread(cm, ny, e_ref, wg_ref, hs, hr, ps, pr, pn, ys, yr)
        swap = Swap(cm)
        down_rows = RowMove(swap, ny, part, ed_ref, wd_ref, dws, dwr, dwl, dys, dyr)
        cm.barrier(movers(ny), [swap.partner])
        columns.start()
        cm.cs_start(w_ref)
        columns.pass_own(0)
        if part * ny > nf:
            ed_ref[nf:, :] = jnp.zeros((part * ny - nf, ed_ref.shape[1]), BF16)
        if part * ny < npad:
            wd_ref[part * ny :, :] = jnp.zeros((npad - part * ny, wd_ref.shape[1]), BF16)
        io.ready()
        ed_ref[:nf, d:] = jnp.zeros((nf, LANES), BF16)
        ed_ref[:nf, d : d + RANK] = ad_ref[...].astype(BF16)

        def down_tile(k):
            at = pl.ds(pl.multiple_of(k * fw, fw), fw)
            ed_ref[:nf, at] = merged_tile(wdown_ref[:, at], ad_ref[...], bd_ref[:, at]).astype(BF16)

        def body(i, carry_on):
            @pl.when(i < nc)
            def _():
                block = a_ref[cm.rows(i), :]
                for role in range(2 * nl):
                    sb[i, role // nl, role % nl] = nn(
                        block, w_ref[:, role * fw : (role + 1) * fw]
                    ).astype(BF16)
                cm.rs_across(i).start()
                lora_ref[cm.rows(i), :] = nn(block, w_ref[:, d:]).astype(BF16)
                io.store(i, 5)

            cm.rs_steps(i)

            @pl.when(i == 3)
            def _():
                total = cm.cs_total()
                sq_ref[...] = jnp.broadcast_to(total, (8, fw))
                sc_ref[...] = jnp.broadcast_to(m_ref[3:4, :] * lax.rsqrt(total), (8, fw))
                for m in range(2, nl):
                    columns.pass_own(m)

            @pl.when(i == 1)
            def _():
                columns.pass_own(1)

            @pl.when((i >= 1) & (i <= tiles))
            def _():
                down_tile(i - 1)

            @pl.when(i == min(6, nc + 1))
            def _():
                columns.pass_crossed(0)

            @pl.when(i == nc + 2)
            def _():
                columns.pass_crossed(1)

            @pl.when((i >= 3) & (i <= nc + 2))
            def _():
                rows = cm.rows(i - 3)
                middle = x_ref[rows, :].astype(F32) + cm.rs_total(i - 3) * sc_ref[0:1, :]
                mid_ref[rows, :] = middle
                u_ref[rows, :] = middle.astype(BF16)
                st_ref[:, rows] = ones_rows(middle * middle)
                io.store(i - 3, 0, 1)

            return carry_on

        lax.fori_loop(0, max(nc + 3, tiles + 1), body, 0)

        def drain(i, carry_on):
            cm.rs_drain(i)
            io.stored(i)
            return carry_on

        down_rows.start()
        for m in range(2, nl):
            columns.pass_crossed(m)
        down_rows.pass_on()
        columns.wait()
        down_rows.wait()
        lax.fori_loop(0, nc, drain, 0)
        cm.cs_drain()
        columns.drain()
        down_rows.drain()

    return call(
        kernel,
        "out_forward",
        (
            shape((t, fw), F32),
            shape((t, fw), BF16),
            shape((8, t), F32),
            shape((8, fw), F32),
            shape((8, fw), F32),
            shape((t, LANES), BF16),
            shape((d, wide), BF16),
            shape((npad, d + LANES), BF16),
        ),
        [VM] * 4 + [ANY, VM, VM, VM],
        (VM,) * 6 + (ANY, VM),
        rs_scratch(nl, nc, tc, fw)
        + cs_scratch(nl, d, fw)
        + spread_scratch(ny, nl)
        + row_move_scratch(ny)
        + [pltpu.VMEM((part * ny, d + LANES), BF16)],
        2,
        90,
        (attended, weights, x, magnitude, blocks, w_down, a_down, b_down),
        late=(5, 6, 7),
        flow=(0, 1, 5),
        step=tc,
    )


def ffn_forward(cfg, npad, nf, u, stats, w_gu, m_gu, w_down, small, middle, cotangent):
    t, fw, d, nl, nc, tc = cfg

    def kernel(
        io, u_ref, st_ref, wg_ref, mg_ref, wd_ref, m_ref, mid_ref, cin_ref,
        gu_ref, hid_ref, out_ref, gm_ref, rate_ref, gp_ref, sg_ref, qg_ref, sd_ref, qd_ref, lora_ref, cot_ref, uf_ref,
        full, own, sd, rd, sc, rc, sb, cb, gb, s1, r1, s2, r2, sa, ss, sr, cpart, cheld, css, csr, keep,
        stage, cs_s, cs_r, cs_l, bs_s, bs_r, bs_l,
    ):
        cm = Comm(nl, nc, tc, fw, out_by_one=0.75, back_by_two=0.25)
        cm.ag_refs(u_ref, full, own, sd, rd, sc, rc)
        cm.rs_refs(sb, cb, gb, s1, r1, s2, r2)
        cm.st_refs(st_ref, sa, ss, sr)
        cm.cs_refs(cpart, cheld, css, csr)
        swap = Swap(cm)
        cm.barrier((), [swap.partner])

        def cot_swap(i):
            rows = cm.rows(i)
            return cin_ref.at[rows], cot_ref.at[rows], (cs_s.at[i], cs_r.at[i], cs_l.at[i])

        def out_swap(i):
            rows = cm.rows(i)
            return stage.at[rows], out_ref.at[rows], (bs_s.at[i], bs_r.at[i], bs_l.at[i])

        def stats_out(i, carry_on):
            cm.st_send(i)
            return carry_on

        lax.fori_loop(0, nc, stats_out, 0)
        cm.ag_start()
        io.ready()

        def cot_out(i, carry_on):
            swap.start(*cot_swap(i))
            return carry_on


        def squares(i, total):
            rows = pl.ds(pl.multiple_of(i * fw, fw), fw)
            gain = (
                wg_ref[rows, nf + RANK : nf + RANK + 1].astype(F32)
                + wg_ref[rows, nf + RANK + 1 : nf + RANK + 2].astype(F32)
            )
            value = wg_ref[rows, :].astype(F32) * (1.0 / gain)
            return total + row_sum(value * value)

        square = lax.fori_loop(0, 2 * nl, squares, jnp.zeros((1, 2 * npad), F32))
        column = lax.rem(lax.broadcasted_iota(jnp.int32, (1, 2 * npad), 1), npad)
        square = jnp.where(column < nf, square, 1.0)
        qg_ref[...] = jnp.broadcast_to(square, (8, 2 * npad))
        sg_ref[...] = jnp.broadcast_to(mg_ref[...] * lax.rsqrt(square), (8, 2 * npad))
        cm.ag_ahead()
        gm_ref[...] = jnp.zeros_like(gm_ref)

        def stored(i):
            rows = cm.rows(i)
            return pltpu.make_async_copy(full.at[rows], uf_ref.at[rows], keep.at[i])

        cm.cs_start(wd_ref)
        lax.fori_loop(0, nc, cot_out, 0)

        def body(i, carry_on):
            @pl.when(i < nc)
            def _():
                cm.ag_step(i + 2)
                cm.ag_wait(i)
                cm.st_wait(i)
                stored(i).start()
                rows = cm.rows(i)
                rate = lax.rsqrt(cm.st_sum(i) / d + EPS)
                rate_ref[rows, :] = rate
                out = nn(full[rows, :], wg_ref[...]) * rate[:, 0:1] * sg_ref[0:1, :]
                gu_ref[rows, :] = out.astype(BF16)
                gate, up = out[:, :npad], out[:, npad:]
                hidden = (gate / (1.0 + jnp.exp(-gate)) * up).astype(BF16)
                hid_ref[rows, :] = hidden
                for role in range(2 * nl):
                    sb[i, role // nl, role % nl] = nn(
                        hidden, wd_ref[:, role * fw : (role + 1) * fw]
                    ).astype(BF16)
                cm.rs_across(i).start()
                lora_ref[rows, :] = nn(hidden, wd_ref[:, d:]).astype(BF16)
                io.store(i, 0, 1, 4, 10)

            cm.rs_steps(i)

            @pl.when(i == 3)
            def _():
                total = cm.cs_total()
                qd_ref[...] = jnp.broadcast_to(total, (8, fw))
                sd_ref[...] = jnp.broadcast_to(m_ref[4:5, :] * lax.rsqrt(total), (8, fw))

            @pl.when(i >= 3)
            def _():
                rows = cm.rows(i - 3)
                down = cm.rs_total(i - 3) * sd_ref[0:1, :]
                stage[rows, :] = (mid_ref[rows, :] + down).astype(BF16)
                swap.start(*out_swap(i - 3))
                swap.wait(*cot_swap(i - 3))
                seed = cot_ref[rows, :].astype(F32)
                gm_ref[0:1, :] += row_sum(seed * down)
                gp_ref[rows, :] = (seed * sd_ref[0:1, :]).astype(BF16)
                io.store(i - 3, 5)

            return carry_on

        lax.fori_loop(0, nc + 3, body, 0)

        def drain(i, carry_on):
            cm.ag_drain(i)
            cm.rs_drain(i)
            cm.st_drain(i)
            stored(i).wait()
            io.stored(i)
            swap.wait(*out_swap(i))
            swap.drain(*out_swap(i))
            swap.drain(*cot_swap(i))
            return carry_on

        lax.fori_loop(0, nc, drain, 0)
        cm.cs_drain()

    dma = pltpu.SemaphoreType.DMA
    return call(
        kernel,
        "ffn_forward",
        (
            shape((t, 2 * npad), BF16),
            shape((t, npad), BF16),
            shape((t, fw), BF16),
            shape((8, fw), F32),
            shape((t, LANES), F32),
            shape((t, fw), BF16),
            shape((8, 2 * npad), F32),
            shape((8, 2 * npad), F32),
            shape((8, fw), F32),
            shape((8, fw), F32),
            shape((t, LANES), BF16),
            shape((t, fw), BF16),
            shape((t, d), BF16),
        ),
        [VM] * 8,
        (VM,) * 12 + (ANY,),
        ag_scratch(nl, nc, t, d)
        + rs_scratch(nl, nc, tc, fw)
        + st_scratch(nl, nc, t)
        + cs_scratch(nl, d, fw)
        + [dma((nc,)), pltpu.VMEM((t, fw), BF16)]
        + [dma((nc,))] * 6,
        3,
        110,
        (u, stats, w_gu, m_gu, w_down, small, middle, cotangent),
        late=(2, 4, 6),
        flow=(0, 1, 4, 5, 10),
        step=tc,
    )


def ffn_backward(cfg, npad, gp, gu, w_gu, sc_gu, b_gu, w_down, b_down, rate, cotangent, middle, x, sc_out):
    t, fw, d, nl, nc, tc = cfg

    def kernel(
        io, gp_ref, gu_hbm, wg_ref, sg_ref, bg_ref, wd_ref, bd_ref, rate_ref, cot_ref, mid_ref, x_ref, so_ref,
        dm_ref, go_ref, gmo_ref, gm_ref, lg_ref, ld_ref, dp_hbm, gf_ref,
        full, own, sd, rd, sc, rc, sb, cb, gb, s1, r1, s2, r2, sa, ss, sr, st, gu_s, keep, load, save,
    ):
        cm = Comm(nl, nc, tc, fw)
        cm.ag_refs(gp_ref, full, own, sd, rd, sc, rc)
        cm.rs_refs(sb, cb, gb, s1, r1, s2, r2)
        cm.st_refs(st, sa, ss, sr)

        def loaded(i):
            rows = cm.rows(i)
            return pltpu.make_async_copy(gu_hbm.at[rows], gu_s.at[rows], load.at[i])

        def saved(i):
            rows = cm.rows(i)
            return pltpu.make_async_copy(gu_s.at[rows], dp_hbm.at[rows], save.at[i])

        def stored(i):
            rows = cm.rows(i)
            return pltpu.make_async_copy(full.at[rows], gf_ref.at[rows], keep.at[i])

        cm.barrier()
        cm.ag_start()

        def start_loads(i, carry_on):
            loaded(i).start()
            return carry_on

        lax.fori_loop(0, nc, start_loads, 0)
        cm.ag_ahead()
        io.ready()
        gm_ref[...] = jnp.zeros_like(gm_ref)
        gmo_ref[...] = jnp.zeros_like(gmo_ref)

        def body(i, carry_on):
            @pl.when(i < nc)
            def _():
                cm.ag_step(i + 2)
                cm.ag_wait(i)
                stored(i).start()
                loaded(i).wait()
                rows = cm.rows(i)
                block = full[rows, :]
                dh = nt(block, wd_ref[:, :d])
                ld_ref[rows, :] = nt(block, bd_ref[...]).astype(BF16)
                gate = gu_s[rows, :npad].astype(F32)
                up = gu_s[rows, npad:].astype(F32)
                sig = 1.0 / (1.0 + jnp.exp(-gate))
                dgate = dh * up * (sig * (1.0 + gate * (1.0 - sig)))
                dup = dh * (gate * sig)
                pg, pu = dgate * gate, dup * up
                gm_ref[0:1, :npad] += jnp.sum(pg, axis=0, keepdims=True)
                gm_ref[0:1, npad:] += jnp.sum(pu, axis=0, keepdims=True)
                st[:, rows] = ones_rows(pg + pu)
                cm.st_send(i)
                gu_s[rows, :npad] = (dgate * sg_ref[0:1, :npad]).astype(BF16)
                gu_s[rows, npad:] = (dup * sg_ref[0:1, npad:]).astype(BF16)
                saved(i).start()
                dp = gu_s[rows, :]
                lg_ref[rows, :] = (nt(dp, bg_ref[...].astype(BF16)) * rate_ref[rows, :]).astype(BF16)
                io.store(i, 4, 5)
                for role in range(2 * nl):
                    sb[i, role // nl, role % nl] = nt(
                        dp, wg_ref[role * fw : (role + 1) * fw, :]
                    ).astype(BF16)
                cm.rs_across(i).start()

            cm.rs_steps(i)

            @pl.when(i >= 3)
            def _():
                k = i - 3
                rows = cm.rows(k)
                cm.st_wait(k)
                r = rate_ref[rows, 0:1]
                inner = cm.st_sum(k)[:, 0:1]
                mid = mid_ref[rows, :]
                dm = (
                    cot_ref[rows, :].astype(F32)
                    + r * cm.rs_total(k)
                    - mid * (r * r * inner / d)
                )
                dm_ref[rows, :] = dm
                go_ref[rows, :] = (dm * so_ref[0:1, :]).astype(BF16)
                io.store(k, 0, 1)
                gmo_ref[0:1, :] += jnp.sum(
                    dm * (mid - x_ref[rows, :].astype(F32)), axis=0, keepdims=True
                )

            return carry_on

        lax.fori_loop(0, nc + 3, body, 0)

        def drain(i, carry_on):
            cm.ag_drain(i)
            cm.rs_drain(i)
            cm.st_drain(i)
            stored(i).wait()
            saved(i).wait()
            io.stored(i)
            return carry_on

        lax.fori_loop(0, nc, drain, 0)

    return call(
        kernel,
        "ffn_backward",
        (
            shape((t, fw), F32),
            shape((t, fw), BF16),
            shape((8, fw), F32),
            shape((8, 2 * npad), F32),
            shape((t, LANES), BF16),
            shape((t, LANES), BF16),
            shape((t, 2 * npad), BF16),
            shape((t, d), BF16),
        ),
        [VM, ANY] + [VM] * 10,
        (VM,) * 6 + (ANY, ANY),
        ag_scratch(nl, nc, t, d)
        + rs_scratch(nl, nc, tc, fw)
        + st_scratch(nl, nc, t)
        + [
            pltpu.VMEM((8, t), F32),
            pltpu.VMEM((t, 2 * npad), BF16),
            pltpu.SemaphoreType.DMA((nc,)),
            pltpu.SemaphoreType.DMA((nc,)),
            pltpu.SemaphoreType.DMA((nc,)),
        ],
        4,
        120,
        (gp, gu, w_gu, sc_gu, b_gu, w_down, b_down, rate, cotangent, middle, x, sc_out),
        late=(2, 4, 5, 6, 7, 8, 9, 10),
        flow=(0, 1, 4, 5),
        step=tc,
    )


def gain_rows(tail, at):
    lane = lax.broadcasted_iota(jnp.int32, (8, LANES), 1)
    pick = jnp.where((lane == at) | (lane == at + 1), 1.0, 0.0).astype(BF16)
    column = tail[:, at : at + 1].astype(F32) + tail[:, at + 1 : at + 2].astype(F32)
    return nt(pick, tail)[0:1, :], column


class Stream:
    def __init__(self, sources, slots, sems, step):
        self.sources, self.slots, self.sems, self.step = sources, slots, sems, step

    def copies(self, i):
        rows = pl.ds(pl.multiple_of(i * self.step, self.step), self.step)
        slot = lax.rem(i, 2)
        return [
            pltpu.make_async_copy(src.at[rows, columns], held.at[slot], self.sems.at[k, slot])
            for k, ((src, columns), held) in enumerate(zip(self.sources, self.slots))
        ]

    def start(self, i):
        for copy in self.copies(i):
            copy.start()

    def wait(self, i):
        for copy in self.copies(i):
            copy.wait()
        return [held[lax.rem(i, 2)] for held in self.slots]


def stream_scratch(step, widths):
    return [pltpu.VMEM((2, step, n), BF16) for n in widths] + [pltpu.SemaphoreType.DMA((len(widths), 2))]


def out_backward(
    cfg, npad, nf, go, weights, b_out, ratios, w_gu, w_down, up_gu, b_down, gm_gu, square_gu, m_gu,
    u_full, lg_gu, gu, dp_gu, hidden, lg_down, lora_down, gp_full,
):
    t, fw, d, nl, nc, tc = cfg
    off = nf - (npad - LANES)
    widths = (d, LANES, LANES, LANES, 2 * npad, npad, LANES, LANES, d)

    def kernel(
        io, go_ref, w_ref, b_ref, q_ref, wg_ref, wd_ref, up_ref, bd_ref, gm_ref, sq_ref, m_ref,
        uf_hbm, lg_hbm, gu_hbm, dp_hbm, hid_hbm, ld_hbm, lo2_hbm, gp_hbm,
        da_ref, lo_ref, qs_ref, sh_ref, lc_ref, gf_ref,
        full, own, sd, rd, sc, rc, keep, qss, qsr, acc_a, acc_g, acc_u, acc_d, acc_p, *streams,
    ):
        cm = Comm(nl, nc, tc, fw)
        cm.ag_refs(go_ref, full, own, sd, rd, sc, rc)
        every = lambda n: pl.ds(0, n)
        stream = Stream(
            [
                (uf_hbm, every(d)),
                (lg_hbm, every(LANES)),
                (gu_hbm, pl.ds(npad - LANES, LANES)),
                (gu_hbm, pl.ds(2 * npad - LANES, LANES)),
                (dp_hbm, every(2 * npad)),
                (hid_hbm, every(npad)),
                (ld_hbm, every(LANES)),
                (lo2_hbm, every(LANES)),
                (gp_hbm, every(d)),
            ],
            streams[:-1],
            streams[-1],
            tc,
        )
        stream.start(jnp.int32(0))
        cm.barrier()

        def ratio_copy(o, m):
            k = o * nl + m
            return cm.copy(
                q_ref, qs_ref.at[:, cm.columns(cm.c, cm.g)], qss.at[k], qsr.at[k], 1 - cm.c if o else cm.c, cm.after(m)
            )

        cm.ag_start()
        for o, m in cm.st_peers():
            ratio_copy(o, m).start()
        qs_ref[:, cm.columns(cm.c, cm.g)] = q_ref[...]
        for acc in (acc_a, acc_g, acc_u, acc_d, acc_p):
            acc[...] = jnp.zeros_like(acc)
        cm.ag_ahead()
        io.ready()

        def stored(i):
            rows = cm.rows(i)
            return pltpu.make_async_copy(full.at[rows], gf_ref.at[rows], keep.at[i])

        def body(i, carry_on):
            cm.ag_step(i + 2)

            @pl.when(i + 1 < nc)
            def _():
                stream.start(i + 1)

            u, lg, low_g, low_u, dp, hid, ld, low_d, gp = stream.wait(i)
            acc_a[...] += tn(lg, u)
            acc_g[...] += tn(low_g, dp[:, :npad])
            acc_u[...] += tn(low_u, dp[:, npad:])
            acc_d[...] += tn(ld, hid)
            acc_p[...] += tn(low_d, gp)
            cm.ag_wait(i)
            stored(i).start()
            rows = cm.rows(i)
            block = full[rows, :]
            da_ref[rows, :] = nt(block, w_ref[:, :d]).astype(BF16)
            lo_ref[rows, :] = nt(block, b_ref[...]).astype(BF16)
            return carry_on

        lax.fori_loop(0, nc, body, 0)

        ratio = -gm_ref[0:1, :] / sq_ref[0:1, :]
        term = nt((up_ref[...] * ratio).astype(BF16), wg_ref[...])
        tail_g, tail_u = wg_ref[:, npad - LANES : npad], wg_ref[:, 2 * npad - LANES :]
        gain_row, gain_column = gain_rows(tail_g, off + RANK)
        inverse = 1.0 / (gain_column * gain_column)
        sh_ref[: 2 * RANK, :] = (
            SCALE * (acc_a[: 2 * RANK, :] * gain_row + term[: 2 * RANK, :] / gain_row)
        ).astype(BF16)
        for k, (acc, tail) in enumerate(((acc_g, tail_g), (acc_u, tail_u))):
            at = slice(k * npad, (k + 1) * npad)
            merged = tn((tail.astype(F32) * inverse).astype(BF16), wg_ref[:, at])
            lc_ref[(1 + k) * RANK : (2 + k) * RANK, :] = (
                SCALE * (acc[off : off + RANK, :] + merged[off : off + RANK, :] * ratio[:, at])
            ).astype(BF16)
            lc_ref[3 * RANK + k : 3 * RANK + k + 1, :] = (gm_ref[0:1, at] / m_ref[0:1, at]).astype(BF16)
        lc_ref[3 * RANK + 2 :, :] = jnp.zeros((RANK - 2, npad), BF16)

        for o, m in cm.st_peers():
            ratio_copy(o, m).wait_recv()
        ratio_down = qs_ref[1:2, :]
        lc_ref[:RANK, :] = (
            SCALE
            * (acc_d[:RANK, :] + nt((bd_ref[...].astype(F32) * ratio_down).astype(BF16), wd_ref[:, :d])[:RANK, :])
        ).astype(BF16)
        sh_ref[2 * RANK :, :] = (
            SCALE * (acc_p[:RANK, :] + tn(wd_ref[:, d:], wd_ref[:, :d])[:RANK, :] * ratio_down)
        ).astype(BF16)

        def drain(i, carry_on):
            cm.ag_drain(i)
            stored(i).wait()
            return carry_on

        lax.fori_loop(0, nc, drain, 0)
        for o, m in cm.st_peers():
            ratio_copy(o, m).wait_send()

    dma = pltpu.SemaphoreType.DMA
    return call(
        kernel,
        "out_backward",
        (
            shape((t, fw), BF16),
            shape((t, LANES), BF16),
            shape((8, d), F32),
            shape((3 * RANK, d), BF16),
            shape((4 * RANK, npad), BF16),
            shape((t, d), BF16),
        ),
        [VM] * 11 + [ANY] * 8,
        (VM,) * 5 + (ANY,),
        ag_scratch(nl, nc, t, d)
        + [dma((nc,)), dma((2 * nl,)), dma((2 * nl,))]
        + [pltpu.VMEM((LANES, n), F32) for n in (d, npad, npad, npad, d)]
        + stream_scratch(tc, widths),
        5,
        60,
        (
            go, weights, b_out, ratios, w_gu, w_down, up_gu, b_down, gm_gu, square_gu, m_gu,
            u_full, lg_gu, gu, dp_gu, hidden, lg_down, lora_down, gp_full,
        ),
        late=(1, 2, 4, 5, 6, 7),
    )


def attention_backward(
    cfg, qkv, attended, grad, lse, seg_column, seg_row, first_block, block, cosine, sine, scale, rate, b_qkv
):
    t, fw = cfg[0], cfg[1]
    heads = fw // HD
    width = 3 * fw

    def kernel(
        io, qkv_ref, att_ref, grad_ref, lse_ref, sc_ref, sr_ref, first_ref, cos_ref, sin_ref, scale_ref, rate_ref, b_ref,
        dp_ref, st_ref, gm_ref, lg_ref, dq, dk, dv,
    ):
        def at(i):
            return pl.ds(pl.multiple_of(i * block, block), block)

        def columns(k, hd):
            return slice(k * fw + hd * HD, k * fw + (hd + 1) * HD)

        gm_ref[...] = jnp.zeros_like(gm_ref)
        dk[...] = jnp.zeros_like(dk)
        dv[...] = jnp.zeros_like(dv)

        def one_query(i, carry_on):
            queries = [qkv_ref[at(i), columns(0, hd)] for hd in range(heads)]
            grads = [grad_ref[at(i), columns(0, hd)] for hd in range(heads)]
            deltas = [
                ones_rows(grads[hd].astype(F32) * att_ref[at(i), columns(0, hd)].astype(F32))[0:1, :]
                for hd in range(heads)
            ]
            query_segment = sr_ref[0:1, at(i)]

            def one_key(j, accs):
                allowed = allowed_of(sc_ref[at(j), 0:1], query_segment, j, i, block)
                out = []
                for hd in range(heads):
                    keys = qkv_ref[at(j), columns(1, hd)]
                    s = nt(keys, queries[hd]) * (HD**-0.5)
                    p = jnp.where(allowed, jnp.exp(s - lse_ref[hd * 8 : hd * 8 + 1, at(i)]), 0.0)
                    ds = (p * (nt(qkv_ref[at(j), columns(2, hd)], grads[hd]) - deltas[hd])).astype(BF16)
                    dv[hd, at(j), :] += nn(p.astype(BF16), grads[hd])
                    dk[hd, at(j), :] += nn(ds, queries[hd])
                    out.append(accs[hd] + tn(ds, keys))
                return tuple(out)

            accs = lax.fori_loop(first_ref[i], i + 1, one_key, (jnp.zeros((block, HD), F32),) * heads)
            for hd in range(heads):
                dq[hd, at(i), :] = accs[hd]
            return carry_on

        lax.fori_loop(0, t // block, one_query, 0)

        def finish(i, carry_on):
            rows = at(i)
            cosine_here, sine_here = cos_ref[rows, :], sin_ref[rows, :]
            inner = jnp.zeros((block, HD), F32)
            for hd in range(heads):
                for n, source in enumerate((dq, dk, dv)):
                    where = columns(n, hd)
                    dout = source[hd, rows, :]
                    value = qkv_ref[rows, where].astype(F32)
                    if n < 2:
                        dout = dout * (HD**-0.5)
                        dout = dout * cosine_here - pltpu.roll(dout, HD // 2, 1) * sine_here
                        value = value * cosine_here - pltpu.roll(value, HD // 2, 1) * sine_here
                    product = dout * value
                    inner = inner + product
                    gm_ref[0:1, where] += row_sum(product)
                    dp_ref[rows, where] = (dout * scale_ref[0:1, where]).astype(BF16)
            st_ref[:, rows] = ones_rows(inner)
            lg_ref[rows, :] = (nt(dp_ref[rows, :], b_ref[...].astype(BF16)) * rate_ref[rows, :]).astype(BF16)
            return carry_on

        lax.fori_loop(0, t // block, finish, 0)

    return call(
        kernel,
        "attention_backward",
        (
            shape((t, width), BF16),
            shape((8, t), F32),
            shape((8, width), F32),
            shape((t, LANES), BF16),
        ),
        [VM] * 6 + [SM] + [VM] * 5,
        (VM,) * 4,
        [pltpu.VMEM((heads, t, HD), F32)] * 3,
        None,
        35,
        (qkv, attended, grad, lse, seg_column, seg_row, first_block, cosine, sine, scale, rate, b_qkv),
    )


def qkv_backward(
    cfg, ny, dp, stats, weights, rate, dm, x, shared, local_gu, w_out, up_qkv, b_out, ratios, gm_qkv, square_qkv,
    gm_out, gm_down, small, x_full, lg_qkv, lora_qkv, attended, lg_out, lora_out, go_full,
):
    t, fw, d, nl, nc, tc = cfg
    width = 3 * fw
    peers = 2 * nl
    step = 2 * tc if nc % 2 == 0 else tc
    parts = t // step
    widths = (d, LANES, LANES, fw, LANES, LANES, d)

    def kernel(
        io, dp_ref, st_ref, w_ref, rate_ref, dm_ref, x_ref, sh_ref, l_ref, wo_ref, up_ref, bo_ref, q_ref,
        gm_ref, sq_ref, gmo_ref, gmd_ref, m_ref, xf_hbm, lg_hbm, lq_hbm, at_hbm, lgo_hbm, lo_hbm, gf_hbm,
        out_ref, as_ref, bs_ref, ls_ref,
        sb, cb, gb, s1, r1, s2, r2, sa, ss, sr,
        stage, gs_s, gs_r, gs_l, group, gsum, gss, gsr, final_a, final_b, final_l, fs, fr, fl,
        a_ref, b_ref, acc_a, acc_b, acc_o, acc_p, *streams,
    ):
        cm = Comm(nl, nc, tc, fw, back_by_two=0.375)
        c, g = cm.c, cm.g
        y, h = lax.axis_index("y"), lax.axis_index("h")
        cm.rs_refs(sb, cb, gb, s1, r1, s2, r2)
        cm.st_refs(st_ref, sa, ss, sr)
        swap = Swap(cm)
        every = lambda n: pl.ds(0, n)
        stream = Stream(
            [
                (xf_hbm, every(d)),
                (lg_hbm, every(LANES)),
                (lq_hbm, every(LANES)),
                (at_hbm, every(fw)),
                (lgo_hbm, every(LANES)),
                (lo_hbm, every(LANES)),
                (gf_hbm, every(d)),
            ],
            streams[:-1],
            streams[-1],
            step,
        )
        stream.start(jnp.int32(0))
        senders = [
            {"y": lax.rem(y + ny - k, ny), "c": h, "h": hh} for k in range(1, ny) for hh in (0, 1)
        ]
        cm.barrier(senders + [{"c": h, "h": 1 - h}], [swap.partner, {"c": h, "h": h}])

        def gather_part(o, m):
            to_c, to_g = 1 - c if o else c, cm.after(m)
            k = o * nl + m
            return cm.copy(
                a_ref.at[:, cm.columns(to_c, to_g)], group.at[k], gss.at[k], gsr.at[k], to_c, to_g
            )

        def sums(k, e):
            device = {"y": lax.rem(y + k, ny), "c": lax.rem(c + e, 2), "h": c}
            slot = k * 2 + h
            return [
                pltpu.make_async_remote_copy(
                    src_ref=src, dst_ref=dst.at[slot], send_sem=fs.at[n, k * 2 + e], recv_sem=fr.at[n, slot],
                    device_id=device, device_id_type=MESH,
                )
                for n, (src, dst) in enumerate(((gsum, final_a), (b_ref, final_b), (l_ref, final_l)))
            ]

        def sums_here():
            return [
                pltpu.make_async_copy(src, dst.at[h], fl.at[n])
                for n, (src, dst) in enumerate(((gsum, final_a), (b_ref, final_b), (l_ref, final_l)))
            ]

        def stats_out(i, carry_on):
            cm.st_send(i)
            return carry_on

        lax.fori_loop(0, nc, stats_out, 0)
        for acc in (acc_a, acc_b, acc_o, acc_p):
            acc[...] = jnp.zeros_like(acc)

        def adapters(k):
            @pl.when(k + 1 < parts)
            def _():
                stream.start(k + 1)

            xf, lg, low_q, att, lg_o, low_o, gf = stream.wait(k)
            rows = pl.ds(pl.multiple_of(k * step, step), step)
            acc_a[...] += tn(lg, xf)
            acc_b[...] += tn(low_q, dp_ref[rows, :])
            acc_o[...] += tn(lg_o, att)
            acc_p[...] += tn(low_o, gf)

        def adapters_end():
            ratio = -gm_ref[0:1, :] / sq_ref[0:1, :]
            ratio_out = q_ref[0:1, :]
            tail = w_ref[:, width:]
            gain_row, gain_column = gain_rows(tail, 3 * RANK)
            term = nt((up_ref[...] * ratio).astype(BF16), w_ref[:, :width])
            a_ref[: 3 * RANK, :] = (
                SCALE * (acc_a[: 3 * RANK, :] * gain_row + term[: 3 * RANK, :] / gain_row)
            ).astype(BF16)
            merged = tn(
                (tail.astype(F32) / (gain_column * gain_column)).astype(BF16), w_ref[:, :width]
            )
            for k in range(3):
                at, low = slice(k * fw, (k + 1) * fw), slice(k * RANK, (k + 1) * RANK)
                b_ref[(1 + k) * RANK : (2 + k) * RANK, :] = (
                    SCALE * (acc_b[low, at] + merged[low, at] * ratio[:, at])
                ).astype(BF16)
                b_ref[4 * RANK + k : 4 * RANK + k + 1, :] = (gm_ref[0:1, at] / m_ref[k : k + 1, :]).astype(BF16)
            b_ref[4 * RANK + 3 : 4 * RANK + 4, :] = (gmo_ref[0:1, :] / m_ref[3:4, :]).astype(BF16)
            b_ref[4 * RANK + 4 : 4 * RANK + 5, :] = (gmd_ref[0:1, :] / m_ref[4:5, :]).astype(BF16)
            b_ref[4 * RANK + 5 :, :] = jnp.zeros((RANK - 5, fw), BF16)
            b_ref[:RANK, :] = (
                SCALE
                * (acc_o[:RANK, :] + nt((bo_ref[...].astype(F32) * ratio_out).astype(BF16), wo_ref[:, :d])[:RANK, :])
            ).astype(BF16)
            a_ref[3 * RANK : 4 * RANK, :] = (
                SCALE * (acc_p[:RANK, :] + tn(wo_ref[:, d:], wo_ref[:, :d])[:RANK, :] * ratio_out)
            ).astype(BF16)
            a_ref[4 * RANK :, :] = sh_ref[...]
            for o, m in cm.st_peers():
                gather_part(o, m).start()

        io.ready()

        def grad_swap(i):
            rows = cm.rows(i)
            return stage.at[rows], out_ref.at[rows], (gs_s.at[i], gs_r.at[i], gs_l.at[i])

        def body(i, carry_on):
            @pl.when(i < nc)
            def _():
                block = dp_ref[cm.rows(i), :]
                for role in range(2 * nl):
                    sb[i, role // nl, role % nl] = nt(
                        block, w_ref[role * fw : (role + 1) * fw, :width]
                    ).astype(BF16)
                cm.rs_across(i).start()

            cm.rs_steps(i)

            @pl.when(i < parts)
            def _():
                adapters(i)

            @pl.when(i == parts)
            def _():
                adapters_end()

            @pl.when(i == min(parts + 3, nc + 2))
            def _():
                total = a_ref[:, cm.columns(c, g)].astype(F32)
                for o, m in cm.st_peers():
                    gather_part(o, m).wait_recv()
                    total = total + group[o * nl + m].astype(F32)
                gsum[...] = total.astype(BF16)
                for k in range(ny):
                    for e in (0, 1):
                        if (k, e) == (0, 0):

                            @pl.when(swap.moves)
                            def _():
                                for copy in sums(0, 0):
                                    copy.start()

                            @pl.when(jnp.logical_not(swap.moves))
                            def _():
                                for copy in sums_here():
                                    copy.start()
                        else:
                            for copy in sums(k, e):
                                copy.start()

            @pl.when(i >= 3)
            def _():
                k = i - 3
                rows = cm.rows(k)
                cm.st_wait(k)
                r = rate_ref[rows, 0:1]
                inner = cm.st_sum(k)[:, 0:1]
                stage[rows, :] = (
                    dm_ref[rows, :]
                    + r * cm.rs_total(k)
                    - x_ref[rows, :].astype(F32) * (r * r * inner / d)
                ).astype(BF16)
                swap.start(*grad_swap(k))

            return carry_on

        lax.fori_loop(0, nc + 3, body, 0)

        for k in range(ny):
            for hh in (0, 1):
                slot = k * 2 + hh

                def arrived():
                    for n, dst in enumerate((final_a, final_b, final_l)):
                        src = (gsum, b_ref, l_ref)[n]
                        pltpu.make_async_remote_copy(
                            src_ref=src, dst_ref=dst.at[slot], send_sem=fs.at[n, 0], recv_sem=fr.at[n, slot],
                            device_id=swap.partner, device_id_type=MESH,
                        ).wait_recv()

                if k == 0:
                    here = jnp.logical_and(c == h, h == hh)

                    @pl.when(here)
                    def _():
                        for copy in sums_here():
                            copy.wait()

                    @pl.when(jnp.logical_not(here))
                    def _():
                        arrived()
                else:
                    arrived()
        for out, held in ((as_ref, final_a), (bs_ref, final_b), (ls_ref, final_l)):
            total = held[0].astype(F32)
            for slot in range(1, 2 * ny):
                total = total + held[slot].astype(F32)
            out[...] = total

        def drain(i, carry_on):
            swap.wait(*grad_swap(i))
            cm.rs_drain(i)
            cm.st_drain(i)
            swap.drain(*grad_swap(i))
            return carry_on

        lax.fori_loop(0, nc, drain, 0)
        for o, m in cm.st_peers():
            gather_part(o, m).wait_send()
        for k in range(ny):
            for e in (0, 1):
                if (k, e) == (0, 0):

                    @pl.when(swap.moves)
                    def _():
                        for copy in sums(0, 0):
                            copy.wait_send()
                else:
                    for copy in sums(k, e):
                        copy.wait_send()

    dma = pltpu.SemaphoreType.DMA
    na, nb, ng = 7 * RANK, (5 * RANK, fw), local_gu.shape
    return call(
        kernel,
        "qkv_backward",
        (shape((t, fw), BF16), shape((na, fw), F32), shape(nb, F32), shape(ng, F32)),
        [VM] * 17 + [ANY] * 7,
        (VM,) * 4,
        rs_scratch(nl, nc, tc, fw)
        + st_scratch(nl, nc, t)
        + [pltpu.VMEM((t, fw), BF16)]
        + [dma((nc,))] * 3
        + [pltpu.VMEM((peers, na, fw), BF16), pltpu.VMEM((na, fw), BF16), dma((peers,)), dma((peers,))]
        + [
            pltpu.VMEM((2 * ny, na, fw), BF16),
            pltpu.VMEM((2 * ny, *nb), BF16),
            pltpu.VMEM((2 * ny, *ng), BF16),
            dma((3, 2 * ny)),
            dma((3, 2 * ny)),
            dma((3,)),
            pltpu.VMEM((na, d), BF16),
            pltpu.VMEM(nb, BF16),
        ]
        + [pltpu.VMEM((LANES, n), F32) for n in (d, width, fw, d)]
        + stream_scratch(step, widths),
        6,
        70,
        (
            dp, stats, weights, rate, dm, x, shared, local_gu, w_out, up_qkv, b_out, ratios, gm_qkv, square_qkv,
            gm_out, gm_down, small, x_full, lg_qkv, lora_qkv, attended, lg_out, lora_out, go_full,
        ),
        late=(2, 3, 4, 5, 6, 7, 8, 9, 10, 11),
    )


def last_step(fw, nf, grad, result, shared, local, local_gu):
    def kernel(
        io, g_ref, r_ref, s_ref, l_ref, u_ref,
        result_ref, grad_ref, aq_ref, bq_ref, mq_ref, ao_ref, bo_ref, mo_ref,
        ag_ref, bg_ref, mg_ref, ad_ref, bd_ref, md_ref,
    ):
        result_ref[...] = r_ref[...]
        grad_ref[...] = g_ref[...].astype(F32)
        for k in range(3):
            aq_ref[k] = s_ref[k * RANK : (k + 1) * RANK, :]
            bq_ref[k] = l_ref[(1 + k) * RANK : (2 + k) * RANK, :]
        for k in range(2):
            ag_ref[k] = s_ref[(4 + k) * RANK : (5 + k) * RANK, :]
            bg_ref[k] = u_ref[(1 + k) * RANK : (2 + k) * RANK, :nf]
        mq_ref[...] = l_ref[4 * RANK : 4 * RANK + 3, :]
        mg_ref[...] = u_ref[3 * RANK : 3 * RANK + 2, :nf]
        ao_ref[...] = l_ref[:RANK, :]
        bo_ref[...] = s_ref[3 * RANK : 4 * RANK, :]
        mo_ref[...] = l_ref[4 * RANK + 3 : 4 * RANK + 4, :]
        ad_ref[...] = u_ref[:RANK, :nf]
        bd_ref[...] = s_ref[6 * RANK :, :]
        md_ref[...] = l_ref[4 * RANK + 4 : 4 * RANK + 5, :]

    f = [
        (3, RANK, fw), (3, RANK, fw), (3, fw), (RANK, fw), (RANK, fw), (1, fw),
        (2, RANK, fw), (2, RANK, nf), (2, nf), (RANK, nf), (RANK, fw), (1, fw),
    ]
    return call(
        kernel,
        "last_step",
        (shape(result.shape, BF16), shape(grad.shape, F32), *[shape(v, F32) for v in f]),
        [VM] * 5,
        (VM,) * 14,
        [],
        None,
        4,
        (grad, result, shared, local, local_gu),
    )


def positions_of(segment_row):
    index = jnp.arange(segment_row.shape[0], dtype=jnp.int32)
    starts = jnp.concatenate([jnp.ones((1,), jnp.bool_), segment_row[1:] != segment_row[:-1]])
    begin = lax.cummax(jnp.where(starts, index, 0), axis=0)
    return index - begin, begin


def padded(rows, total):
    return jnp.pad(rows, ((0, 0), (0, total - rows.shape[1])))


def on_device(ny, nl, *operands):
    (
        inputs, segments, gain_attn, gain_ffn, w_qkv, a_qkv, b_qkv, m_qkv, w_out, a_out, b_out, m_out,
        w_gu, a_gu, b_gu, m_gu, w_down, a_down, b_down, m_down, cotangent,
    ) = operands
    t, fw = inputs.shape
    mp = 2 * nl
    d = mp * fw
    nf = m_gu.shape[1]
    npad = -(-(nf + RANK) // LANES) * LANES
    width = 3 * fw
    nc = 8 if t % 1024 == 0 else 1
    cfg = (t, fw, d, nl, nc, t // nc)
    block = min(256, t)
    y, c, h, g = (lax.axis_index(name) for name in ("y", "c", "h", "g"))
    role = c * nl + g

    def merged_of(frozen, down, up):
        return frozen.astype(F32) + SCALE * jnp.einsum(
            "kdr,krn->kdn", down, up, precision=HIGHEST
        )

    def two_parts(gain):
        high = gain.astype(BF16)
        return [high[:, None], (gain - high.astype(F32)).astype(BF16)[:, None]]

    tail_qkv = padded(
        jnp.concatenate(
            [(a_qkv[k] * gain_attn[:, None]).astype(BF16) for k in range(3)] + two_parts(gain_attn), axis=1
        ),
        LANES,
    )
    tail_gu = jnp.stack(
        [
            jnp.pad(
                jnp.concatenate(
                    [(a_gu[k] * gain_ffn[:, None]).astype(BF16)] + two_parts(gain_ffn), axis=1
                ),
                ((0, 0), (nf, npad - nf - RANK - 2)),
            )
            for k in range(2)
        ]
    )
    gains = padded(jnp.stack([gain_attn, gain_ffn], axis=1), LANES)
    b_gu_padded = jnp.pad(
        b_gu.reshape(2, RANK, mp, nf), ((0, 0), (0, 0), (0, 0), (0, npad - nf))
    ).transpose(0, 2, 1, 3)
    rows_out = jnp.concatenate(
        [
            merged_of(w_out[None], a_out[None], b_out[None])[0].astype(BF16),
            padded(a_out, LANES).astype(BF16),
        ],
        axis=1,
    )
    small = jnp.concatenate([m_qkv, m_out[None], m_down[None], jnp.zeros((3, fw), F32)], axis=0)
    small_gu = jnp.broadcast_to(
        jnp.pad(m_gu, ((0, 0), (0, npad - nf)), constant_values=1.0).reshape(1, 2 * npad), (8, 2 * npad)
    )

    def take(whole, n, axis):
        return lax.dynamic_slice_in_dim(whole, role * n, n, axis)

    b_qkv_here = take(b_qkv, fw, 2)
    b_gu_here = take(b_gu, nf, 2)

    def block_up(up, pad):
        k, _, n = up.shape
        wide = jnp.pad(up, ((0, 0), (0, 0), (0, pad - n)))[:, :, None, :]
        same = (jnp.arange(k)[:, None] == jnp.arange(k)[None, :])[:, None, :, None]
        rows = jnp.where(same, wide, 0.0).reshape(k * RANK, k * pad)
        return jnp.pad(rows, ((0, LANES - k * RANK), (0, 0)))

    up_qkv = block_up(b_qkv_here, fw)
    up_gu = block_up(b_gu_here, npad)
    up_out = jnp.pad(b_out, ((0, LANES - RANK), (0, 0))).astype(BF16)
    up_down = jnp.pad(b_down, ((0, LANES - RANK), (0, 0))).astype(BF16)

    segment = lax.dynamic_index_in_dim(
        lax.all_gather(segments, "c", axis=0, tiled=True), h, 0, keepdims=False
    )
    positions, begin = positions_of(segment)
    first_block = begin[::block] // block
    seg_row = jnp.broadcast_to(segment[None, :], (8, t))
    seg_column = jnp.broadcast_to(segment[:, None], (t, LANES))
    frequencies = jnp.exp(jnp.arange(HD // 2, dtype=F32) * (-2.0 * math.log(10000.0) / HD))
    angles = positions.astype(F32)[:, None] * frequencies[None, :]
    cosine = jnp.cos(angles)
    sine = jnp.sin(angles)
    cosine = jnp.concatenate([cosine, cosine], axis=1)
    sine = jnp.concatenate([-sine, sine], axis=1)

    (
        x, weights_qkv, weights_out, small, small_gu, scale_qkv, square_qkv, qkv, lora_qkv_in, rate_attn,
        blocks_gu, x_full,
    ) = qkv_forward(
        cfg, ny, npad, nf, inputs, w_qkv, a_qkv, b_qkv, tail_qkv, gains, rows_out, small, small_gu, cosine, sine,
        w_gu, a_gu, b_gu_padded, tail_gu,
    )
    attended, lse = attention_forward(cfg, qkv, seg_column, seg_row, first_block, block)
    middle, u, stats, sc_out, square_out, lora_out, weights_gu, weights_down = out_forward(
        cfg, ny, npad, attended, weights_out, x, small, blocks_gu, w_down, a_down, b_down
    )
    (
        gu, hidden, block_out, gm_down, rate_ffn, gp, scale_gu, square_gu, sc_down, square_down,
        lora_down, grad_seed, u_full,
    ) = ffn_forward(
        cfg, npad, nf, u, stats, weights_gu, small_gu[0:1], weights_down, small, middle, cotangent
    )

    dm, go, gm_out, gm_gu, lg_gu, lg_down, dp_gu, gp_full = ffn_backward(
        cfg, npad, gp, gu, weights_gu, scale_gu, up_gu, weights_down, up_down, rate_ffn,
        grad_seed, middle, x, sc_out,
    )
    ratios = jnp.concatenate(
        [-gm_out[0:1] / square_out[0:1], -gm_down[0:1] / square_down[0:1], jnp.zeros((6, fw), F32)], axis=0
    )
    grad_attended, lg_out, ratios, shared, local_gu, go_full = out_backward(
        cfg, npad, nf, go, weights_out, up_out, ratios, weights_gu, weights_down, up_gu, up_down, gm_gu, square_gu,
        small_gu, u_full, lg_gu, gu, dp_gu, hidden, lg_down, lora_down, gp_full,
    )
    dp_qkv, inner, gm_qkv, lg_qkv = attention_backward(
        cfg, qkv, attended, grad_attended, lse, seg_column, seg_row, first_block, block, cosine, sine,
        scale_qkv, rate_attn, up_qkv,
    )

    grad_input, shared, local, local_gu = qkv_backward(
        cfg, ny, dp_qkv, inner, weights_qkv, rate_attn, dm, x, shared, local_gu, weights_out, up_qkv, up_out, ratios,
        gm_qkv, square_qkv, gm_out, gm_down, small, x_full, lg_qkv, lora_qkv_in, attended, lg_out, lora_out, go_full,
    )
    out = list(last_step(fw, nf, grad_input, block_out, shared, local, local_gu))
    out[2], out[8] = out[2].transpose(0, 2, 1), out[8].transpose(0, 2, 1)
    out[5], out[11] = out[5].T, out[11].T
    out[7], out[13] = out[7][0], out[13][0]
    return tuple(out)


def solution(mesh):
    dp, mp = mesh.shape["dp"], mesh.shape["mp"]
    ny, nl = dp // 2, mp // 2
    fine = Mesh(mesh.devices.reshape(ny, 2, 2, nl), ("y", "c", "h", "g"))
    rows, cols = ("y", "c"), ("h", "g")
    in_specs = (
        P(rows, cols),
        P(rows, None),
        P(cols),
        P(cols),
        P(None, cols, None),
        P(None, cols, None),
        P(),
        P(None, cols),
        P(cols, None),
        P(cols, None),
        P(),
        P(cols),
        P(None, cols, None),
        P(None, cols, None),
        P(),
        P(None, cols),
        P(cols, None),
        P(cols, None),
        P(),
        P(cols),
        P(rows, cols),
    )
    out_specs = (
        P(rows, cols),
        P(rows, cols),
        P(None, cols, None),
        P(None, None, cols),
        P(None, cols),
        P(cols, None),
        P(None, cols),
        P(cols),
        P(None, cols, None),
        P(None, None, cols),
        P(None, cols),
        P(cols, None),
        P(None, cols),
        P(cols),
    )
    return jax.shard_map(
        lambda *operands: on_device(ny, nl, *operands),
        mesh=fine,
        in_specs=in_specs,
        out_specs=out_specs,
        check_vma=False,
    )
```

time: 3700 us -> 691 us (0.19)
  waiting for transfers between devices: 2160 us -> 0 us
  Pallas kernels: 0 us -> 653 us
  matrix products: 637 us -> 1.93 us
  blocking collectives: 542 us -> 2.03 us
  local copies, waits for them, and re-layouts: 190 us -> 16.1 us
  other arithmetic: 113 us -> 11.9 us
    reduce_scatter x10 -> x0, waiting for transfers between devices: 1650 us -> none  [the longest x4 1090 us: sharded_forward(): lax.psum_scatter(sharded_output, 'mp', scatter_dimension=2, tiled=True)]
    pallas_call x0 -> x9, Pallas kernels: none -> 653 us  [call(): pl.pallas_call(whole, name=name, out_shape=outs, in_specs=in_specs, out_s...]
    dot_general x126 -> x1, matrix products: 596 us -> 1.93 us  [merged_of(): jnp.einsum('kdr,krn->kdn', down, up, precision=HIGHEST)]
    all_gather x6 -> x1, blocking collectives: 449 us -> 2.03 us  [on_device(): lax.all_gather(segments, 'c', axis=0, tiled=True)]
    all_gather x6 -> x0, waiting for transfers between devices: 304 us -> none  [the longest x4 176 us: column_forward(): entire_rows = lax.all_gather(input_portion, 'mp', axis=1, tiled=True)]
    psum x4 -> x0, waiting for transfers between devices: 206 us -> none  [the longest x3 206 us: sharded_forward(): lax.psum(jnp.einsum('ti,kir->tkr', input_portion, adapter_down_factor, pr...]
    psum x4 -> x0, blocking collectives: 92.7 us -> none  [norm_forward(): squares = lax.psum(jnp.sum(residual * residual, axis=1), 'mp')]
    unnamed x254 -> x35, local copies, waits for them, and re-layouts: 62.4 us -> 2.79 us
  transfers between devices with their start and end apart: 24 -> 0, of which waited for: 14 -> 0; matrix products, arithmetic and copies ran while one was open for 18% -> 0% of each run, Pallas kernels for 0% -> 0%
where the time goes in v1:
time: 691 us; the launch traced here: 686 us
  Pallas kernels  653 us (95%)
  local copies, waits for them, and re-layouts  16.1 us (2%)
  other arithmetic  11.9 us (2%)
    pallas_call x9, Pallas kernels, call(): pl.pallas_call(whole, name=name, out_shape=outs, in_specs=in_specs, out_s...  653 us

profile of v1, /device:TPU:1, one launch (start us, length us, event | category | flops | bytes accessed | tf_op | source)
XLA Modules:
  0.0 686.3 jit_solution(12433061925268340891)
XLA Ops:
  0.7 2.0 all-gather
  3.5 3.7 fusion.4
  7.2 1.9 pad_maximum_fusion
  9.7 0.9 pad_maximum_fusion.2.refs_14_
  12.0 1.0 pad_bitcast_fusion.refs_13_
  13.0 1.9 fusion.1
  15.1 1.1 fusion.3.refs_6_
  16.2 0.9 copy.77.refs_2_
  20.2 121.8 %qkv_forward.1 = (bf16[2048,256]{1,0:T(8,128)(2,1)}, bf16[2048,896]{1,0:T(8,128)(2,1)}, bf16[256,2176]{1,0:T(8,128)(2,1)}, f32[8,256]{1,0:T(8,128)}, f32[8,1536]...) custom-call(bf16[2048,256]{1,0:T(8,128)(2,1)} %refs_0_.1, ...), custom_call_target="tpu_custom_call" | custom-call | flops 44999999488 | bytes 270000000 | tf_op jit(solution)/shard_map/qkv_forward/pallas_call | solution.py:682
  142.5 1.3 broadcast_in_dim.123.refs_1_.refs_4_
  144.5 20.1 %attention_forward.1 = (bf16[2048,256]{1,0:T(8,128)(2,1)}, f32[16,2048]{1,0:T(8,128)}) custom-call(bf16[2048,768]{1,0:T(8,128)(2,1)} %get-tuple-element.84.refs_0_, s32[2048,128]{1,0:T(8,128)} %broadcast_in_dim.123.refs_1_.refs_4_, s32[8,2048]{1,0:T(8,128)} %broadcast_in_dim.124.refs_2_.refs_5_, s32[8]{0:T(128)} %and_select_fusion.refs_3_.refs_6_), custom_call_target="tpu_custom_call" | custom-call | flops 7500000256 | bytes 45000000 | tf_op jit(solution)/shard_map/attention_forward/pallas_call | solution.py:682
  164.6 0.9 copy.79.refs_6_
  165.5 139.8 %out_forward.1 = (f32[2048,256]{1,0:T(8,128)}, bf16[2048,256]{1,0:T(8,128)(2,1)}, f32[8,2048]{1,0:T(8,128)}, f32[8,256]{1,0:T(8,128)}, f32[8,256]{1,0:T(8,128)},...) custom-call(bf16[2048,256]{1,0:T(8,128)(2,1)} %get-tuple-element.85.refs_0_.refs_1_.refs_20_, ...), custom_call_target="tpu_custom_call" | custom-call | flops 44999999488 | bytes 270000000 | tf_op jit(solution)/shard_map/out_forward/pallas_call | solution.py:682
  305.3 1.4 slice.58.refs_3_
  306.7 124.6 %ffn_forward.1 = (bf16[2048,1536]{1,0:T(8,128)(2,1)}, bf16[2048,768]{1,0:T(8,128)(2,1)}, bf16[2048,256]{1,0:T(8,128)(2,1)}, f32[8,256]{1,0:T(8,128)}, f32[2048,1...) custom-call(bf16[2048,256]{1,0:T(8,128)(2,1)} %get-tuple-element.90., ...), custom_call_target="tpu_custom_call" | custom-call | flops 54999998464 | bytes 330000000 | tf_op jit(solution)/shard_map/ffn_forward/pallas_call | solution.py:682
  431.3 1.0 constant_dynamic-slice_fusion.1
  432.5 1.0 pad.57.refs_4_.refs_6_
  433.5 0.9 pad.58.refs_6_.refs_7_
  434.4 81.6 %ffn_backward.1 = (f32[2048,256]{1,0:T(8,128)}, bf16[2048,256]{1,0:T(8,128)(2,1)}, f32[8,256]{1,0:T(8,128)}, f32[8,1536]{1,0:T(8,128)}, bf16[2048,128]{1,0:T(8,1...) custom-call(bf16[2048,256]{1,0:T(8,128)(2,1)} %get-tuple-element.96.refs_0_, ...), custom_call_target="tpu_custom_call" | custom-call | flops 60000002048 | bytes 360000000 | tf_op jit(solution)/shard_map/ffn_backward/pallas_call | solution.py:682
  518.3 0.9 pad.59.refs_2_.refs_10_
  519.1 53.1 %out_backward.1 = (bf16[2048,256]{1,0:T(8,128)(2,1)}, bf16[2048,128]{1,0:T(8,128)(2,1)}, f32[8,2048]{1,0:T(8,128)}, bf16[48,2048]{1,0:T(8,128)(2,1)}, bf16[64,76...) custom-call(bf16[2048,256]{1,0:T(8,128)(2,1)} %get-tuple-element.102.refs_0_, ...), custom_call_target="tpu_custom_call" | custom-call | flops 30000001024 | bytes 180000000 | tf_op jit(solution)/shard_map/out_backward/pallas_call | solution.py:682
  574.0 30.7 %attention_backward.1 = (bf16[2048,768]{1,0:T(8,128)(2,1)}, f32[8,2048]{1,0:T(8,128)}, f32[8,768]{1,0:T(8,128)}, bf16[2048,128]{1,0:T(8,128)(2,1)}) custom-call(bf16[2048,768]{1,0:T(8,128)(2,1)} %get-tuple-element.84.refs_0_, bf16[2048,256]{1,0:T(8,128)(2,1)} %get-tuple-element.85.refs_0_.refs_1_.refs_20_, bf16[2048,256]{1,0:T(8,128)(2,1)} %get-tuple-element.116.refs_2_, ...), custom_call_target="tpu_custom_call" | custom-call | flops 17500000256 | bytes 105000000 | tf_op jit(solution)/shard_map/attention_backward/pallas_call | solution.py:682
  604.7 77.5 %qkv_backward.1 = (bf16[2048,256]{1,0:T(8,128)(2,1)}, f32[112,256]{1,0:T(8,128)}, f32[80,256]{1,0:T(8,128)}, f32[64,768]{1,0:T(8,128)}) custom-call(bf16[2048,768]{1,0:T(8,128)(2,1)} %get-tuple-element.120.refs_0_, f32[8,2048]{1,0:T(8,128)} %get-tuple-element.121.refs_1_, bf16[2048,896]{1,0:T(8,128)(2,1)} %get-tuple-element.122.refs_2_, ...), custom_call_target="tpu_custom_call" | custom-call | flops 35000000512 | bytes 210000000 | tf_op jit(solution)/shard_map/qkv_backward/pallas_call | solution.py:682
  682.2 3.6 last_step.1
  (88 shorter events, 11.1 us)
Async XLA Ops:
  7.2 2.0 copy-start.5
  7.2 2.0 copy-start.10
  9.2 1.4 copy-start.4
  9.2 1.4 copy-start.9
  9.2 2.3 copy-start.1
  11.5 1.5 copy-start
  11.5 1.5 copy-start.2
  11.5 1.5 copy-start.7
  14.9 3.9 copy-start.11
  14.9 4.6 copy-start.12
  14.9 4.6 copy-start.13
  14.9 4.6 copy-start.14
  144.5 20.1 %copy-start.8 = (f32[704,16]{0,1:T(8,128)S(1)}, f32[704,16]{0,1:T(8,128)}, u32[]{:S(2)}) copy-start(f32[704,16]{0,1:T(8,128)} %param.38) | copy-start | bytes 135172
  306.7 126.8 %copy-start.6 = (f32[16,2048]{1,0:T(8,128)S(1)}, f32[16,2048]{1,0:T(8,128)}, u32[]{:S(2)}) copy-start(f32[16,2048]{1,0:T(8,128)} %refs_7_.2) | copy-start | bytes 393220
  434.4 83.9 %copy-start.3 = (f32[16,2048]{1,0:T(8,128)S(1)}, f32[16,2048]{1,0:T(8,128)}, u32[]{:S(2)}) copy-start(f32[16,2048]{1,0:T(8,128)} %param.31) | copy-start | bytes 393220

commit v2 on v1

--- a/solution.py
+++ b/solution.py
@@ -40,6 +40,7 @@
 
 
 WINDOW = 3
+EARLY = 1
 
 
 class Comm:
@@ -312,11 +313,12 @@
         self.st, self.sa, self.ss, self.sr = st, sa, ss, sr
 
     def st_copy(self, i, other, m):
-        rows = self.rows(i)
-        place = pl.ds(pl.multiple_of((self.c * self.nl + self.g) * 8, 8), 8)
+        mine = self.c * self.nl + self.g
+        src, dst = (self.st, self.sa.at[mine]) if i is None else (self.st.at[i], self.sa.at[mine, i])
+        i = 0 if i is None else i
         return self.copy(
-            self.st.at[:, rows],
-            self.sa.at[place, rows],
+            src,
+            dst,
             self.ss.at[i, other * self.nl + m],
             self.sr.at[i, other * self.nl + m],
             1 - self.c if other else self.c,
@@ -329,16 +331,21 @@
     def st_send(self, i):
         for o, m in self.st_peers():
             self.st_copy(i, o, m).start()
-        place = pl.ds(pl.multiple_of((self.c * self.nl + self.g) * 8, 8), 8)
-        self.sa[place, self.rows(i)] = self.st[:, self.rows(i)]
+        mine = self.c * self.nl + self.g
+        if i is None:
+            self.sa[mine] = self.st[...]
+        else:
+            self.sa[mine, i] = self.st[i]
 
     def st_wait(self, i):
         for o, m in self.st_peers():
             self.st_copy(i, o, m).wait_recv()
 
     def st_sum(self, i):
-        held = self.sa[:, self.rows(i)]
-        return tn(held, jnp.full((held.shape[0], LANES), 0.125, F32), HIGHEST)
+        total = self.sa[0, i]
+        for role in range(1, 2 * self.nl):
+            total = total + self.sa[role, i]
+        return jnp.broadcast_to(total, (8, self.tc)).T[:, 0:1]
 
     def st_drain(self, i):
         for o, m in self.st_peers():
@@ -522,42 +529,59 @@
             device_id={"y": lax.rem(self.y + k, self.ny)}, device_id_type=MESH,
         )
 
-    def start(self):
-        self.here().start()
-        for m in range(1, self.cm.nl):
-            self.piece(m).start()
-
-    def pass_own(self, m):
+    def start(self, steps):
+        for m in steps:
+            if m == 0:
+                self.here().start()
+            else:
+                self.piece(m).start()
+
+    def own(self, m):
         if m == 0:
             self.here().wait()
         else:
             self.piece(m).wait_recv()
-        if m < 2:
-            self.crossed(m, self.h).start()
+
+    def start_crossing(self, m):
+        self.crossed(m, self.h).start()
+
+    def wait_crossing(self, m):
+        self.crossed(m, 1 - self.h).wait_recv()
+
+    def share(self, side, m):
         for k in range(1, self.ny):
-            self.shared(0, m, k, self.y).start()
-
-    def pass_crossed(self, m):
-        self.crossed(m, 1 - self.h).wait_recv()
-        if m + 2 < self.cm.nl:
-            self.crossed(m + 2, self.h).start()
-        for k in range(1, self.ny):
-            self.shared(1, m, k, self.y).start()
-
-    def wait(self):
-        for side in (0, 1):
-            for m in range(self.cm.nl):
-                for k in range(1, self.ny):
-                    self.shared(side, m, k, lax.rem(self.y + self.ny - k, self.ny)).wait_recv()
-
-    def drain(self):
-        for m in range(self.cm.nl):
-            self.crossed(m, self.h).wait_send()
+            self.shared(side, m, k, self.y).start()
+
+    def pass_own(self, m, cross=True):
+        self.own(m)
+        if cross:
+            self.start_crossing(m)
+        self.share(0, m)
+
+    def pass_crossed(self, m, following=None):
+        self.wait_crossing(m)
+        if following is not None and following < self.cm.nl:
+            self.start_crossing(following)
+        self.share(1, m)
+
+    def wait(self, side, steps):
+        for m in steps:
+            for k in range(1, self.ny):
+                self.shared(side, m, k, lax.rem(self.y + self.ny - k, self.ny)).wait_recv()
+
+    def drain_own(self, steps):
+        for m in steps:
             if m > 0:
                 self.piece(m).wait_send()
-            for side in (0, 1):
-                for k in range(1, self.ny):
-                    self.shared(side, m, k, self.y).wait_send()
+
+    def drain_crossing(self, steps):
+        for m in steps:
+            self.crossed(m, self.h).wait_send()
+
+    def drain_shared(self, side, steps):
+        for m in steps:
+            for k in range(1, self.ny):
+                self.shared(side, m, k, self.y).wait_send()
 
 
 def spread_scratch(ny, nl):
@@ -603,7 +627,7 @@
 
 def st_scratch(nl, nc, t):
     return [
-        pltpu.VMEM((2 * nl * 8, t), F32),
+        pltpu.VMEM((2 * nl, nc, 1, t // nc), F32),
         pltpu.SemaphoreType.DMA((nc, 2 * nl)),
         pltpu.SemaphoreType.DMA((nc, 2 * nl)),
     ]
@@ -647,7 +671,7 @@
             self.copy(k, i).wait()
 
 
-def call(kernel, name, outs, in_specs, out_specs, scratch, collective, us, args, late=(), flow=(), step=1):
+def call(kernel, name, outs, in_specs, out_specs, scratch, collective, us, args, late=(), flow=(), step=1, aliases=None):
     extra = {}
     if collective is not None:
         extra = {"collective_id": collective, "has_side_effects": True}
@@ -686,6 +710,7 @@
         in_specs=in_specs,
         out_specs=out_specs[0] if single else tuple(out_specs),
         scratch_shapes=scratch + more,
+        input_output_aliases=aliases or {},
         compiler_params=pltpu.CompilerParams(vmem_limit_bytes=VMEM_LIMIT, **extra),
         cost_estimate=pl.CostEstimate(
             flops=int(us * 5e8), bytes_accessed=int(us * 3e6), transcendentals=0
@@ -708,27 +733,32 @@
     return jnp.sum(values, axis=0, keepdims=True)
 
 
+def down_part(nf, ny):
+    return -(-(-(-nf // ny)) // (16 * PIECES)) * 16 * PIECES
+
+
 def merged_tile(frozen, down, up):
     return frozen.astype(F32) + SCALE * nn(down, up, HIGHEST)
 
 
 def qkv_forward(
     cfg, ny, npad, nf, x_in, w_qkv, a_qkv, b_qkv, tail_qkv, gains, rows_out, small, small_gu, cosine, sine,
-    w_gu, a_gu, b_gu, tail_gu,
+    w_gu, a_gu, b_gu, tail_gu, w_down, a_down, b_down,
 ):
     t, fw, d, nl, nc, tc = cfg
     width = 3 * fw
     wide = width + LANES
     part = fw // ny
+    down_rows = down_part(nf, ny) * ny
     ff_half = w_gu.shape[2] // 2
 
     def kernel(
         io, x_ref, wq_hbm, aq_ref, bq_ref, tq_ref, gain_ref, eo_ref, m_ref, mg_ref, cos_ref, sin_ref,
-        wg_hbm, ag_ref, bg_ref, tg_ref,
-        xs_ref, w_ref, wo_ref, ms_ref, mgs_ref, sc_ref, sq_ref, qkv_ref, lora_ref, rate_ref, eg_ref, out_ref,
+        wg_hbm, ag_ref, bg_ref, tg_ref, wdown_ref, ad_ref, bd_ref,
+        xs_ref, w_ref, wo_ref, ms_ref, mgs_ref, sc_ref, sq_ref, qkv_ref, lora_ref, rate_ref, eg_ref, ed_ref, wgs_ref, out_ref,
         full, own, sd, rd, sc, rc, keep, xs_s, xs_r, xs_l, small_sems,
         hs, hr, ps, pr, pn, ys, yr, os, orr, ol, oys, oyr,
-        e_ref, wq, wg, wload,
+        e_ref, wq, wg, wload, ghs, ghr, gps, gpr, gpn, gys, gyr,
     ):
         cm = Comm(nl, nc, tc, fw, out_by_one=0.9375)
         cm.ag_refs(xs_ref, full, own, sd, rd, sc, rc)
@@ -743,6 +773,7 @@
         )
         load_q.start()
         load_g.start()
+        later = Spread(cm, ny, eg_ref, wgs_ref, ghs, ghr, gps, gpr, gpn, gys, gyr)
         output = RowMove(swap, ny, fw // ny, eo_ref, wo_ref, os, orr, ol, oys, oyr)
         cm.barrier(movers(ny), [swap.partner])
 
@@ -768,7 +799,7 @@
                 tile = merged_tile(wq[k, :, gg * fw : (gg + 1) * fw], aq_ref[k, mine, :], bq_ref[k, :, columns])
                 e_ref[gg, :, k * fw : (k + 1) * fw] = (tile * gain_attn).astype(BF16)
             e_ref[gg, :, width:] = tq_ref[mine, :]
-        weights.start()
+        weights.start(range(nl))
 
         def gate_up(gg):
             off = gg * nf % LANES
@@ -783,6 +814,16 @@
                     lane < nf, tile, tg_ref[k, mine, :].astype(F32)
                 ).astype(BF16)
 
+        def down_tiles(k):
+            if k == 0:
+                if down_rows > nf:
+                    ed_ref[nf:, :] = jnp.zeros((down_rows - nf, ed_ref.shape[1]), BF16)
+                ed_ref[:nf, d:] = jnp.zeros((nf, LANES), BF16)
+                ed_ref[:nf, d : d + RANK] = ad_ref[...].astype(BF16)
+            for n in (2 * k, 2 * k + 1):
+                at = slice(n * fw, (n + 1) * fw)
+                ed_ref[:nf, at] = merged_tile(wdown_ref[:, at], ad_ref[...], bd_ref[:, at]).astype(BF16)
+
         def gather(i, carry_on):
             swap.wait(*token_swap(i))
 
@@ -803,14 +844,19 @@
         weights.pass_own(1)
         lax.fori_loop(half, nc, gather, 0)
         for m in range(2, nl):
-            weights.pass_own(m)
+            weights.pass_own(m, cross=False)
         load_g.wait()
         io.ready()
         for m in range(nl):
             lax.fori_loop(nc * m // nl, nc * (m + 1) // nl, forward, 0)
             gate_up(m)
-            weights.pass_crossed(m)
+            weights.pass_crossed(m, m + 2)
+            down_tiles(m)
         output.start()
+        later.start(range(EARLY + 1))
+        for m in range(EARLY):
+            later.own(m)
+            later.start_crossing(m)
         cm.ag_step(jnp.int32(nc), more=False)
 
         def stored(i):
@@ -826,7 +872,8 @@
             return carry_on
 
         lax.fori_loop(0, nc, rates, 0)
-        weights.wait()
+        for side in (0, 1):
+            weights.wait(side, range(nl))
         output.pass_on()
 
         def squares(i, total):
@@ -863,6 +910,9 @@
             return carry_on
 
         lax.fori_loop(0, t // big, body, 0)
+        for m in range(EARLY):
+            later.wait_crossing(m)
+        later.own(EARLY)
         output.wait()
         swap.wait(*mg_swap)
 
@@ -876,7 +926,12 @@
         lax.fori_loop(0, nc, drain, 0)
         swap.drain(*m_swap)
         swap.drain(*mg_swap)
-        weights.drain()
+        weights.drain_own(range(nl))
+        weights.drain_crossing(range(nl))
+        for side in (0, 1):
+            weights.drain_shared(side, range(nl))
+        later.drain_own(range(EARLY + 1))
+        later.drain_crossing(range(EARLY))
         output.drain()
 
     dma = pltpu.SemaphoreType.DMA
@@ -895,10 +950,12 @@
             shape((t, LANES), BF16),
             shape((t, LANES), F32),
             shape((nl, part, 2 * npad), BF16),
+            shape((down_rows, d + LANES), BF16),
+            shape((d, 2 * npad), BF16),
             shape((t, d), BF16),
         ),
-        [VM, ANY, VM, VM, VM, VM, ANY, VM, VM, VM, VM, ANY, VM, VM, VM],
-        (VM,) * 11 + (ANY,),
+        [VM, ANY, VM, VM, VM, VM, ANY, VM, VM, VM, VM, ANY, VM, VM, VM, VM, VM, VM],
+        (VM,) * 12 + (ANY, ANY),
         ag_scratch(nl, nc, t, d)
         + [dma((nc,))] * 4
         + [dma((6,))]
@@ -909,14 +966,15 @@
             pltpu.VMEM((3, part, d // 2), BF16),
             pltpu.VMEM((2, part, ff_half), BF16),
             dma((2,)),
-        ],
+        ]
+        + spread_scratch(ny, nl),
         1,
         90,
         (
             x_in, w_qkv, a_qkv, b_qkv, tail_qkv, gains, rows_out, small, small_gu, cosine, sine,
-            w_gu, a_gu, b_gu, tail_gu,
+            w_gu, a_gu, b_gu, tail_gu, w_down, a_down, b_down,
         ),
-        late=(9, 10, 12, 13, 14),
+        late=(9, 10, 12, 13, 14, 15, 16, 17),
         flow=(7, 8, 9),
         step=tc,
     )
@@ -987,18 +1045,15 @@
     )
 
 
-def out_forward(cfg, ny, npad, attended, weights, x, magnitude, blocks, w_down, a_down, b_down):
+def out_forward(cfg, ny, npad, attended, weights, x, magnitude, w_gu, blocks, rows_down):
     t, fw, d, nl, nc, tc = cfg
-    wide = blocks.shape[2]
-    nf = w_down.shape[0]
-    part = -(-(-(-nf // ny)) // (16 * PIECES)) * 16 * PIECES
-    tiles = 2 * nl
+    part = rows_down.shape[0] // ny
 
     def kernel(
-        io, a_ref, w_ref, x_ref, m_ref, e_ref, wdown_ref, ad_ref, bd_ref,
+        io, a_ref, w_ref, x_ref, m_ref, w_in, e_ref, ed_ref,
         mid_ref, u_ref, st_ref, sc_ref, sq_ref, lora_ref, wg_ref, wd_ref,
         sb, cb, gb, s1, r1, s2, r2, cpart, cheld, css, csr,
-        hs, hr, ps, pr, pn, ys, yr, dws, dwr, dwl, dys, dyr, ed_ref,
+        hs, hr, ps, pr, pn, ys, yr, dws, dwr, dwl, dys, dyr,
     ):
         cm = Comm(nl, nc, tc, fw, back_by_two=0.0625)
         cm.rs_refs(sb, cb, gb, s1, r1, s2, r2)
@@ -1007,21 +1062,16 @@
         swap = Swap(cm)
         down_rows = RowMove(swap, ny, part, ed_ref, wd_ref, dws, dwr, dwl, dys, dyr)
         cm.barrier(movers(ny), [swap.partner])
-        columns.start()
+        down_rows.start()
+        columns.start_crossing(EARLY)
+        columns.start(range(EARLY + 1, nl))
+        for m in range(EARLY):
+            columns.share(0, m)
+            columns.share(1, m)
+        columns.share(0, EARLY)
         cm.cs_start(w_ref)
-        columns.pass_own(0)
-        if part * ny > nf:
-            ed_ref[nf:, :] = jnp.zeros((part * ny - nf, ed_ref.shape[1]), BF16)
         if part * ny < npad:
             wd_ref[part * ny :, :] = jnp.zeros((npad - part * ny, wd_ref.shape[1]), BF16)
-        io.ready()
-        ed_ref[:nf, d:] = jnp.zeros((nf, LANES), BF16)
-        ed_ref[:nf, d : d + RANK] = ad_ref[...].astype(BF16)
-
-        def down_tile(k):
-            at = pl.ds(pl.multiple_of(k * fw, fw), fw)
-            ed_ref[:nf, at] = merged_tile(wdown_ref[:, at], ad_ref[...], bd_ref[:, at]).astype(BF16)
-
         def body(i, carry_on):
             @pl.when(i < nc)
             def _():
@@ -1041,24 +1091,23 @@
                 total = cm.cs_total()
                 sq_ref[...] = jnp.broadcast_to(total, (8, fw))
                 sc_ref[...] = jnp.broadcast_to(m_ref[3:4, :] * lax.rsqrt(total), (8, fw))
-                for m in range(2, nl):
-                    columns.pass_own(m)
+
+            @pl.when(i == 5)
+            def _():
+                down_rows.pass_on()
 
             @pl.when(i == 1)
             def _():
-                columns.pass_own(1)
-
-            @pl.when((i >= 1) & (i <= tiles))
+                columns.pass_own(EARLY + 1)
+
+            @pl.when(i == 3)
             def _():
-                down_tile(i - 1)
-
-            @pl.when(i == min(6, nc + 1))
+                for m in range(EARLY + 2, nl):
+                    columns.pass_own(m, cross=False)
+
+            @pl.when(i == min(6, nc + 2))
             def _():
-                columns.pass_crossed(0)
-
-            @pl.when(i == nc + 2)
-            def _():
-                columns.pass_crossed(1)
+                columns.pass_crossed(EARLY, EARLY + 2)
 
             @pl.when((i >= 3) & (i <= nc + 2))
             def _():
@@ -1066,27 +1115,29 @@
                 middle = x_ref[rows, :].astype(F32) + cm.rs_total(i - 3) * sc_ref[0:1, :]
                 mid_ref[rows, :] = middle
                 u_ref[rows, :] = middle.astype(BF16)
-                st_ref[:, rows] = ones_rows(middle * middle)
+                st_ref[i - 3] = ones_rows(middle * middle)[0:1, :]
                 io.store(i - 3, 0, 1)
 
             return carry_on
 
-        lax.fori_loop(0, max(nc + 3, tiles + 1), body, 0)
+        lax.fori_loop(0, nc + 3, body, 0)
 
         def drain(i, carry_on):
             cm.rs_drain(i)
             io.stored(i)
             return carry_on
 
-        down_rows.start()
-        for m in range(2, nl):
-            columns.pass_crossed(m)
-        down_rows.pass_on()
-        columns.wait()
+        for m in range(EARLY + 1, nl):
+            columns.pass_crossed(m, m + 2)
+        for side in (0, 1):
+            columns.wait(side, range(nl))
         down_rows.wait()
         lax.fori_loop(0, nc, drain, 0)
         cm.cs_drain()
-        columns.drain()
+        columns.drain_own(range(EARLY + 1, nl))
+        columns.drain_crossing(range(EARLY, nl))
+        for side in (0, 1):
+            columns.drain_shared(side, range(nl))
         down_rows.drain()
 
     return call(
@@ -1095,26 +1146,25 @@
         (
             shape((t, fw), F32),
             shape((t, fw), BF16),
-            shape((8, t), F32),
+            shape((nc, 1, tc), F32),
             shape((8, fw), F32),
             shape((8, fw), F32),
             shape((t, LANES), BF16),
-            shape((d, wide), BF16),
+            shape(w_gu.shape, BF16),
             shape((npad, d + LANES), BF16),
         ),
-        [VM] * 4 + [ANY, VM, VM, VM],
+        [VM] * 4 + [ANY, ANY, ANY],
         (VM,) * 6 + (ANY, VM),
         rs_scratch(nl, nc, tc, fw)
         + cs_scratch(nl, d, fw)
         + spread_scratch(ny, nl)
-        + row_move_scratch(ny)
-        + [pltpu.VMEM((part * ny, d + LANES), BF16)],
+        + row_move_scratch(ny),
         2,
         90,
-        (attended, weights, x, magnitude, blocks, w_down, a_down, b_down),
-        late=(5, 6, 7),
+        (attended, weights, x, magnitude, w_gu, blocks, rows_down),
         flow=(0, 1, 5),
         step=tc,
+        aliases={4: 6},
     )
 
 
@@ -1125,9 +1175,9 @@
         io, u_ref, st_ref, wg_ref, mg_ref, wd_ref, m_ref, mid_ref, cin_ref,
         gu_ref, hid_ref, out_ref, gm_ref, rate_ref, gp_ref, sg_ref, qg_ref, sd_ref, qd_ref, lora_ref, cot_ref, uf_ref,
         full, own, sd, rd, sc, rc, sb, cb, gb, s1, r1, s2, r2, sa, ss, sr, cpart, cheld, css, csr, keep,
-        stage, cs_s, cs_r, cs_l, bs_s, bs_r, bs_l,
+        cs_s, cs_r, cs_l,
     ):
-        cm = Comm(nl, nc, tc, fw, out_by_one=0.75, back_by_two=0.25)
+        cm = Comm(nl, nc, tc, fw, out_by_one=0.625, back_by_two=0.375)
         cm.ag_refs(u_ref, full, own, sd, rd, sc, rc)
         cm.rs_refs(sb, cb, gb, s1, r1, s2, r2)
         cm.st_refs(st_ref, sa, ss, sr)
@@ -1139,15 +1189,7 @@
             rows = cm.rows(i)
             return cin_ref.at[rows], cot_ref.at[rows], (cs_s.at[i], cs_r.at[i], cs_l.at[i])
 
-        def out_swap(i):
-            rows = cm.rows(i)
-            return stage.at[rows], out_ref.at[rows], (bs_s.at[i], bs_r.at[i], bs_l.at[i])
-
-        def stats_out(i, carry_on):
-            cm.st_send(i)
-            return carry_on
-
-        lax.fori_loop(0, nc, stats_out, 0)
+        cm.st_send(None)
         cm.ag_start()
         io.ready()
 
@@ -1185,12 +1227,16 @@
             def _():
                 cm.ag_step(i + 2)
                 cm.ag_wait(i)
-                cm.st_wait(i)
+
+                @pl.when(i == 0)
+                def _():
+                    cm.st_wait(None)
+
                 stored(i).start()
                 rows = cm.rows(i)
                 rate = lax.rsqrt(cm.st_sum(i) / d + EPS)
-                rate_ref[rows, :] = rate
-                out = nn(full[rows, :], wg_ref[...]) * rate[:, 0:1] * sg_ref[0:1, :]
+                rate_ref[rows, :] = jnp.broadcast_to(rate, (tc, LANES))
+                out = nn(full[rows, :], wg_ref[...]) * rate * sg_ref[0:1, :]
                 gu_ref[rows, :] = out.astype(BF16)
                 gate, up = out[:, :npad], out[:, npad:]
                 hidden = (gate / (1.0 + jnp.exp(-gate)) * up).astype(BF16)
@@ -1215,13 +1261,12 @@
             def _():
                 rows = cm.rows(i - 3)
                 down = cm.rs_total(i - 3) * sd_ref[0:1, :]
-                stage[rows, :] = (mid_ref[rows, :] + down).astype(BF16)
-                swap.start(*out_swap(i - 3))
+                out_ref[rows, :] = (mid_ref[rows, :] + down).astype(BF16)
                 swap.wait(*cot_swap(i - 3))
                 seed = cot_ref[rows, :].astype(F32)
                 gm_ref[0:1, :] += row_sum(seed * down)
                 gp_ref[rows, :] = (seed * sd_ref[0:1, :]).astype(BF16)
-                io.store(i - 3, 5)
+                io.store(i - 3, 2, 5)
 
             return carry_on
 
@@ -1230,15 +1275,13 @@
         def drain(i, carry_on):
             cm.ag_drain(i)
             cm.rs_drain(i)
-            cm.st_drain(i)
             stored(i).wait()
             io.stored(i)
-            swap.wait(*out_swap(i))
-            swap.drain(*out_swap(i))
             swap.drain(*cot_swap(i))
             return carry_on
 
         lax.fori_loop(0, nc, drain, 0)
+        cm.st_drain(None)
         cm.cs_drain()
 
     dma = pltpu.SemaphoreType.DMA
@@ -1266,13 +1309,12 @@
         + rs_scratch(nl, nc, tc, fw)
         + st_scratch(nl, nc, t)
         + cs_scratch(nl, d, fw)
-        + [dma((nc,)), pltpu.VMEM((t, fw), BF16)]
-        + [dma((nc,))] * 6,
+        + [dma((nc,))] * 4,
         3,
         110,
         (u, stats, w_gu, m_gu, w_down, small, middle, cotangent),
         late=(2, 4, 6),
-        flow=(0, 1, 4, 5, 10),
+        flow=(0, 1, 2, 4, 5, 10),
         step=tc,
     )
 
@@ -1334,7 +1376,7 @@
                 pg, pu = dgate * gate, dup * up
                 gm_ref[0:1, :npad] += jnp.sum(pg, axis=0, keepdims=True)
                 gm_ref[0:1, npad:] += jnp.sum(pu, axis=0, keepdims=True)
-                st[:, rows] = ones_rows(pg + pu)
+                st[i] = ones_rows(pg + pu)[0:1, :]
                 cm.st_send(i)
                 gu_s[rows, :npad] = (dgate * sg_ref[0:1, :npad]).astype(BF16)
                 gu_s[rows, npad:] = (dup * sg_ref[0:1, npad:]).astype(BF16)
@@ -1356,7 +1398,7 @@
                 rows = cm.rows(k)
                 cm.st_wait(k)
                 r = rate_ref[rows, 0:1]
-                inner = cm.st_sum(k)[:, 0:1]
+                inner = cm.st_sum(k)
                 mid = mid_ref[rows, :]
                 dm = (
                     cot_ref[rows, :].astype(F32)
@@ -1404,7 +1446,7 @@
         + rs_scratch(nl, nc, tc, fw)
         + st_scratch(nl, nc, t)
         + [
-            pltpu.VMEM((8, t), F32),
+            pltpu.VMEM((nc, 1, tc), F32),
             pltpu.VMEM((t, 2 * npad), BF16),
             pltpu.SemaphoreType.DMA((nc,)),
             pltpu.SemaphoreType.DMA((nc,)),
@@ -1454,7 +1496,7 @@
 
 def out_backward(
     cfg, npad, nf, go, weights, b_out, ratios, w_gu, w_down, up_gu, b_down, gm_gu, square_gu, m_gu,
-    u_full, lg_gu, gu, dp_gu, hidden, lg_down, lora_down, gp_full,
+    u_full, lg_gu, gu, dp_gu, hidden, lg_down, lora_down, gp_full, result,
 ):
     t, fw, d, nl, nc, tc = cfg
     off = nf - (npad - LANES)
@@ -1462,11 +1504,13 @@
 
     def kernel(
         io, go_ref, w_ref, b_ref, q_ref, wg_ref, wd_ref, up_ref, bd_ref, gm_ref, sq_ref, m_ref,
-        uf_hbm, lg_hbm, gu_hbm, dp_hbm, hid_hbm, ld_hbm, lo2_hbm, gp_hbm,
-        da_ref, lo_ref, qs_ref, sh_ref, lc_ref, gf_ref,
-        full, own, sd, rd, sc, rc, keep, qss, qsr, acc_a, acc_g, acc_u, acc_d, acc_p, *streams,
+        uf_hbm, lg_hbm, gu_hbm, dp_hbm, hid_hbm, ld_hbm, lo2_hbm, gp_hbm, res_hbm,
+        da_ref, lo_ref, qs_ref, sh_ref, lc_ref, gf_ref, moved_ref,
+        full, own, sd, rd, sc, rc, keep, qss, qsr, res_sems, acc_a, acc_g, acc_u, acc_d, acc_p, *streams,
     ):
-        cm = Comm(nl, nc, tc, fw)
+        cm = Comm(nl, nc, tc, fw, out_by_one=0.75)
+        swap = Swap(cm)
+        result_swap = (res_hbm, moved_ref, tuple(res_sems.at[k] for k in range(3)))
         cm.ag_refs(go_ref, full, own, sd, rd, sc, rc)
         every = lambda n: pl.ds(0, n)
         stream = Stream(
@@ -1486,7 +1530,7 @@
             tc,
         )
         stream.start(jnp.int32(0))
-        cm.barrier()
+        cm.barrier((), [swap.partner])
 
         def ratio_copy(o, m):
             k = o * nl + m
@@ -1498,6 +1542,7 @@
         for o, m in cm.st_peers():
             ratio_copy(o, m).start()
         qs_ref[:, cm.columns(cm.c, cm.g)] = q_ref[...]
+        swap.start(*result_swap)
         for acc in (acc_a, acc_g, acc_u, acc_d, acc_p):
             acc[...] = jnp.zeros_like(acc)
         cm.ag_ahead()
@@ -1564,6 +1609,8 @@
             return carry_on
 
         lax.fori_loop(0, nc, drain, 0)
+        swap.wait(*result_swap)
+        swap.drain(*result_swap)
         for o, m in cm.st_peers():
             ratio_copy(o, m).wait_send()
 
@@ -1578,18 +1625,19 @@
             shape((3 * RANK, d), BF16),
             shape((4 * RANK, npad), BF16),
             shape((t, d), BF16),
+            shape((t, fw), BF16),
         ),
-        [VM] * 11 + [ANY] * 8,
-        (VM,) * 5 + (ANY,),
+        [VM] * 11 + [ANY] * 9,
+        (VM,) * 5 + (ANY, ANY),
         ag_scratch(nl, nc, t, d)
-        + [dma((nc,)), dma((2 * nl,)), dma((2 * nl,))]
+        + [dma((nc,)), dma((2 * nl,)), dma((2 * nl,)), dma((3,))]
         + [pltpu.VMEM((LANES, n), F32) for n in (d, npad, npad, npad, d)]
         + stream_scratch(tc, widths),
         5,
         60,
         (
             go, weights, b_out, ratios, w_gu, w_down, up_gu, b_down, gm_gu, square_gu, m_gu,
-            u_full, lg_gu, gu, dp_gu, hidden, lg_down, lora_down, gp_full,
+            u_full, lg_gu, gu, dp_gu, hidden, lg_down, lora_down, gp_full, result,
         ),
         late=(1, 2, 4, 5, 6, 7),
     )
@@ -1662,7 +1710,7 @@
                     inner = inner + product
                     gm_ref[0:1, where] += row_sum(product)
                     dp_ref[rows, where] = (dout * scale_ref[0:1, where]).astype(BF16)
-            st_ref[:, rows] = ones_rows(inner)
+            st_ref[i] = ones_rows(inner)[0:1, :]
             lg_ref[rows, :] = (nt(dp_ref[rows, :], b_ref[...].astype(BF16)) * rate_ref[rows, :]).astype(BF16)
             return carry_on
 
@@ -1673,7 +1721,7 @@
         "attention_backward",
         (
             shape((t, width), BF16),
-            shape((8, t), F32),
+            shape((t // block, 1, block), F32),
             shape((8, width), F32),
             shape((t, LANES), BF16),
         ),
@@ -1705,7 +1753,7 @@
         stage, gs_s, gs_r, gs_l, group, gsum, gss, gsr, final_a, final_b, final_l, fs, fr, fl,
         a_ref, b_ref, acc_a, acc_b, acc_o, acc_p, *streams,
     ):
-        cm = Comm(nl, nc, tc, fw, back_by_two=0.375)
+        cm = Comm(nl, nc, tc, fw, back_by_two=0.25)
         c, g = cm.c, cm.g
         y, h = lax.axis_index("y"), lax.axis_index("h")
         cm.rs_refs(sb, cb, gb, s1, r1, s2, r2)
@@ -1756,11 +1804,7 @@
                 for n, (src, dst) in enumerate(((gsum, final_a), (b_ref, final_b), (l_ref, final_l)))
             ]
 
-        def stats_out(i, carry_on):
-            cm.st_send(i)
-            return carry_on
-
-        lax.fori_loop(0, nc, stats_out, 0)
+        cm.st_send(None)
         for acc in (acc_a, acc_b, acc_o, acc_p):
             acc[...] = jnp.zeros_like(acc)
 
@@ -1862,9 +1906,13 @@
             def _():
                 k = i - 3
                 rows = cm.rows(k)
-                cm.st_wait(k)
+
+                @pl.when(k == 0)
+                def _():
+                    cm.st_wait(None)
+
                 r = rate_ref[rows, 0:1]
-                inner = cm.st_sum(k)[:, 0:1]
+                inner = cm.st_sum(k)
                 stage[rows, :] = (
                     dm_ref[rows, :]
                     + r * cm.rs_total(k)
@@ -1910,11 +1958,11 @@
         def drain(i, carry_on):
             swap.wait(*grad_swap(i))
             cm.rs_drain(i)
-            cm.st_drain(i)
             swap.drain(*grad_swap(i))
             return carry_on
 
         lax.fori_loop(0, nc, drain, 0)
+        cm.st_drain(None)
         for o, m in cm.st_peers():
             gather_part(o, m).wait_send()
         for k in range(ny):
@@ -2026,9 +2074,9 @@
     nf = m_gu.shape[1]
     npad = -(-(nf + RANK) // LANES) * LANES
     width = 3 * fw
-    nc = 8 if t % 1024 == 0 else 1
-    cfg = (t, fw, d, nl, nc, t // nc)
-    block = min(256, t)
+    nc = t // 256 if t % 256 == 0 else 1
+    block = t // nc
+    cfg = (t, fw, d, nl, nc, block)
     y, c, h, g = (lax.axis_index(name) for name in ("y", "c", "h", "g"))
     role = c * nl + g
 
@@ -2108,14 +2156,14 @@
 
     (
         x, weights_qkv, weights_out, small, small_gu, scale_qkv, square_qkv, qkv, lora_qkv_in, rate_attn,
-        blocks_gu, x_full,
+        blocks_gu, rows_down, weights_gu, x_full,
     ) = qkv_forward(
         cfg, ny, npad, nf, inputs, w_qkv, a_qkv, b_qkv, tail_qkv, gains, rows_out, small, small_gu, cosine, sine,
-        w_gu, a_gu, b_gu_padded, tail_gu,
+        w_gu, a_gu, b_gu_padded, tail_gu, w_down, a_down, b_down,
     )
     attended, lse = attention_forward(cfg, qkv, seg_column, seg_row, first_block, block)
     middle, u, stats, sc_out, square_out, lora_out, weights_gu, weights_down = out_forward(
-        cfg, ny, npad, attended, weights_out, x, small, blocks_gu, w_down, a_down, b_down
+        cfg, ny, npad, attended, weights_out, x, small, weights_gu, blocks_gu, rows_down
     )
     (
         gu, hidden, block_out, gm_down, rate_ffn, gp, scale_gu, square_gu, sc_down, square_down,
@@ -2131,9 +2179,9 @@
     ratios = jnp.concatenate(
         [-gm_out[0:1] / square_out[0:1], -gm_down[0:1] / square_down[0:1], jnp.zeros((6, fw), F32)], axis=0
     )
-    grad_attended, lg_out, ratios, shared, local_gu, go_full = out_backward(
+    grad_attended, lg_out, ratios, shared, local_gu, go_full, block_out = out_backward(
         cfg, npad, nf, go, weights_out, up_out, ratios, weights_gu, weights_down, up_gu, up_down, gm_gu, square_gu,
-        small_gu, u_full, lg_gu, gu, dp_gu, hidden, lg_down, lora_down, gp_full,
+        small_gu, u_full, lg_gu, gu, dp_gu, hidden, lg_down, lora_down, gp_full, block_out,
     )
     dp_qkv, inner, gm_qkv, lg_qkv = attention_backward(
         cfg, qkv, attended, grad_attended, lse, seg_column, seg_row, first_block, block, cosine, sine,

time: 691 us -> 673 us (0.974)
  Pallas kernels: 653 us -> 633 us
    pallas_call x9, Pallas kernels: 653 us -> 633 us  [call(): pl.pallas_call(whole, name=name, out_shape=outs, in_specs=in_specs, out_s...]
where the time goes in v2:
time: 673 us; the launch traced here: 666 us
  Pallas kernels  633 us (94%)
  local copies, waits for them, and re-layouts  16.1 us (2%)
  other arithmetic  12 us (2%)
    pallas_call x9, Pallas kernels, call(): pl.pallas_call(whole, name=name, out_shape=outs, in_specs=in_specs, out_s...  633 us

profile of v2, /device:TPU:1, one launch (start us, length us, event | category | flops | bytes accessed | tf_op | source)
XLA Modules:
  0.0 666.3 jit_solution(2045334390853943788)
XLA Ops:
  0.7 2.0 all-gather
  3.5 3.7 fusion.4
  7.2 1.9 pad_maximum_fusion
  9.7 1.0 pad_maximum_fusion.2.refs_14_
  12.0 1.0 pad_bitcast_fusion.refs_13_
  13.0 1.9 fusion.1
  15.1 1.1 fusion.3.refs_6_
  16.2 0.9 copy.78.refs_2_
  17.1 0.9 copy.80.refs_16_
  18.9 0.9 copy.79.refs_12_
  21.1 134.8 %qkv_forward.1 = (bf16[2048,256]{1,0:T(8,128)(2,1)}, bf16[2048,896]{1,0:T(8,128)(2,1)}, bf16[256,2176]{1,0:T(8,128)(2,1)}, f32[8,256]{1,0:T(8,128)}, f32[8,1536]...) custom-call(bf16[2048,256]{1,0:T(8,128)(2,1)} %refs_0_.1, ...), custom_call_target="tpu_custom_call" | custom-call | flops 44999999488 | bytes 270000000 | tf_op jit(solution)/shard_map/qkv_forward/pallas_call | solution.py:706
  156.6 1.3 broadcast_in_dim.123.refs_1_.refs_4_
  158.5 20.1 %attention_forward.1 = (bf16[2048,256]{1,0:T(8,128)(2,1)}, f32[16,2048]{1,0:T(8,128)}) custom-call(bf16[2048,768]{1,0:T(8,128)(2,1)} %get-tuple-element.87.refs_0_, s32[2048,128]{1,0:T(8,128)} %broadcast_in_dim.123.refs_1_.refs_4_, s32[8,2048]{1,0:T(8,128)} %broadcast_in_dim.124.refs_2_.refs_5_, s32[8]{0:T(128)} %and_select_fusion.refs_3_.refs_6_), custom_call_target="tpu_custom_call" | custom-call | flops 7500000256 | bytes 45000000 | tf_op jit(solution)/shard_map/attention_forward/pallas_call | solution.py:706
  178.6 128.6 %out_forward.1 = (f32[2048,256]{1,0:T(8,128)}, bf16[2048,256]{1,0:T(8,128)(2,1)}, f32[8,1,256]{2,1,0:T(1,128)}, f32[8,256]{1,0:T(8,128)}, f32[8,256]{1,0:T(8,128...) custom-call(bf16[2048,256]{1,0:T(8,128)(2,1)} %get-tuple-element.88., ...), custom_call_target="tpu_custom_call", output_to_operand_aliasing={{6}: (4, {})} | custom-call | flops 44999999488 | bytes 270000000 | tf_op jit(solution)/shard_map/out_forward/pallas_call | solution.py:706
  307.2 1.4 slice.58.refs_3_
  308.6 95.5 %ffn_forward.1 = (bf16[2048,1536]{1,0:T(8,128)(2,1)}, bf16[2048,768]{1,0:T(8,128)(2,1)}, bf16[2048,256]{1,0:T(8,128)(2,1)}, f32[8,256]{1,0:T(8,128)}, f32[2048,1...) custom-call(bf16[2048,256]{1,0:T(8,128)(2,1)} %get-tuple-element.95., ...), custom_call_target="tpu_custom_call" | custom-call | flops 54999998464 | bytes 330000000 | tf_op jit(solution)/shard_map/ffn_forward/pallas_call | solution.py:706
  404.1 1.0 constant_dynamic-slice_fusion.1
  405.3 1.0 pad.57.refs_4_.refs_6_
  407.1 78.4 %ffn_backward.1 = (f32[2048,256]{1,0:T(8,128)}, bf16[2048,256]{1,0:T(8,128)(2,1)}, f32[8,256]{1,0:T(8,128)}, f32[8,1536]{1,0:T(8,128)}, bf16[2048,128]{1,0:T(8,1...) custom-call(bf16[2048,256]{1,0:T(8,128)(2,1)} %get-tuple-element.101.refs_0_, ...), custom_call_target="tpu_custom_call" | custom-call | flops 60000002048 | bytes 360000000 | tf_op jit(solution)/shard_map/ffn_backward/pallas_call | solution.py:706
  487.7 0.9 pad.59.refs_2_.refs_10_
  488.6 63.4 %out_backward.1 = (bf16[2048,256]{1,0:T(8,128)(2,1)}, bf16[2048,128]{1,0:T(8,128)(2,1)}, f32[8,2048]{1,0:T(8,128)}, bf16[48,2048]{1,0:T(8,128)(2,1)}, bf16[64,76...) custom-call(bf16[2048,256]{1,0:T(8,128)(2,1)} %get-tuple-element.107.refs_0_, ...), custom_call_target="tpu_custom_call" | custom-call | flops 30000001024 | bytes 180000000 | tf_op jit(solution)/shard_map/out_backward/pallas_call | solution.py:706
  553.7 30.7 %attention_backward.1 = (bf16[2048,768]{1,0:T(8,128)(2,1)}, f32[8,1,256]{2,1,0:T(1,128)}, f32[8,768]{1,0:T(8,128)}, bf16[2048,128]{1,0:T(8,128)(2,1)}) custom-call(bf16[2048,768]{1,0:T(8,128)(2,1)} %get-tuple-element.87.refs_0_, bf16[2048,256]{1,0:T(8,128)(2,1)} %get-tuple-element.88.refs_0_.refs_1_.refs_20_, bf16[2048,256]{1,0:T(8,128)(2,1)} %get-tuple-element.122.refs_2_, ...), custom_call_target="tpu_custom_call" | custom-call | flops 17500000256 | bytes 105000000 | tf_op jit(solution)/shard_map/attention_backward/pallas_call | solution.py:706
  584.5 78.1 %qkv_backward.1 = (bf16[2048,256]{1,0:T(8,128)(2,1)}, f32[112,256]{1,0:T(8,128)}, f32[80,256]{1,0:T(8,128)}, f32[64,768]{1,0:T(8,128)}) custom-call(bf16[2048,768]{1,0:T(8,128)(2,1)} %get-tuple-element.126.refs_0_, f32[8,1,256]{2,1,0:T(1,128)} %get-tuple-element.127.refs_1_, bf16[2048,896]{1,0:T(8,128)(2,1)} %get-tuple-element.128.refs_2_, ...), custom_call_target="tpu_custom_call" | custom-call | flops 35000000512 | bytes 210000000 | tf_op jit(solution)/shard_map/qkv_backward/pallas_call | solution.py:706
  662.5 3.6 last_step.1
  (88 shorter events, 11.1 us)
Async XLA Ops:
  7.2 2.0 copy-start.5
  7.2 2.0 copy-start.10
  9.2 1.5 copy-start.4
  9.2 1.5 copy-start.9
  9.2 2.3 copy-start.1
  11.5 1.5 copy-start
  11.5 1.5 copy-start.2
  11.5 1.5 copy-start.7
  13.0 4.1 copy-start.8
  14.9 4.8 copy-start.11
  15.0 5.5 copy-start.12
  15.0 5.5 copy-start.13
  15.0 5.5 copy-start.14
  308.6 97.6 %copy-start.6 = (f32[16,2048]{1,0:T(8,128)S(1)}, f32[16,2048]{1,0:T(8,128)}, u32[]{:S(2)}) copy-start(f32[16,2048]{1,0:T(8,128)} %refs_17_.1) | copy-start | bytes 393220
  407.1 80.6 %copy-start.3 = (f32[16,2048]{1,0:T(8,128)S(1)}, f32[16,2048]{1,0:T(8,128)}, u32[]{:S(2)}) copy-start(f32[16,2048]{1,0:T(8,128)} %param.31) | copy-start | bytes 393220

commit v3 on v2

--- a/solution.py
+++ b/solution.py
@@ -1,7 +1,6 @@
-import math
-
 import jax
 import jax.numpy as jnp
+import numpy as np
 from jax import lax
 from jax.experimental import pallas as pl
 from jax.experimental.pallas import tpu as pltpu
@@ -18,6 +17,7 @@
 F32 = jnp.float32
 BF16 = jnp.bfloat16
 LANES = 128
+SEGMENTS = 8
 VMEM_LIMIT = 60 * 1024 * 1024
 
 
@@ -738,12 +738,16 @@
 
 
 def merged_tile(frozen, down, up):
-    return frozen.astype(F32) + SCALE * nn(down, up, HIGHEST)
+    down_high, up_high = down.astype(BF16), up.astype(BF16)
+    down_low = (down - down_high.astype(F32)).astype(BF16)
+    up_low = (up - up_high.astype(F32)).astype(BF16)
+    low = nn(down_high, up_high) + (nn(down_high, up_low) + nn(down_low, up_high))
+    return frozen.astype(F32) + SCALE * low
 
 
 def qkv_forward(
-    cfg, ny, npad, nf, x_in, w_qkv, a_qkv, b_qkv, tail_qkv, gains, rows_out, small, small_gu, cosine, sine,
-    w_gu, a_gu, b_gu, tail_gu, w_down, a_down, b_down,
+    cfg, ny, npad, nf, x_in, w_qkv, a_qkv, b_qkv, tail_qkv, gains, w_out, small, small_gu, segments, turns,
+    w_gu, a_gu, b_gu, tail_gu, w_down, a_down, b_down, a_out, b_out,
 ):
     t, fw, d, nl, nc, tc = cfg
     width = 3 * fw
@@ -753,12 +757,12 @@
     ff_half = w_gu.shape[2] // 2
 
     def kernel(
-        io, x_ref, wq_hbm, aq_ref, bq_ref, tq_ref, gain_ref, eo_ref, m_ref, mg_ref, cos_ref, sin_ref,
-        wg_hbm, ag_ref, bg_ref, tg_ref, wdown_ref, ad_ref, bd_ref,
-        xs_ref, w_ref, wo_ref, ms_ref, mgs_ref, sc_ref, sq_ref, qkv_ref, lora_ref, rate_ref, eg_ref, ed_ref, wgs_ref, out_ref,
+        io, x_ref, wq_hbm, aq_ref, bq_ref, tq_ref, gain_ref, wout_ref, m_ref, mg_ref, seg_ref, ta_ref, tb_ref,
+        wg_hbm, ag_ref, bg_ref, tg_ref, wdown_ref, ad_ref, bd_ref, ao_ref, bo_ref,
+        xs_ref, w_ref, wo_ref, ms_ref, mgs_ref, sc_ref, sq_ref, qkv_ref, lora_ref, rate_ref, eg_ref, ed_ref, wgs_ref, out_ref, cos_ref, sin_ref, sgc_ref, sgr_ref,
         full, own, sd, rd, sc, rc, keep, xs_s, xs_r, xs_l, small_sems,
         hs, hr, ps, pr, pn, ys, yr, os, orr, ol, oys, oyr,
-        e_ref, wq, wg, wload, ghs, ghr, gps, gpr, gpn, gys, gyr,
+        e_ref, wq, wg, wload, eo_ref, sg, place, ghs, ghr, gps, gpr, gpn, gys, gyr,
     ):
         cm = Comm(nl, nc, tc, fw, out_by_one=0.9375)
         cm.ag_refs(xs_ref, full, own, sd, rd, sc, rc)
@@ -784,6 +788,8 @@
         m_swap = (m_ref, ms_ref, tuple(small_sems.at[k] for k in range(3)))
         mg_swap = (mg_ref, mgs_ref, tuple(small_sems.at[k] for k in range(3, 6)))
 
+        seg_swap = (seg_ref, sg, tuple(small_sems.at[k] for k in range(6, 9)))
+
         def start_swap(i, carry_on):
             swap.start(*token_swap(i))
             return carry_on
@@ -791,6 +797,7 @@
         lax.fori_loop(0, min(WINDOW, nc), start_swap, 0)
         swap.start(*m_swap)
         swap.start(*mg_swap)
+        swap.start(*seg_swap)
         load_q.wait()
         gain_attn, gain_ffn = gain_ref[mine, 0:1], gain_ref[mine, 1:2]
         for gg in range(nl):
@@ -814,14 +821,17 @@
                     lane < nf, tile, tg_ref[k, mine, :].astype(F32)
                 ).astype(BF16)
 
-        def down_tiles(k):
+        def merged_rows(k):
             if k == 0:
                 if down_rows > nf:
                     ed_ref[nf:, :] = jnp.zeros((down_rows - nf, ed_ref.shape[1]), BF16)
                 ed_ref[:nf, d:] = jnp.zeros((nf, LANES), BF16)
                 ed_ref[:nf, d : d + RANK] = ad_ref[...].astype(BF16)
+                eo_ref[:, d:] = jnp.zeros((fw, LANES), BF16)
+                eo_ref[:, d : d + RANK] = ao_ref[...].astype(BF16)
             for n in (2 * k, 2 * k + 1):
                 at = slice(n * fw, (n + 1) * fw)
+                eo_ref[:, at] = merged_tile(wout_ref[:, at], ao_ref[...], bo_ref[:, at]).astype(BF16)
                 ed_ref[:nf, at] = merged_tile(wdown_ref[:, at], ad_ref[...], bd_ref[:, at]).astype(BF16)
 
         def gather(i, carry_on):
@@ -851,7 +861,7 @@
             lax.fori_loop(nc * m // nl, nc * (m + 1) // nl, forward, 0)
             gate_up(m)
             weights.pass_crossed(m, m + 2)
-            down_tiles(m)
+            merged_rows(m)
         output.start()
         later.start(range(EARLY + 1))
         for m in range(EARLY):
@@ -863,7 +873,37 @@
             rows = cm.rows(i)
             return pltpu.make_async_copy(full.at[rows], out_ref.at[rows], keep.at[i])
 
+        swap.wait(*seg_swap)
+        number = sg[...]
+        begin = jnp.zeros((1, t), F32)
+        for n in range(1, SEGMENTS):
+            before = jnp.sum(jnp.where(number < n, 1.0, 0.0), axis=1, keepdims=True)
+            begin = jnp.where(number == n, before, begin)
+        standing = lax.broadcasted_iota(jnp.int32, (1, t), 1).astype(F32) - begin
+        high = jnp.floor(standing * (1.0 / 32.0))
+        place[0:1, :] = high.astype(jnp.int32)
+        place[1:2, :] = (standing - 32.0 * high).astype(jnp.int32)
+        sgr_ref[...] = jnp.broadcast_to(number, (8, t))
+
+        def turn_tables(rows):
+            def chosen(row, count):
+                return jnp.where(lax.broadcasted_iota(jnp.int32, (count, tc), 0) == row, 1.0, 0.0)
+
+            def looked_up(row, table):
+                parts = tn(chosen(row, 32).astype(BF16), table)
+                both = parts[:, : 2 * HD] + parts[:, 2 * HD :]
+                return both[:, :HD], both[:, HD:]
+
+            ca, sa = looked_up(place[0:1, rows], ta_ref[...])
+            cb, sb = looked_up(place[1:2, rows], tb_ref[...])
+            sign = jnp.where(lax.broadcasted_iota(jnp.int32, (tc, HD), 1) < HD // 2, -1.0, 1.0)
+            cos_ref[rows, :] = ca * cb - sa * sb
+            sin_ref[rows, :] = (sa * cb + ca * sb) * sign
+            numbers = lax.broadcasted_iota(jnp.int32, (SEGMENTS, LANES), 0).astype(F32)
+            sgc_ref[rows, :] = tn(chosen(sgr_ref[0:1, rows], SEGMENTS), numbers).astype(jnp.int32)
+
         def rates(i, carry_on):
+            turn_tables(cm.rows(i))
             cm.ag_wait(i)
             stored(i).start()
             wide_block = full[cm.rows(i), :].astype(F32)
@@ -874,7 +914,6 @@
         lax.fori_loop(0, nc, rates, 0)
         for side in (0, 1):
             weights.wait(side, range(nl))
-        output.pass_on()
 
         def squares(i, total):
             rows = pl.ds(pl.multiple_of(i * fw, fw), fw)
@@ -906,10 +945,11 @@
                     qkv_ref[rows, at : at + HD] = value.astype(BF16)
             lora_ref[rows, :] = out[:, width:].astype(BF16)
             for k in range(big // tc):
-                io.store(i * (big // tc) + k, 7, 8, 9)
+                io.store(i * (big // tc) + k, 7, 8, 9, 14, 15, 16)
             return carry_on
 
         lax.fori_loop(0, t // big, body, 0)
+        output.pass_on()
         for m in range(EARLY):
             later.wait_crossing(m)
         later.own(EARLY)
@@ -926,6 +966,7 @@
         lax.fori_loop(0, nc, drain, 0)
         swap.drain(*m_swap)
         swap.drain(*mg_swap)
+        swap.drain(*seg_swap)
         weights.drain_own(range(nl))
         weights.drain_crossing(range(nl))
         for side in (0, 1):
@@ -941,7 +982,7 @@
         (
             shape((t, fw), BF16),
             shape((d, wide), BF16),
-            shape(rows_out.shape, BF16),
+            shape((fw, d + LANES), BF16),
             shape(small.shape, F32),
             shape(small_gu.shape, F32),
             shape((8, wide), F32),
@@ -953,12 +994,16 @@
             shape((down_rows, d + LANES), BF16),
             shape((d, 2 * npad), BF16),
             shape((t, d), BF16),
+            shape((t, HD), F32),
+            shape((t, HD), F32),
+            shape((t, LANES), jnp.int32),
+            shape((8, t), jnp.int32),
         ),
-        [VM, ANY, VM, VM, VM, VM, ANY, VM, VM, VM, VM, ANY, VM, VM, VM, VM, VM, VM],
-        (VM,) * 12 + (ANY, ANY),
+        [VM, ANY] + [VM] * 10 + [ANY] + [VM] * 8,
+        (VM,) * 12 + (ANY, ANY) + (VM,) * 4,
         ag_scratch(nl, nc, t, d)
         + [dma((nc,))] * 4
-        + [dma((6,))]
+        + [dma((9,))]
         + spread_scratch(ny, nl)
         + row_move_scratch(ny)
         + [
@@ -966,16 +1011,19 @@
             pltpu.VMEM((3, part, d // 2), BF16),
             pltpu.VMEM((2, part, ff_half), BF16),
             dma((2,)),
+            pltpu.VMEM((fw, d + LANES), BF16),
+            pltpu.VMEM((1, t), jnp.int32),
+            pltpu.VMEM((8, t), jnp.int32),
         ]
         + spread_scratch(ny, nl),
         1,
         90,
         (
-            x_in, w_qkv, a_qkv, b_qkv, tail_qkv, gains, rows_out, small, small_gu, cosine, sine,
-            w_gu, a_gu, b_gu, tail_gu, w_down, a_down, b_down,
+            x_in, w_qkv, a_qkv, b_qkv, tail_qkv, gains, w_out, small, small_gu, segments, *turns,
+            w_gu, a_gu, b_gu, tail_gu, w_down, a_down, b_down, a_out, b_out,
         ),
-        late=(9, 10, 12, 13, 14, 15, 16, 17),
-        flow=(7, 8, 9),
+        late=(6, 10, 11, *range(13, 21)),
+        flow=(7, 8, 9, 14, 15, 16),
         step=tc,
     )
 
@@ -1177,7 +1225,7 @@
         full, own, sd, rd, sc, rc, sb, cb, gb, s1, r1, s2, r2, sa, ss, sr, cpart, cheld, css, csr, keep,
         cs_s, cs_r, cs_l,
     ):
-        cm = Comm(nl, nc, tc, fw, out_by_one=0.625, back_by_two=0.375)
+        cm = Comm(nl, nc, tc, fw, out_by_one=0.5, back_by_two=0.5)
         cm.ag_refs(u_ref, full, own, sd, rd, sc, rc)
         cm.rs_refs(sb, cb, gb, s1, r1, s2, r2)
         cm.st_refs(st_ref, sa, ss, sr)
@@ -2052,11 +2100,16 @@
     )
 
 
-def positions_of(segment_row):
-    index = jnp.arange(segment_row.shape[0], dtype=jnp.int32)
-    starts = jnp.concatenate([jnp.ones((1,), jnp.bool_), segment_row[1:] != segment_row[:-1]])
-    begin = lax.cummax(jnp.where(starts, index, 0), axis=0)
-    return index - begin, begin
+def turn_constants():
+    f = 10000.0 ** (-2.0 * np.arange(HD // 2) / HD)
+    out = []
+    for scale in (32.0, 1.0):
+        angle = scale * np.arange(32)[:, None] * f[None, :]
+        table = np.concatenate([np.cos(angle), np.cos(angle), np.sin(angle), np.sin(angle)], axis=1)
+        high = table.astype(BF16)
+        low = (table - high.astype(np.float64)).astype(BF16)
+        out.append(jnp.asarray(np.concatenate([high, low], axis=1)))
+    return out
 
 
 def padded(rows, total):
@@ -2080,11 +2133,6 @@
     y, c, h, g = (lax.axis_index(name) for name in ("y", "c", "h", "g"))
     role = c * nl + g
 
-    def merged_of(frozen, down, up):
-        return frozen.astype(F32) + SCALE * jnp.einsum(
-            "kdr,krn->kdn", down, up, precision=HIGHEST
-        )
-
     def two_parts(gain):
         high = gain.astype(BF16)
         return [high[:, None], (gain - high.astype(F32)).astype(BF16)[:, None]]
@@ -2110,13 +2158,6 @@
     b_gu_padded = jnp.pad(
         b_gu.reshape(2, RANK, mp, nf), ((0, 0), (0, 0), (0, 0), (0, npad - nf))
     ).transpose(0, 2, 1, 3)
-    rows_out = jnp.concatenate(
-        [
-            merged_of(w_out[None], a_out[None], b_out[None])[0].astype(BF16),
-            padded(a_out, LANES).astype(BF16),
-        ],
-        axis=1,
-    )
     small = jnp.concatenate([m_qkv, m_out[None], m_down[None], jnp.zeros((3, fw), F32)], axis=0)
     small_gu = jnp.broadcast_to(
         jnp.pad(m_gu, ((0, 0), (0, npad - nf)), constant_values=1.0).reshape(1, 2 * npad), (8, 2 * npad)
@@ -2140,27 +2181,15 @@
     up_out = jnp.pad(b_out, ((0, LANES - RANK), (0, 0))).astype(BF16)
     up_down = jnp.pad(b_down, ((0, LANES - RANK), (0, 0))).astype(BF16)
 
-    segment = lax.dynamic_index_in_dim(
-        lax.all_gather(segments, "c", axis=0, tiled=True), h, 0, keepdims=False
-    )
-    positions, begin = positions_of(segment)
-    first_block = begin[::block] // block
-    seg_row = jnp.broadcast_to(segment[None, :], (8, t))
-    seg_column = jnp.broadcast_to(segment[:, None], (t, LANES))
-    frequencies = jnp.exp(jnp.arange(HD // 2, dtype=F32) * (-2.0 * math.log(10000.0) / HD))
-    angles = positions.astype(F32)[:, None] * frequencies[None, :]
-    cosine = jnp.cos(angles)
-    sine = jnp.sin(angles)
-    cosine = jnp.concatenate([cosine, cosine], axis=1)
-    sine = jnp.concatenate([-sine, sine], axis=1)
-
     (
         x, weights_qkv, weights_out, small, small_gu, scale_qkv, square_qkv, qkv, lora_qkv_in, rate_attn,
-        blocks_gu, rows_down, weights_gu, x_full,
+        blocks_gu, rows_down, weights_gu, x_full, cosine, sine, seg_column, seg_row,
     ) = qkv_forward(
-        cfg, ny, npad, nf, inputs, w_qkv, a_qkv, b_qkv, tail_qkv, gains, rows_out, small, small_gu, cosine, sine,
-        w_gu, a_gu, b_gu_padded, tail_gu, w_down, a_down, b_down,
-    )
+        cfg, ny, npad, nf, inputs, w_qkv, a_qkv, b_qkv, tail_qkv, gains, w_out, small, small_gu, segments,
+        turn_constants(), w_gu, a_gu, b_gu_padded, tail_gu, w_down, a_down, b_down, a_out, b_out,
+    )
+    first_number = seg_row[0, ::block]
+    first_block = jnp.sum((seg_row[0][None, :] < first_number[:, None]).astype(jnp.int32), axis=1) // block
     attended, lse = attention_forward(cfg, qkv, seg_column, seg_row, first_block, block)
     middle, u, stats, sc_out, square_out, lora_out, weights_gu, weights_down = out_forward(
         cfg, ny, npad, attended, weights_out, x, small, weights_gu, blocks_gu, rows_down

time: 673 us -> 648 us (0.963)
  Pallas kernels: 633 us -> 622 us
    pallas_call x9, Pallas kernels: 633 us -> 622 us  [call(): pl.pallas_call(whole, name=name, out_shape=outs, in_specs=in_specs, out_s...]
where the time goes in v3:
time: 648 us; the launch traced here: 647 us
  Pallas kernels  622 us (96%)
  local copies, waits for them, and re-layouts  16.3 us (3%)
  other arithmetic  7.86 us (1%)
    pallas_call x9, Pallas kernels, call(): pl.pallas_call(whole, name=name, out_shape=outs, in_specs=in_specs, out_s...  622 us

profile of v3, /device:TPU:1, one launch (start us, length us, event | category | flops | bytes accessed | tf_op | source)
XLA Modules:
  0.0 646.9 jit_solution(17318425612274990183)
XLA Ops:
  0.7 0.8 fusion.1
  2.7 0.9 pad_maximum_fusion.refs_15_
  6.5 0.9 pad_bitcast_fusion.refs_14_
  7.5 0.9 copy.79.refs_2_
  8.4 0.9 copy.81.refs_17_
  10.2 0.8 copy.80.refs_13_
  13.2 125.2 %qkv_forward.1 = (bf16[2048,256]{1,0:T(8,128)(2,1)}, bf16[2048,896]{1,0:T(8,128)(2,1)}, bf16[256,2176]{1,0:T(8,128)(2,1)}, f32[8,256]{1,0:T(8,128)}, f32[8,1536]...) custom-call(bf16[2048,256]{1,0:T(8,128)(2,1)} %refs_0_.1, ...), custom_call_target="tpu_custom_call" | custom-call | flops 44999999488 | bytes 270000000 | tf_op jit(solution)/shard_map/qkv_forward/pallas_call | solution.py:706
  138.4 0.8 slice.41
  139.3 0.9 slice.42
  140.9 20.8 %attention_forward.1 = (bf16[2048,256]{1,0:T(8,128)(2,1)}, f32[16,2048]{1,0:T(8,128)}) custom-call(bf16[2048,768]{1,0:T(8,128)(2,1)} %get-tuple-element.91.refs_0_, s32[2048,128]{1,0:T(8,128)} %get-tuple-element.92.refs_1_.refs_4_, s32[8,2048]{1,0:T(8,128)} %get-tuple-element.93.refs_2_.refs_5_, s32[8]{0:T(128)} %and_select_fusion.refs_3_.refs_6_), custom_call_target="tpu_custom_call" | custom-call | flops 7500000256 | bytes 45000000 | tf_op jit(solution)/shard_map/attention_forward/pallas_call | solution.py:706
  161.7 126.4 %out_forward.1 = (f32[2048,256]{1,0:T(8,128)}, bf16[2048,256]{1,0:T(8,128)(2,1)}, f32[8,1,256]{2,1,0:T(1,128)}, f32[8,256]{1,0:T(8,128)}, f32[8,256]{1,0:T(8,128...) custom-call(bf16[2048,256]{1,0:T(8,128)(2,1)} %get-tuple-element.94., ...), custom_call_target="tpu_custom_call", output_to_operand_aliasing={{6}: (4, {})} | custom-call | flops 44999999488 | bytes 270000000 | tf_op jit(solution)/shard_map/out_forward/pallas_call | solution.py:706
  288.1 1.4 slice.43.refs_3_
  289.5 92.0 %ffn_forward.1 = (bf16[2048,1536]{1,0:T(8,128)(2,1)}, bf16[2048,768]{1,0:T(8,128)(2,1)}, bf16[2048,256]{1,0:T(8,128)(2,1)}, f32[8,256]{1,0:T(8,128)}, f32[2048,1...) custom-call(bf16[2048,256]{1,0:T(8,128)(2,1)} %get-tuple-element.101, ...), custom_call_target="tpu_custom_call" | custom-call | flops 54999998464 | bytes 330000000 | tf_op jit(solution)/shard_map/ffn_forward/pallas_call | solution.py:706
  381.5 1.0 constant_dynamic-slice_fusion.1
  382.7 1.0 pad.51.refs_4_.refs_6_
  383.6 0.8 pad.52.refs_6_.refs_7_
  384.5 78.0 %ffn_backward.1 = (f32[2048,256]{1,0:T(8,128)}, bf16[2048,256]{1,0:T(8,128)(2,1)}, f32[8,256]{1,0:T(8,128)}, f32[8,1536]{1,0:T(8,128)}, bf16[2048,128]{1,0:T(8,1...) custom-call(bf16[2048,256]{1,0:T(8,128)(2,1)} %get-tuple-element.107.refs_0_, ...), custom_call_target="tpu_custom_call" | custom-call | flops 60000002048 | bytes 360000000 | tf_op jit(solution)/shard_map/ffn_backward/pallas_call | solution.py:706
  464.7 0.9 pad.53.refs_2_.refs_10_
  465.5 64.4 %out_backward.1 = (bf16[2048,256]{1,0:T(8,128)(2,1)}, bf16[2048,128]{1,0:T(8,128)(2,1)}, f32[8,2048]{1,0:T(8,128)}, bf16[48,2048]{1,0:T(8,128)(2,1)}, bf16[64,76...) custom-call(bf16[2048,256]{1,0:T(8,128)(2,1)} %get-tuple-element.113.refs_0_, ...), custom_call_target="tpu_custom_call" | custom-call | flops 30000001024 | bytes 180000000 | tf_op jit(solution)/shard_map/out_backward/pallas_call | solution.py:706
  530.0 0.8 constant_dynamic-slice_fusion
  531.0 0.8 pad.54.refs_11_.refs_9_
  531.8 31.5 %attention_backward.1 = (bf16[2048,768]{1,0:T(8,128)(2,1)}, f32[8,1,256]{2,1,0:T(1,128)}, f32[8,768]{1,0:T(8,128)}, bf16[2048,128]{1,0:T(8,128)(2,1)}) custom-call(bf16[2048,768]{1,0:T(8,128)(2,1)} %get-tuple-element.91.refs_0_, bf16[2048,256]{1,0:T(8,128)(2,1)} %get-tuple-element.94.refs_0_.refs_1_.refs_20_, bf16[2048,256]{1,0:T(8,128)(2,1)} %get-tuple-element.128.refs_2_, ...), custom_call_target="tpu_custom_call" | custom-call | flops 17500000256 | bytes 105000000 | tf_op jit(solution)/shard_map/attention_backward/pallas_call | solution.py:706
  563.3 79.9 %qkv_backward.1 = (bf16[2048,256]{1,0:T(8,128)(2,1)}, f32[112,256]{1,0:T(8,128)}, f32[80,256]{1,0:T(8,128)}, f32[64,768]{1,0:T(8,128)}) custom-call(bf16[2048,768]{1,0:T(8,128)(2,1)} %get-tuple-element.134.refs_0_, f32[8,1,256]{2,1,0:T(1,128)} %get-tuple-element.135.refs_1_, bf16[2048,896]{1,0:T(8,128)(2,1)} %get-tuple-element.136.refs_2_, ...), custom_call_target="tpu_custom_call" | custom-call | flops 35000000512 | bytes 210000000 | tf_op jit(solution)/shard_map/qkv_backward/pallas_call | solution.py:706
  643.2 3.6 last_step.1
  (68 shorter events, 10.3 us)
Async XLA Ops:
  0.6 5.4 copy-start
  2.6 4.8 copy-start.1
  2.6 5.8 copy-start.5
  2.7 6.7 %copy-start.7 = (f32[256]{0:T(256)S(1)}, f32[256]{0:T(256)}, u32[]{:S(2)}) copy-start(f32[256]{0:T(256)} %param.25) | copy-start | bytes 3076
  2.7 6.7 %copy-start.8 = (f32[256]{0:T(256)S(1)}, f32[256]{0:T(256)}, u32[]{:S(2)}) copy-start(f32[256]{0:T(256)} %param.26) | copy-start | bytes 3076
  3.6 6.5 %copy-start.2 = (f32[2,256,16]{1,2,0:T(8,128)S(1)}, f32[2,256,16]{1,2,0:T(8,128)}, u32[]{:S(2)}) copy-start(f32[2,256,16]{1,2,0:T(8,128)} %param.36) | copy-start | bytes 98308
  3.6 7.4 %copy-start.6 = (f32[256,16]{0,1:T(8,128)S(1)}, f32[256,16]{0,1:T(8,128)}, u32[]{:S(2)}) copy-start(f32[256,16]{0,1:T(8,128)} %param.32) | copy-start | bytes 49156
  4.4 7.4 %copy-start.9 = (f32[2,704]{1,0:T(2,128)S(1)}, f32[2,704]{1,0:T(2,128)}, u32[]{:S(2)}) copy-start(f32[2,704]{1,0:T(2,128)} %param.38) | copy-start | bytes 16900
  5.2 7.3 %copy-start.10 = (f32[3,256]{1,0:T(4,128)S(1)}, f32[3,256]{1,0:T(4,128)}, u32[]{:S(2)}) copy-start(f32[3,256]{1,0:T(4,128)} %param.30) | copy-start | bytes 9220
  5.2 7.3 %copy-start.11 = (f32[256]{0:T(256)S(1)}, f32[256]{0:T(256)}, u32[]{:S(2)}) copy-start(f32[256]{0:T(256)} %param.42) | copy-start | bytes 3076
  5.2 7.3 %copy-start.12 = (f32[256]{0:T(256)S(1)}, f32[256]{0:T(256)}, u32[]{:S(2)}) copy-start(f32[256]{0:T(256)} %param.34) | copy-start | bytes 3076
  289.5 94.2 %copy-start.3 = (f32[16,2048]{1,0:T(8,128)S(1)}, f32[16,2048]{1,0:T(8,128)}, u32[]{:S(2)}) copy-start(f32[16,2048]{1,0:T(8,128)} %refs_18_.1) | copy-start | bytes 393220
  384.5 80.2 %copy-start.4 = (f32[16,2048]{1,0:T(8,128)S(1)}, f32[16,2048]{1,0:T(8,128)}, u32[]{:S(2)}) copy-start(f32[16,2048]{1,0:T(8,128)} %refs_20_.1) | copy-start | bytes 393220

commit v4 on v3

--- a/solution.py
+++ b/solution.py
@@ -762,7 +762,7 @@
         xs_ref, w_ref, wo_ref, ms_ref, mgs_ref, sc_ref, sq_ref, qkv_ref, lora_ref, rate_ref, eg_ref, ed_ref, wgs_ref, out_ref, cos_ref, sin_ref, sgc_ref, sgr_ref,
         full, own, sd, rd, sc, rc, keep, xs_s, xs_r, xs_l, small_sems,
         hs, hr, ps, pr, pn, ys, yr, os, orr, ol, oys, oyr,
-        e_ref, wq, wg, wload, eo_ref, sg, place, ghs, ghr, gps, gpr, gpn, gys, gyr,
+        e_ref, wq, wg, wload, eo_ref, sg, place, aq_t, ag_t, ao_t, ghs, ghr, gps, gpr, gpn, gys, gyr,
     ):
         cm = Comm(nl, nc, tc, fw, out_by_one=0.9375)
         cm.ag_refs(xs_ref, full, own, sd, rd, sc, rc)
@@ -798,12 +798,14 @@
         swap.start(*m_swap)
         swap.start(*mg_swap)
         swap.start(*seg_swap)
+        for k in range(3):
+            aq_t[k] = aq_ref[k].T
         load_q.wait()
         gain_attn, gain_ffn = gain_ref[mine, 0:1], gain_ref[mine, 1:2]
         for gg in range(nl):
             columns = pl.ds(pl.multiple_of((cm.c * nl + gg) * fw, fw), fw)
             for k in range(3):
-                tile = merged_tile(wq[k, :, gg * fw : (gg + 1) * fw], aq_ref[k, mine, :], bq_ref[k, :, columns])
+                tile = merged_tile(wq[k, :, gg * fw : (gg + 1) * fw], aq_t[k, mine, :], bq_ref[k, :, columns])
                 e_ref[gg, :, k * fw : (k + 1) * fw] = (tile * gain_attn).astype(BF16)
             e_ref[gg, :, width:] = tq_ref[mine, :]
         weights.start(range(nl))
@@ -815,7 +817,7 @@
                 raw = wg[k, :, gg * nf - off : gg * nf - off + window].astype(F32)
                 if off:
                     raw = pltpu.roll(raw, window - off, 1)
-                tile = merged_tile(raw[:, :npad], ag_ref[k, mine, :], bg_ref[k, cm.c * nl + gg]) * gain_ffn
+                tile = merged_tile(raw[:, :npad], ag_t[k, mine, :], bg_ref[k, cm.c * nl + gg]) * gain_ffn
                 lane = lax.broadcasted_iota(jnp.int32, tile.shape, 1)
                 eg_ref[gg, :, k * npad : (k + 1) * npad] = jnp.where(
                     lane < nf, tile, tg_ref[k, mine, :].astype(F32)
@@ -828,10 +830,10 @@
                 ed_ref[:nf, d:] = jnp.zeros((nf, LANES), BF16)
                 ed_ref[:nf, d : d + RANK] = ad_ref[...].astype(BF16)
                 eo_ref[:, d:] = jnp.zeros((fw, LANES), BF16)
-                eo_ref[:, d : d + RANK] = ao_ref[...].astype(BF16)
+                eo_ref[:, d : d + RANK] = ao_t[...].astype(BF16)
             for n in (2 * k, 2 * k + 1):
                 at = slice(n * fw, (n + 1) * fw)
-                eo_ref[:, at] = merged_tile(wout_ref[:, at], ao_ref[...], bo_ref[:, at]).astype(BF16)
+                eo_ref[:, at] = merged_tile(wout_ref[:, at], ao_t[...], bo_ref[:, at]).astype(BF16)
                 ed_ref[:nf, at] = merged_tile(wdown_ref[:, at], ad_ref[...], bd_ref[:, at]).astype(BF16)
 
         def gather(i, carry_on):
@@ -857,6 +859,9 @@
             weights.pass_own(m, cross=False)
         load_g.wait()
         io.ready()
+        for k in range(2):
+            ag_t[k] = ag_ref[k].T
+        ao_t[...] = ao_ref[...].T
         for m in range(nl):
             lax.fori_loop(nc * m // nl, nc * (m + 1) // nl, forward, 0)
             gate_up(m)
@@ -1014,6 +1019,9 @@
             pltpu.VMEM((fw, d + LANES), BF16),
             pltpu.VMEM((1, t), jnp.int32),
             pltpu.VMEM((8, t), jnp.int32),
+            pltpu.VMEM((3, fw, RANK), F32),
+            pltpu.VMEM((2, fw, RANK), F32),
+            pltpu.VMEM((fw, RANK), F32),
         ]
         + spread_scratch(ny, nl),
         1,
@@ -1221,7 +1229,7 @@
 
     def kernel(
         io, u_ref, st_ref, wg_ref, mg_ref, wd_ref, m_ref, mid_ref, cin_ref,
-        gu_ref, hid_ref, out_ref, gm_ref, rate_ref, gp_ref, sg_ref, qg_ref, sd_ref, qd_ref, lora_ref, cot_ref, uf_ref,
+        gu_ref, hid_ref, out_ref, gm_ref, rate_ref, gp_ref, sg_ref, qg_ref, sd_ref, qd_ref, lora_ref, cot_ref, am_ref, ad_ref, uf_ref,
         full, own, sd, rd, sc, rc, sb, cb, gb, s1, r1, s2, r2, sa, ss, sr, cpart, cheld, css, csr, keep,
         cs_s, cs_r, cs_l,
     ):
@@ -1296,6 +1304,17 @@
                 cm.rs_across(i).start()
                 lora_ref[rows, :] = nn(hidden, wd_ref[:, d:]).astype(BF16)
                 io.store(i, 0, 1, 4, 10)
+
+            @pl.when(i == nc)
+            def _():
+                off = nf - (npad - LANES)
+                for k in range(2):
+                    tail = wg_ref[:, (k + 1) * npad - LANES : (k + 1) * npad]
+                    _, gain = gain_rows(tail, off + RANK)
+                    factor = (tail.astype(F32) / (gain * gain)).astype(BF16)
+                    product = tn(factor, wg_ref[:, k * npad : (k + 1) * npad])
+                    am_ref[k * RANK : (k + 1) * RANK, :] = product[off : off + RANK, :]
+                ad_ref[...] = tn(wd_ref[:, d:], wd_ref[:, :d])[:RANK, :]
 
             cm.rs_steps(i)
 
@@ -1349,10 +1368,12 @@
             shape((8, fw), F32),
             shape((t, LANES), BF16),
             shape((t, fw), BF16),
+            shape((2 * RANK, npad), F32),
+            shape((RANK, d), F32),
             shape((t, d), BF16),
         ),
         [VM] * 8,
-        (VM,) * 12 + (ANY,),
+        (VM,) * 14 + (ANY,),
         ag_scratch(nl, nc, t, d)
         + rs_scratch(nl, nc, tc, fw)
         + st_scratch(nl, nc, t)
@@ -1543,18 +1564,18 @@
 
 
 def out_backward(
-    cfg, npad, nf, go, weights, b_out, ratios, w_gu, w_down, up_gu, b_down, gm_gu, square_gu, m_gu,
-    u_full, lg_gu, gu, dp_gu, hidden, lg_down, lora_down, gp_full, result,
+    cfg, npad, nf, go, weights, b_out, sums, w_gu, w_down, up_gu, b_down, gm_gu, square_gu, m_gu,
+    u_full, lg_gu, gu, dp_gu, hidden, lg_down, lora_down, gp_full, result, merged_low_gu, merged_low_down,
 ):
     t, fw, d, nl, nc, tc = cfg
     off = nf - (npad - LANES)
     widths = (d, LANES, LANES, LANES, 2 * npad, npad, LANES, LANES, d)
 
     def kernel(
-        io, go_ref, w_ref, b_ref, q_ref, wg_ref, wd_ref, up_ref, bd_ref, gm_ref, sq_ref, m_ref,
-        uf_hbm, lg_hbm, gu_hbm, dp_hbm, hid_hbm, ld_hbm, lo2_hbm, gp_hbm, res_hbm,
+        io, go_ref, w_ref, b_ref, s1_ref, s2_ref, s3_ref, s4_ref, wg_ref, wd_ref, up_ref, bd_ref, gm_ref, sq_ref, m_ref,
+        uf_hbm, lg_hbm, gu_hbm, dp_hbm, hid_hbm, ld_hbm, lo2_hbm, gp_hbm, res_hbm, am_ref, amd_ref,
         da_ref, lo_ref, qs_ref, sh_ref, lc_ref, gf_ref, moved_ref,
-        full, own, sd, rd, sc, rc, keep, qss, qsr, res_sems, acc_a, acc_g, acc_u, acc_d, acc_p, *streams,
+        full, own, sd, rd, sc, rc, keep, qss, qsr, res_sems, acc_a, acc_g, acc_u, acc_d, acc_p, term, term_d, q_ref, *streams,
     ):
         cm = Comm(nl, nc, tc, fw, out_by_one=0.75)
         swap = Swap(cm)
@@ -1587,14 +1608,19 @@
             )
 
         cm.ag_start()
+        q_ref[...] = jnp.zeros_like(q_ref)
+        q_ref[0:1, :] = -s1_ref[0:1, :] / s2_ref[0:1, :]
+        q_ref[1:2, :] = -s3_ref[0:1, :] / s4_ref[0:1, :]
         for o, m in cm.st_peers():
             ratio_copy(o, m).start()
         qs_ref[:, cm.columns(cm.c, cm.g)] = q_ref[...]
         swap.start(*result_swap)
         for acc in (acc_a, acc_g, acc_u, acc_d, acc_p):
             acc[...] = jnp.zeros_like(acc)
+        io.ready()
+        ratio = -gm_ref[0:1, :] / sq_ref[0:1, :]
+        term[...] = nt((up_ref[...] * ratio).astype(BF16), wg_ref[...])[: 2 * RANK, :]
         cm.ag_ahead()
-        io.ready()
 
         def stored(i):
             rows = cm.rows(i)
@@ -1602,6 +1628,12 @@
 
         def body(i, carry_on):
             cm.ag_step(i + 2)
+
+            @pl.when(i == min(2, nc - 1))
+            def _():
+                for o, m in cm.st_peers():
+                    ratio_copy(o, m).wait_recv()
+                term_d[...] = nt((bd_ref[...].astype(F32) * qs_ref[1:2, :]).astype(BF16), wd_ref[:, :d])[:RANK, :]
 
             @pl.when(i + 1 < nc)
             def _():
@@ -1623,33 +1655,17 @@
 
         lax.fori_loop(0, nc, body, 0)
 
-        ratio = -gm_ref[0:1, :] / sq_ref[0:1, :]
-        term = nt((up_ref[...] * ratio).astype(BF16), wg_ref[...])
-        tail_g, tail_u = wg_ref[:, npad - LANES : npad], wg_ref[:, 2 * npad - LANES :]
-        gain_row, gain_column = gain_rows(tail_g, off + RANK)
-        inverse = 1.0 / (gain_column * gain_column)
-        sh_ref[: 2 * RANK, :] = (
-            SCALE * (acc_a[: 2 * RANK, :] * gain_row + term[: 2 * RANK, :] / gain_row)
-        ).astype(BF16)
-        for k, (acc, tail) in enumerate(((acc_g, tail_g), (acc_u, tail_u))):
-            at = slice(k * npad, (k + 1) * npad)
-            merged = tn((tail.astype(F32) * inverse).astype(BF16), wg_ref[:, at])
+        gain_row, _ = gain_rows(wg_ref[:, npad - LANES : npad], off + RANK)
+        sh_ref[: 2 * RANK, :] = (SCALE * (acc_a[: 2 * RANK, :] * gain_row + term[...] / gain_row)).astype(BF16)
+        for k, acc in enumerate((acc_g, acc_u)):
+            at, low = slice(k * npad, (k + 1) * npad), slice(k * RANK, (k + 1) * RANK)
             lc_ref[(1 + k) * RANK : (2 + k) * RANK, :] = (
-                SCALE * (acc[off : off + RANK, :] + merged[off : off + RANK, :] * ratio[:, at])
+                SCALE * (acc[off : off + RANK, :] + am_ref[low, :] * ratio[:, at])
             ).astype(BF16)
             lc_ref[3 * RANK + k : 3 * RANK + k + 1, :] = (gm_ref[0:1, at] / m_ref[0:1, at]).astype(BF16)
         lc_ref[3 * RANK + 2 :, :] = jnp.zeros((RANK - 2, npad), BF16)
-
-        for o, m in cm.st_peers():
-            ratio_copy(o, m).wait_recv()
-        ratio_down = qs_ref[1:2, :]
-        lc_ref[:RANK, :] = (
-            SCALE
-            * (acc_d[:RANK, :] + nt((bd_ref[...].astype(F32) * ratio_down).astype(BF16), wd_ref[:, :d])[:RANK, :])
-        ).astype(BF16)
-        sh_ref[2 * RANK :, :] = (
-            SCALE * (acc_p[:RANK, :] + tn(wd_ref[:, d:], wd_ref[:, :d])[:RANK, :] * ratio_down)
-        ).astype(BF16)
+        lc_ref[:RANK, :] = (SCALE * (acc_d[:RANK, :] + term_d[...])).astype(BF16)
+        sh_ref[2 * RANK :, :] = (SCALE * (acc_p[:RANK, :] + amd_ref[...] * qs_ref[1:2, :])).astype(BF16)
 
         def drain(i, carry_on):
             cm.ag_drain(i)
@@ -1675,19 +1691,20 @@
             shape((t, d), BF16),
             shape((t, fw), BF16),
         ),
-        [VM] * 11 + [ANY] * 9,
+        [VM] * 14 + [ANY] * 9 + [VM] * 2,
         (VM,) * 5 + (ANY, ANY),
         ag_scratch(nl, nc, t, d)
         + [dma((nc,)), dma((2 * nl,)), dma((2 * nl,)), dma((3,))]
         + [pltpu.VMEM((LANES, n), F32) for n in (d, npad, npad, npad, d)]
+        + [pltpu.VMEM((2 * RANK, d), F32), pltpu.VMEM((RANK, npad), F32), pltpu.VMEM((8, fw), F32)]
         + stream_scratch(tc, widths),
         5,
         60,
         (
-            go, weights, b_out, ratios, w_gu, w_down, up_gu, b_down, gm_gu, square_gu, m_gu,
-            u_full, lg_gu, gu, dp_gu, hidden, lg_down, lora_down, gp_full, result,
+            go, weights, b_out, *sums, w_gu, w_down, up_gu, b_down, gm_gu, square_gu, m_gu,
+            u_full, lg_gu, gu, dp_gu, hidden, lg_down, lora_down, gp_full, result, merged_low_gu, merged_low_down,
         ),
-        late=(1, 2, 4, 5, 6, 7),
+        late=(1, 2, 7, 8, 9, 10),
     )
 
 
@@ -2185,8 +2202,8 @@
         x, weights_qkv, weights_out, small, small_gu, scale_qkv, square_qkv, qkv, lora_qkv_in, rate_attn,
         blocks_gu, rows_down, weights_gu, x_full, cosine, sine, seg_column, seg_row,
     ) = qkv_forward(
-        cfg, ny, npad, nf, inputs, w_qkv, a_qkv, b_qkv, tail_qkv, gains, w_out, small, small_gu, segments,
-        turn_constants(), w_gu, a_gu, b_gu_padded, tail_gu, w_down, a_down, b_down, a_out, b_out,
+        cfg, ny, npad, nf, inputs, w_qkv, a_qkv.transpose(0, 2, 1), b_qkv, tail_qkv, gains, w_out, small, small_gu, segments,
+        turn_constants(), w_gu, a_gu.transpose(0, 2, 1), b_gu_padded, tail_gu, w_down, a_down, b_down, a_out.T, b_out,
     )
     first_number = seg_row[0, ::block]
     first_block = jnp.sum((seg_row[0][None, :] < first_number[:, None]).astype(jnp.int32), axis=1) // block
@@ -2196,7 +2213,7 @@
     )
     (
         gu, hidden, block_out, gm_down, rate_ffn, gp, scale_gu, square_gu, sc_down, square_down,
-        lora_down, grad_seed, u_full,
+        lora_down, grad_seed, merged_low_gu, merged_low_down, u_full,
     ) = ffn_forward(
         cfg, npad, nf, u, stats, weights_gu, small_gu[0:1], weights_down, small, middle, cotangent
     )
@@ -2205,12 +2222,10 @@
         cfg, npad, gp, gu, weights_gu, scale_gu, up_gu, weights_down, up_down, rate_ffn,
         grad_seed, middle, x, sc_out,
     )
-    ratios = jnp.concatenate(
-        [-gm_out[0:1] / square_out[0:1], -gm_down[0:1] / square_down[0:1], jnp.zeros((6, fw), F32)], axis=0
-    )
     grad_attended, lg_out, ratios, shared, local_gu, go_full, block_out = out_backward(
-        cfg, npad, nf, go, weights_out, up_out, ratios, weights_gu, weights_down, up_gu, up_down, gm_gu, square_gu,
+        cfg, npad, nf, go, weights_out, up_out, (gm_out, square_out, gm_down, square_down), weights_gu, weights_down, up_gu, up_down, gm_gu, square_gu,
         small_gu, u_full, lg_gu, gu, dp_gu, hidden, lg_down, lora_down, gp_full, block_out,
+        merged_low_gu, merged_low_down,
     )
     dp_qkv, inner, gm_qkv, lg_qkv = attention_backward(
         cfg, qkv, attended, grad_attended, lse, seg_column, seg_row, first_block, block, cosine, sine,

time: 648 us -> 652 us (level); the launches traced: 647 us -> 643 us
  no operation moved by 1% of the time
where the time goes in v4:
time: 652 us; the launch traced here: 643 us
  Pallas kernels  622 us (95%)
  local copies, waits for them, and re-layouts  13.6 us (2%)
    pallas_call x9, Pallas kernels, call(): pl.pallas_call(whole, name=name, out_shape=outs, in_specs=in_specs, out_s...  622 us

profile of v4, /device:TPU:1, one launch (start us, length us, event | category | flops | bytes accessed | tf_op | source)
XLA Modules:
  0.0 642.9 jit_solution(5187044955504395898)
XLA Ops:
  0.7 0.8 fusion.1
  2.7 0.9 pad_maximum_fusion.refs_15_
  3.6 0.8 fusion.2
  4.4 0.8 subtract_convert_fusion.1
  6.5 0.9 pad_bitcast_fusion.refs_14_
  7.5 0.9 copy.70.refs_17_
  10.6 125.7 %qkv_forward.1 = (bf16[2048,256]{1,0:T(8,128)(2,1)}, bf16[2048,896]{1,0:T(8,128)(2,1)}, bf16[256,2176]{1,0:T(8,128)(2,1)}, f32[8,256]{1,0:T(8,128)}, f32[8,1536]...) custom-call(bf16[2048,256]{1,0:T(8,128)(2,1)} %refs_0_.1, ...), custom_call_target="tpu_custom_call" | custom-call | flops 44999999488 | bytes 270000000 | tf_op jit(solution)/shard_map/qkv_forward/pallas_call | solution.py:706
  136.3 0.8 slice.29
  137.2 0.9 slice.30
  138.8 20.0 %attention_forward.1 = (bf16[2048,256]{1,0:T(8,128)(2,1)}, f32[16,2048]{1,0:T(8,128)}) custom-call(bf16[2048,768]{1,0:T(8,128)(2,1)} %get-tuple-element.93.refs_0_, s32[2048,128]{1,0:T(8,128)} %get-tuple-element.94.refs_1_.refs_4_, s32[8,2048]{1,0:T(8,128)} %get-tuple-element.95.refs_2_.refs_5_, s32[8]{0:T(128)} %and_select_fusion.refs_3_.refs_6_), custom_call_target="tpu_custom_call" | custom-call | flops 7500000256 | bytes 45000000 | tf_op jit(solution)/shard_map/attention_forward/pallas_call | solution.py:706
  158.8 128.7 %out_forward.1 = (f32[2048,256]{1,0:T(8,128)}, bf16[2048,256]{1,0:T(8,128)(2,1)}, f32[8,1,256]{2,1,0:T(1,128)}, f32[8,256]{1,0:T(8,128)}, f32[8,256]{1,0:T(8,128...) custom-call(bf16[2048,256]{1,0:T(8,128)(2,1)} %get-tuple-element.96., ...), custom_call_target="tpu_custom_call", output_to_operand_aliasing={{6}: (4, {})} | custom-call | flops 44999999488 | bytes 270000000 | tf_op jit(solution)/shard_map/out_forward/pallas_call | solution.py:706
  287.5 1.4 slice.31.refs_3_
  288.9 94.1 %ffn_forward.1 = (bf16[2048,1536]{1,0:T(8,128)(2,1)}, bf16[2048,768]{1,0:T(8,128)(2,1)}, bf16[2048,256]{1,0:T(8,128)(2,1)}, f32[8,256]{1,0:T(8,128)}, f32[2048,1...) custom-call(bf16[2048,256]{1,0:T(8,128)(2,1)} %get-tuple-element.103, ...), custom_call_target="tpu_custom_call" | custom-call | flops 54999998464 | bytes 330000000 | tf_op jit(solution)/shard_map/ffn_forward/pallas_call | solution.py:706
  383.0 1.0 constant_dynamic-slice_fusion.1
  384.2 1.0 pad.51.refs_4_.refs_9_
  385.2 0.8 pad.52.refs_6_.refs_10_
  386.0 78.0 %ffn_backward.1 = (f32[2048,256]{1,0:T(8,128)}, bf16[2048,256]{1,0:T(8,128)(2,1)}, f32[8,256]{1,0:T(8,128)}, f32[8,1536]{1,0:T(8,128)}, bf16[2048,128]{1,0:T(8,1...) custom-call(bf16[2048,256]{1,0:T(8,128)(2,1)} %get-tuple-element.109.refs_0_, ...), custom_call_target="tpu_custom_call" | custom-call | flops 60000002048 | bytes 360000000 | tf_op jit(solution)/shard_map/ffn_backward/pallas_call | solution.py:706
  464.1 0.9 pad.53.refs_2_.refs_10_
  465.0 59.8 %out_backward.1 = (bf16[2048,256]{1,0:T(8,128)(2,1)}, bf16[2048,128]{1,0:T(8,128)(2,1)}, f32[8,2048]{1,0:T(8,128)}, bf16[48,2048]{1,0:T(8,128)(2,1)}, bf16[64,76...) custom-call(bf16[2048,256]{1,0:T(8,128)(2,1)} %get-tuple-element.115.refs_0_, ...), custom_call_target="tpu_custom_call" | custom-call | flops 30000001024 | bytes 180000000 | tf_op jit(solution)/shard_map/out_backward/pallas_call | solution.py:706
  524.8 0.8 constant_dynamic-slice_fusion
  525.8 0.8 pad.54.refs_11_.refs_9_
  526.6 30.7 %attention_backward.1 = (bf16[2048,768]{1,0:T(8,128)(2,1)}, f32[8,1,256]{2,1,0:T(1,128)}, f32[8,768]{1,0:T(8,128)}, bf16[2048,128]{1,0:T(8,128)(2,1)}) custom-call(bf16[2048,768]{1,0:T(8,128)(2,1)} %get-tuple-element.93.refs_0_, bf16[2048,256]{1,0:T(8,128)(2,1)} %get-tuple-element.96.refs_0_.refs_1_.refs_20_, bf16[2048,256]{1,0:T(8,128)(2,1)} %get-tuple-element.132.refs_2_, ...), custom_call_target="tpu_custom_call" | custom-call | flops 17500000256 | bytes 105000000 | tf_op jit(solution)/shard_map/attention_backward/pallas_call | solution.py:706
  557.3 81.5 %qkv_backward.1 = (bf16[2048,256]{1,0:T(8,128)(2,1)}, f32[112,256]{1,0:T(8,128)}, f32[80,256]{1,0:T(8,128)}, f32[64,768]{1,0:T(8,128)}) custom-call(bf16[2048,768]{1,0:T(8,128)(2,1)} %get-tuple-element.138.refs_0_, f32[8,1,256]{2,1,0:T(1,128)} %get-tuple-element.139.refs_1_, bf16[2048,896]{1,0:T(8,128)(2,1)} %get-tuple-element.140.refs_2_, ...), custom_call_target="tpu_custom_call" | custom-call | flops 35000000512 | bytes 210000000 | tf_op jit(solution)/shard_map/qkv_backward/pallas_call | solution.py:706
  638.8 3.6 last_step.1
  (54 shorter events, 5.8 us)
Async XLA Ops:
  0.6 5.4 copy-start
  2.6 4.8 copy-start.3
  2.6 5.7 copy-start.4
  2.7 5.7 copy-start.5
  2.7 6.5 %copy-start.6 = (f32[2,704]{1,0:T(2,128)S(1)}, f32[2,704]{1,0:T(2,128)}, u32[]{:S(2)}) copy-start(f32[2,704]{1,0:T(2,128)} %param.38) | copy-start | bytes 16900
  3.6 6.3 copy-start.7
  3.6 6.3 copy-start.8
  3.6 6.3 copy-start.9
  288.9 96.2 %copy-start.1 = (f32[16,2048]{1,0:T(8,128)S(1)}, f32[16,2048]{1,0:T(8,128)}, u32[]{:S(2)}) copy-start(f32[16,2048]{1,0:T(8,128)} %refs_18_.1) | copy-start | bytes 393220
  386.0 78.1 %copy-start.2 = (f32[16,2048]{1,0:T(8,128)S(1)}, f32[16,2048]{1,0:T(8,128)}, u32[]{:S(2)}) copy-start(f32[16,2048]{1,0:T(8,128)} %refs_20_.1) | copy-start | bytes 393220

commit v5 on v4

--- a/solution.py
+++ b/solution.py
@@ -1154,16 +1154,20 @@
 
             @pl.when(i == 1)
             def _():
-                columns.pass_own(EARLY + 1)
+                columns.pass_own(EARLY + 1, cross=False)
 
             @pl.when(i == 3)
             def _():
                 for m in range(EARLY + 2, nl):
                     columns.pass_own(m, cross=False)
 
-            @pl.when(i == min(6, nc + 2))
-            def _():
-                columns.pass_crossed(EARLY, EARLY + 2)
+            @pl.when(i == min(4, nc + 2))
+            def _():
+                columns.pass_crossed(EARLY, EARLY + 1)
+
+            @pl.when(i == min(7, nc + 2))
+            def _():
+                columns.pass_crossed(EARLY + 1, EARLY + 2)
 
             @pl.when((i >= 3) & (i <= nc + 2))
             def _():
@@ -1183,8 +1187,8 @@
             io.stored(i)
             return carry_on
 
-        for m in range(EARLY + 1, nl):
-            columns.pass_crossed(m, m + 2)
+        for m in range(EARLY + 2, nl):
+            columns.pass_crossed(m, m + 1)
         for side in (0, 1):
             columns.wait(side, range(nl))
         down_rows.wait()

time: 652 us -> 632 us (0.969)
  Pallas kernels: 622 us -> 604 us
    pallas_call x9, Pallas kernels: 622 us -> 604 us  [call(): pl.pallas_call(whole, name=name, out_shape=outs, in_specs=in_specs, out_s...]
where the time goes in v5:
time: 632 us; the launch traced here: 624 us
  Pallas kernels  604 us (96%)
  local copies, waits for them, and re-layouts  13.6 us (2%)
    pallas_call x9, Pallas kernels, call(): pl.pallas_call(whole, name=name, out_shape=outs, in_specs=in_specs, out_s...  604 us

profile of v5, /device:TPU:1, one launch (start us, length us, event | category | flops | bytes accessed | tf_op | source)
XLA Modules:
  0.0 624.4 jit_solution(3988050011189031424)
XLA Ops:
  0.7 0.8 fusion.1
  1.5 0.8 subtract_convert_fusion
  2.7 0.9 pad_maximum_fusion.refs_15_
  3.6 0.8 fusion.2
  6.5 0.9 pad_bitcast_fusion.refs_14_
  7.5 0.9 copy.70.refs_17_
  10.6 125.7 %qkv_forward.1 = (bf16[2048,256]{1,0:T(8,128)(2,1)}, bf16[2048,896]{1,0:T(8,128)(2,1)}, bf16[256,2176]{1,0:T(8,128)(2,1)}, f32[8,256]{1,0:T(8,128)}, f32[8,1536]...) custom-call(bf16[2048,256]{1,0:T(8,128)(2,1)} %refs_0_.1, ...), custom_call_target="tpu_custom_call" | custom-call | flops 44999999488 | bytes 270000000 | tf_op jit(solution)/shard_map/qkv_forward/pallas_call | solution.py:706
  136.3 0.8 slice.29
  137.2 0.9 slice.30
  138.8 20.0 %attention_forward.1 = (bf16[2048,256]{1,0:T(8,128)(2,1)}, f32[16,2048]{1,0:T(8,128)}) custom-call(bf16[2048,768]{1,0:T(8,128)(2,1)} %get-tuple-element.93.refs_0_, s32[2048,128]{1,0:T(8,128)} %get-tuple-element.94.refs_1_.refs_4_, s32[8,2048]{1,0:T(8,128)} %get-tuple-element.95.refs_2_.refs_5_, s32[8]{0:T(128)} %and_select_fusion.refs_3_.refs_6_), custom_call_target="tpu_custom_call" | custom-call | flops 7500000256 | bytes 45000000 | tf_op jit(solution)/shard_map/attention_forward/pallas_call | solution.py:706
  158.8 110.8 %out_forward.1 = (f32[2048,256]{1,0:T(8,128)}, bf16[2048,256]{1,0:T(8,128)(2,1)}, f32[8,1,256]{2,1,0:T(1,128)}, f32[8,256]{1,0:T(8,128)}, f32[8,256]{1,0:T(8,128...) custom-call(bf16[2048,256]{1,0:T(8,128)(2,1)} %get-tuple-element.96., ...), custom_call_target="tpu_custom_call", output_to_operand_aliasing={{6}: (4, {})} | custom-call | flops 44999999488 | bytes 270000000 | tf_op jit(solution)/shard_map/out_forward/pallas_call | solution.py:706
  269.6 1.4 slice.31.refs_3_
  271.0 92.6 %ffn_forward.1 = (bf16[2048,1536]{1,0:T(8,128)(2,1)}, bf16[2048,768]{1,0:T(8,128)(2,1)}, bf16[2048,256]{1,0:T(8,128)(2,1)}, f32[8,256]{1,0:T(8,128)}, f32[2048,1...) custom-call(bf16[2048,256]{1,0:T(8,128)(2,1)} %get-tuple-element.103, ...), custom_call_target="tpu_custom_call" | custom-call | flops 54999998464 | bytes 330000000 | tf_op jit(solution)/shard_map/ffn_forward/pallas_call | solution.py:706
  363.7 1.0 constant_dynamic-slice_fusion.1
  364.9 1.0 pad.51.refs_4_.refs_9_
  365.8 0.8 pad.52.refs_6_.refs_10_
  366.7 77.9 %ffn_backward.1 = (f32[2048,256]{1,0:T(8,128)}, bf16[2048,256]{1,0:T(8,128)(2,1)}, f32[8,256]{1,0:T(8,128)}, f32[8,1536]{1,0:T(8,128)}, bf16[2048,128]{1,0:T(8,1...) custom-call(bf16[2048,256]{1,0:T(8,128)(2,1)} %get-tuple-element.109.refs_0_, ...), custom_call_target="tpu_custom_call" | custom-call | flops 60000002048 | bytes 360000000 | tf_op jit(solution)/shard_map/ffn_backward/pallas_call | solution.py:706
  444.6 0.9 pad.53.refs_2_.refs_10_
  445.5 61.3 %out_backward.1 = (bf16[2048,256]{1,0:T(8,128)(2,1)}, bf16[2048,128]{1,0:T(8,128)(2,1)}, f32[8,2048]{1,0:T(8,128)}, bf16[48,2048]{1,0:T(8,128)(2,1)}, bf16[64,76...) custom-call(bf16[2048,256]{1,0:T(8,128)(2,1)} %get-tuple-element.115.refs_0_, ...), custom_call_target="tpu_custom_call" | custom-call | flops 30000001024 | bytes 180000000 | tf_op jit(solution)/shard_map/out_backward/pallas_call | solution.py:706
  506.8 0.8 constant_dynamic-slice_fusion
  507.8 0.8 pad.54.refs_11_.refs_9_
  508.6 30.7 %attention_backward.1 = (bf16[2048,768]{1,0:T(8,128)(2,1)}, f32[8,1,256]{2,1,0:T(1,128)}, f32[8,768]{1,0:T(8,128)}, bf16[2048,128]{1,0:T(8,128)(2,1)}) custom-call(bf16[2048,768]{1,0:T(8,128)(2,1)} %get-tuple-element.93.refs_0_, bf16[2048,256]{1,0:T(8,128)(2,1)} %get-tuple-element.96.refs_0_.refs_1_.refs_20_, bf16[2048,256]{1,0:T(8,128)(2,1)} %get-tuple-element.132.refs_2_, ...), custom_call_target="tpu_custom_call" | custom-call | flops 17500000256 | bytes 105000000 | tf_op jit(solution)/shard_map/attention_backward/pallas_call | solution.py:706
  539.3 81.0 %qkv_backward.1 = (bf16[2048,256]{1,0:T(8,128)(2,1)}, f32[112,256]{1,0:T(8,128)}, f32[80,256]{1,0:T(8,128)}, f32[64,768]{1,0:T(8,128)}) custom-call(bf16[2048,768]{1,0:T(8,128)(2,1)} %get-tuple-element.138.refs_0_, f32[8,1,256]{2,1,0:T(1,128)} %get-tuple-element.139.refs_1_, bf16[2048,896]{1,0:T(8,128)(2,1)} %get-tuple-element.140.refs_2_, ...), custom_call_target="tpu_custom_call" | custom-call | flops 35000000512 | bytes 210000000 | tf_op jit(solution)/shard_map/qkv_backward/pallas_call | solution.py:706
  620.4 3.6 last_step.1
  (54 shorter events, 5.8 us)
Async XLA Ops:
  0.6 5.4 copy-start
  2.6 4.8 copy-start.3
  2.6 5.7 copy-start.4
  2.7 5.7 copy-start.5
  2.7 6.5 %copy-start.6 = (f32[2,704]{1,0:T(2,128)S(1)}, f32[2,704]{1,0:T(2,128)}, u32[]{:S(2)}) copy-start(f32[2,704]{1,0:T(2,128)} %param.38) | copy-start | bytes 16900
  3.6 6.3 %copy-start.7 = (f32[3,256]{1,0:T(4,128)S(1)}, f32[3,256]{1,0:T(4,128)}, u32[]{:S(2)}) copy-start(f32[3,256]{1,0:T(4,128)} %param.30) | copy-start | bytes 9220
  3.6 6.3 %copy-start.8 = (f32[256]{0:T(256)S(1)}, f32[256]{0:T(256)}, u32[]{:S(2)}) copy-start(f32[256]{0:T(256)} %param.42) | copy-start | bytes 3076
  3.6 6.3 %copy-start.9 = (f32[256]{0:T(256)S(1)}, f32[256]{0:T(256)}, u32[]{:S(2)}) copy-start(f32[256]{0:T(256)} %param.34) | copy-start | bytes 3076
  271.0 94.8 %copy-start.1 = (f32[16,2048]{1,0:T(8,128)S(1)}, f32[16,2048]{1,0:T(8,128)}, u32[]{:S(2)}) copy-start(f32[16,2048]{1,0:T(8,128)} %refs_18_.1) | copy-start | bytes 393220
  366.7 77.9 %copy-start.2 = (f32[16,2048]{1,0:T(8,128)S(1)}, f32[16,2048]{1,0:T(8,128)}, u32[]{:S(2)}) copy-start(f32[16,2048]{1,0:T(8,128)} %refs_20_.1) | copy-start | bytes 393220

commit v6 on v5

--- a/solution.py
+++ b/solution.py
@@ -39,7 +39,7 @@
     )
 
 
-WINDOW = 3
+WINDOW = 2
 EARLY = 1
 
 

time: 632 us -> 634 us (level)
  no operation moved by 1% of the time
where the time goes in v6:
time: 634 us; the launch traced here: 624 us
  Pallas kernels  603 us (95%)
  local copies, waits for them, and re-layouts  13.6 us (2%)
    pallas_call x9, Pallas kernels, call(): pl.pallas_call(whole, name=name, out_shape=outs, in_specs=in_specs, out_s...  603 us

profile of v6, /device:TPU:1, one launch (start us, length us, event | category | flops | bytes accessed | tf_op | source)
XLA Modules:
  0.0 624.0 jit_solution(8164758333188586226)
XLA Ops:
  0.7 0.8 fusion.1
  1.5 0.8 subtract_convert_fusion
  2.7 0.9 pad_maximum_fusion.refs_15_
  3.6 0.8 fusion.2
  6.5 0.9 pad_bitcast_fusion.refs_14_
  7.5 0.9 copy.70.refs_17_
  10.6 125.2 %qkv_forward.1 = (bf16[2048,256]{1,0:T(8,128)(2,1)}, bf16[2048,896]{1,0:T(8,128)(2,1)}, bf16[256,2176]{1,0:T(8,128)(2,1)}, f32[8,256]{1,0:T(8,128)}, f32[8,1536]...) custom-call(bf16[2048,256]{1,0:T(8,128)(2,1)} %refs_0_.1, ...), custom_call_target="tpu_custom_call" | custom-call | flops 44999999488 | bytes 270000000 | tf_op jit(solution)/shard_map/qkv_forward/pallas_call | solution.py:706
  135.8 0.8 slice.29
  136.7 0.9 slice.30
  138.3 20.0 %attention_forward.1 = (bf16[2048,256]{1,0:T(8,128)(2,1)}, f32[16,2048]{1,0:T(8,128)}) custom-call(bf16[2048,768]{1,0:T(8,128)(2,1)} %get-tuple-element.93.refs_0_, s32[2048,128]{1,0:T(8,128)} %get-tuple-element.94.refs_1_.refs_4_, s32[8,2048]{1,0:T(8,128)} %get-tuple-element.95.refs_2_.refs_5_, s32[8]{0:T(128)} %and_select_fusion.refs_3_.refs_6_), custom_call_target="tpu_custom_call" | custom-call | flops 7500000256 | bytes 45000000 | tf_op jit(solution)/shard_map/attention_forward/pallas_call | solution.py:706
  158.4 111.2 %out_forward.1 = (f32[2048,256]{1,0:T(8,128)}, bf16[2048,256]{1,0:T(8,128)(2,1)}, f32[8,1,256]{2,1,0:T(1,128)}, f32[8,256]{1,0:T(8,128)}, f32[8,256]{1,0:T(8,128...) custom-call(bf16[2048,256]{1,0:T(8,128)(2,1)} %get-tuple-element.96., ...), custom_call_target="tpu_custom_call", output_to_operand_aliasing={{6}: (4, {})} | custom-call | flops 44999999488 | bytes 270000000 | tf_op jit(solution)/shard_map/out_forward/pallas_call | solution.py:706
  269.5 1.4 slice.31.refs_3_
  270.9 92.5 %ffn_forward.1 = (bf16[2048,1536]{1,0:T(8,128)(2,1)}, bf16[2048,768]{1,0:T(8,128)(2,1)}, bf16[2048,256]{1,0:T(8,128)(2,1)}, f32[8,256]{1,0:T(8,128)}, f32[2048,1...) custom-call(bf16[2048,256]{1,0:T(8,128)(2,1)} %get-tuple-element.103, ...), custom_call_target="tpu_custom_call" | custom-call | flops 54999998464 | bytes 330000000 | tf_op jit(solution)/shard_map/ffn_forward/pallas_call | solution.py:706
  363.5 1.0 constant_dynamic-slice_fusion.1
  364.7 1.0 pad.51.refs_4_.refs_9_
  365.6 0.8 pad.52.refs_6_.refs_10_
  366.5 78.8 %ffn_backward.1 = (f32[2048,256]{1,0:T(8,128)}, bf16[2048,256]{1,0:T(8,128)(2,1)}, f32[8,256]{1,0:T(8,128)}, f32[8,1536]{1,0:T(8,128)}, bf16[2048,128]{1,0:T(8,1...) custom-call(bf16[2048,256]{1,0:T(8,128)(2,1)} %get-tuple-element.109.refs_0_, ...), custom_call_target="tpu_custom_call" | custom-call | flops 60000002048 | bytes 360000000 | tf_op jit(solution)/shard_map/ffn_backward/pallas_call | solution.py:706
  445.3 0.9 pad.53.refs_2_.refs_10_
  446.2 61.4 %out_backward.1 = (bf16[2048,256]{1,0:T(8,128)(2,1)}, bf16[2048,128]{1,0:T(8,128)(2,1)}, f32[8,2048]{1,0:T(8,128)}, bf16[48,2048]{1,0:T(8,128)(2,1)}, bf16[64,76...) custom-call(bf16[2048,256]{1,0:T(8,128)(2,1)} %get-tuple-element.115.refs_0_, ...), custom_call_target="tpu_custom_call" | custom-call | flops 30000001024 | bytes 180000000 | tf_op jit(solution)/shard_map/out_backward/pallas_call | solution.py:706
  507.6 0.8 constant_dynamic-slice_fusion
  508.6 0.8 pad.54.refs_11_.refs_9_
  509.4 30.7 %attention_backward.1 = (bf16[2048,768]{1,0:T(8,128)(2,1)}, f32[8,1,256]{2,1,0:T(1,128)}, f32[8,768]{1,0:T(8,128)}, bf16[2048,128]{1,0:T(8,128)(2,1)}) custom-call(bf16[2048,768]{1,0:T(8,128)(2,1)} %get-tuple-element.93.refs_0_, bf16[2048,256]{1,0:T(8,128)(2,1)} %get-tuple-element.96.refs_0_.refs_1_.refs_20_, bf16[2048,256]{1,0:T(8,128)(2,1)} %get-tuple-element.132.refs_2_, ...), custom_call_target="tpu_custom_call" | custom-call | flops 17500000256 | bytes 105000000 | tf_op jit(solution)/shard_map/attention_backward/pallas_call | solution.py:706
  540.1 79.9 %qkv_backward.1 = (bf16[2048,256]{1,0:T(8,128)(2,1)}, f32[112,256]{1,0:T(8,128)}, f32[80,256]{1,0:T(8,128)}, f32[64,768]{1,0:T(8,128)}) custom-call(bf16[2048,768]{1,0:T(8,128)(2,1)} %get-tuple-element.138.refs_0_, f32[8,1,256]{2,1,0:T(1,128)} %get-tuple-element.139.refs_1_, bf16[2048,896]{1,0:T(8,128)(2,1)} %get-tuple-element.140.refs_2_, ...), custom_call_target="tpu_custom_call" | custom-call | flops 35000000512 | bytes 210000000 | tf_op jit(solution)/shard_map/qkv_backward/pallas_call | solution.py:706
  620.0 3.6 last_step.1
  (54 shorter events, 5.8 us)
Async XLA Ops:
  0.6 5.4 copy-start
  2.6 4.8 copy-start.3
  2.6 5.7 copy-start.4
  2.7 5.7 copy-start.5
  2.7 6.5 %copy-start.6 = (f32[2,704]{1,0:T(2,128)S(1)}, f32[2,704]{1,0:T(2,128)}, u32[]{:S(2)}) copy-start(f32[2,704]{1,0:T(2,128)} %param.38) | copy-start | bytes 16900
  3.6 6.3 %copy-start.7 = (f32[3,256]{1,0:T(4,128)S(1)}, f32[3,256]{1,0:T(4,128)}, u32[]{:S(2)}) copy-start(f32[3,256]{1,0:T(4,128)} %param.30) | copy-start | bytes 9220
  3.6 6.3 %copy-start.8 = (f32[256]{0:T(256)S(1)}, f32[256]{0:T(256)}, u32[]{:S(2)}) copy-start(f32[256]{0:T(256)} %param.42) | copy-start | bytes 3076
  3.6 6.3 %copy-start.9 = (f32[256]{0:T(256)S(1)}, f32[256]{0:T(256)}, u32[]{:S(2)}) copy-start(f32[256]{0:T(256)} %param.34) | copy-start | bytes 3076
  270.9 94.7 %copy-start.1 = (f32[16,2048]{1,0:T(8,128)S(1)}, f32[16,2048]{1,0:T(8,128)}, u32[]{:S(2)}) copy-start(f32[16,2048]{1,0:T(8,128)} %refs_18_.1) | copy-start | bytes 393220
  366.5 78.8 %copy-start.2 = (f32[16,2048]{1,0:T(8,128)S(1)}, f32[16,2048]{1,0:T(8,128)}, u32[]{:S(2)}) copy-start(f32[16,2048]{1,0:T(8,128)} %refs_20_.1) | copy-start | bytes 393220
